TPU v7x, 32 devices: a whole 2x2x4 slice. The times are simulated.
32 devices in a mesh: space: 8 (over y, x, core), mode: 4 (over z).
Axes of the slice: x: 2, y: 2, z: 4, core: 2. Of those that a mesh axis runs over, the one named last changes fastest.
Arguments:
- modes: bfloat16 [512, 96, 2048], P('mode', 'space'), may hold values from -6 to 6
- phases: int32 [96, 2048], P('space'), may hold values from 0 to 2
- velocity: float32 [3], replicated, may hold values from 0.5 to 1.5
Outputs:
- reduced: float32 [512, 512], P('space', 'mode')
All inputs are finite; a program needn't handle non-finite values.
Results may differ from a plain program's by a relative error of at most 0.0028.
Values may be sent and summed in bfloat16 or wider, within the bound.
No kernel may reach another device: no remote copies, remote signals or barrier semaphores. Data moves between devices by JAX's collectives and lax.ppermute only.
A program may use at most 192 MiB of HBM per device.

v0:
```python
import math

import jax
import jax.numpy as jnp
from jax import lax
from jax.sharding import PartitionSpec as P

NZ = 64


def extended(array, sides, width):
    for axis, dim in sides:
        devices, length = (lax.axis_size(axis), array.shape[dim])
        up = [(i, (i + 1) % devices) for i in range(devices - 1)]
        down = [(j, i) for i, j in up]
        last = lax.slice_in_dim(array, length - width, length, axis=dim)
        initial = lax.slice_in_dim(array, 0, width, axis=dim)
        before = lax.ppermute(last, axis, up)
        after = lax.ppermute(initial, axis, down)
        array = jnp.concatenate([before, array, after], axis=dim)
    return array


def shifted(field, offset):
    width = field.shape[-1]
    zeros_part = jnp.zeros(field.shape[:-1] + (abs(offset),), jnp.float32)
    if offset > 0:
        return jnp.concatenate([field[..., offset:], zeros_part], axis=-1)
    return jnp.concatenate([zeros_part, field[..., : width + offset]], axis=-1)


def inner_rows(left, right):
    left_flat = left.reshape(left.shape[0], -1)
    right_flat = right.reshape(right.shape[0], -1)
    return lax.dot_general(
        left_flat, right_flat, (((1,), (1,)), ((), ())), preferred_element_type=jnp.float32
    )


def local(modes, phases, velocity):
    weight = jnp.where(phases == 0, 0.1, jnp.where(phases == 1, 1.0, 0.5)).astype(jnp.float32)
    total_cells = lax.axis_size("space") * modes.shape[1] * modes.shape[2]
    eps = 1.0 / math.sqrt(total_cells)
    padded = extended(modes, (("space", 1),), 1).astype(jnp.float32)
    center = padded[:, 1:-1]
    x_up = padded[:, 2:]
    x_down = padded[:, :-2]
    zpos = lax.broadcasted_iota(jnp.int32, (1, 1, center.shape[-1]), 2) % NZ
    z_up = jnp.where(zpos == NZ - 1, 0.0, shifted(center, 1))
    z_down = jnp.where(zpos == 0, 0.0, shifted(center, -1))
    y_up = shifted(center, NZ)
    y_down = shifted(center, -NZ)
    spread = x_up + x_down + y_up + y_down + z_up + z_down - 6.0 * center
    drift = (
        velocity[0] * (x_up - x_down)
        + velocity[1] * (y_up - y_down)
        + velocity[2] * (z_up - z_down)
    )
    applied = (weight[None] * (eps * spread - 0.5 * drift)).astype(jnp.bfloat16)
    partial_cols = inner_rows(lax.all_gather(modes, "mode", axis=0, tiled=True), applied)
    summed = lax.psum_scatter(partial_cols, "space", scatter_dimension=0, tiled=True)
    return summed * eps


def solution(mesh):
    placed = (P("mode", "space", None), P("space", None), P())
    return jax.shard_map(
        local, mesh=mesh, in_specs=placed, out_specs=P("space", "mode"), check_vma=False
    )
```

profile of v0, /device:TPU:1, one launch (start us, length us, event | category | flops | bytes accessed | tf_op | source)
XLA Modules:
  0.0 491.8 jit_solution(3091800072277738935)
XLA Ops:
  6.5 0.0 all-gather.2.cloned.1.call-start
  6.5 0.7 all-gather.2.cloned.1.call-update
  7.3 0.0 reduce-scatter.4.cloned.1.call-start
  7.3 1.3 fusion.21
  8.6 4.5 collective-permute-start
  13.1 1.9 collective-permute-start.1
  15.0 1.4 fusion.22
  16.4 0.9 select_select_fusion
  17.3 1.9 collective-permute-done
  19.2 7.3 %collective-permute-done.1 = bf16[128,1,2048]{2,0,1:T(8,128)(2,1)S(1)} collective-permute-done((bf16[128,1,2048]{2,0,1:T(8,128)(2,1)S(1)}, bf16[128,1,2048]{2,0,1:T(8,128)(2,1)S(1)}, u32[]{:S(2)}, u32[]{:S(2)}) %collective-permute-start.1) | collective-permute-done | bytes 524320 | tf_op jit(solution)/shard_map/ppermute | solution.py:19
  26.5 10.5 %maximum_convert_fusion = f32[128,14,2048]{2,0,1:T(8,128)} fusion(bf16[128,1,2048]{2,0,1:T(8,128)(2,1)S(1)} %collective-permute-done.1, bf16[128,12,2048]{2,0,1:T(8,128)(2,1)} %param.3, bf16[128,1,2048]{2,0,1:T(8,128)(2,1)S(1)} %collective-permute-done), kind=kLoop, calls=%fused_computation.6 | loop fusion | flops 11010048 | bytes 22020096 | tf_op jit(solution)/shard_map/convert_element_type | solution.py:44
  37.0 0.0 copy-start
  37.0 22.8 %fusion.19 = (f32[128,12,1984]{2,0,1:T(8,128)}, f32[128,12,1984]{2,0,1:T(8,128)}) fusion(f32[128,14,2048]{2,0,1:T(8,128)} %maximum_convert_fusion), kind=kLoop, calls=%fused_computation.22 | loop fusion | bytes 48758784 | tf_op jit(solution)/shard_map/slice | solution.py:28
  59.8 0.0 copy-done
  59.8 10.1 %fusion.20 = (f32[128,12,2047]{2,0,1:T(8,128)}, f32[128,12,2047]{2,0,1:T(8,128)}) fusion(f32[128,14,2048]{2,0,1:T(8,128)S(1)} %copy-done), kind=kLoop, calls=%fused_computation.23 | loop fusion | bytes 50307072 | tf_op jit(solution)/shard_map/slice | solution.py:28
  69.9 34.3 %fusion.27 = bf16[128,12,2048]{2,0,1:T(8,128)(2,1)} fusion(f32[128,14,2048]{2,0,1:T(8,128)} %maximum_convert_fusion, f32[128,12,2047]{2,0,1:T(8,128)} %get-tuple-element.8, f32[128,12,2047]{2,0,1:T(8,128)} %get-tuple-element.7, f32[128,12,1984]{2,0,1:T(8,128)} %get-tuple-element.6, f32[128,12,1984]{2,0,1:T(8,128)} %get-tuple-element.5, ...), kind=kLoop, calls=%fused_computation.5.clone.clone.clone.clone.1 | loop fusion | flops 69206016 | bytes 93675536 | tf_op jit(solution)/shard_map/dot_general | solution.py:35
  104.2 332.3 %all-gather.2.cloned.1.call-done = bf16[512,12,2048]{2,0,1:T(8,128)(2,1)} async-done(((bf16[128,12,2048]{2,0,1:T(8,128)(2,1)}), bf16[512,12,2048]{2,0,1:T(8,128)(2,1)}) %all-gather.2.cloned.1.call-update) | async-done | bytes 25165840 | tf_op jit(solution)/shard_map/all_gather | solution.py:60
  436.4 15.1 %fusion.7 = f32[512,128]{0,1:T(8,128)S(1)} fusion(bf16[512,12,2048]{2,0,1:T(8,128)(2,1)} %all-gather.2.cloned.1.call-done, bf16[128,12,2048]{2,0,1:T(8,128)(2,1)} %fusion.27), kind=kOutput, calls=%fused_computation.8 | convolution fusion | flops 3221225472 | bytes 31719424 | tf_op jit(solution)/shard_map/dot_general | solution.py:35
  451.5 0.8 copy.7
  452.4 0.0 reduce-scatter.4.cloned.1.call-update
  452.4 31.3 %reduce-scatter.4.cloned.1.call-done = f32[64,128]{1,0:T(8,128)} async-done(((f32[512,128]{1,0:T(8,128)}), f32[64,128]{1,0:T(8,128)}) %reduce-scatter.4.cloned.1.call-update) | async-done | bytes 32784 | tf_op jit(solution)/shard_map/reduce_scatter | solution.py:61
  483.6 1.4 broadcast_multiply_fusion
  (1 shorter events, 0.0 us)
Async XLA Ops:
  6.5 429.9 %all-gather.2.cloned.1.call-start = ((), (), s32[]{:S(2)}) async-start(), calls=%async_computation.1 | async-start | bytes 31457280 | tf_op jit(solution)/shard_map/all_gather | solution.py:60
  7.3 476.4 %reduce-scatter.4.cloned.1.call-start = ((), (), s32[]{:S(2)}) async-start(), calls=%async_computation.2 | async-start | bytes 294912 | tf_op jit(solution)/shard_map/reduce_scatter | solution.py:61
  8.6 10.6 %collective-permute-start = (bf16[128,1,2048]{2,0,1:T(8,128)(2,1)S(1)}, bf16[128,1,2048]{2,0,1:T(8,128)(2,1)S(1)}, u32[]{:S(2)}, u32[]{:S(2)}) collective-permute-start(bf16[128,1,2048]{2,0,1:T(8,128)(2,1)S(1)} %get-tuple-element.9), channel_id=1, source_target_pairs={{0,4},{4,8},{8,12},{12,16},{16,20},{20,24},{24,28},{1,5},{5,9},{9,... | collective-permute-start | bytes 1572872 | tf_op jit(solution)/shard_map/ppermute | solution.py:18
  13.1 13.4 %collective-permute-start.1 = (bf16[128,1,2048]{2,0,1:T(8,128)(2,1)S(1)}, bf16[128,1,2048]{2,0,1:T(8,128)(2,1)S(1)}, u32[]{:S(2)}, u32[]{:S(2)}) collective-permute-start(bf16[128,1,2048]{2,0,1:T(8,128)(2,1)S(1)} %get-tuple-element.10), channel_id=1, source_target_pairs={{4,0},{8,4},{12,8},{16,12},{20,16},{24,20},{28,24},{5,1},{9,5},{13... | collective-permute-start | bytes 1572872 | tf_op jit(solution)/shard_map/ppermute | solution.py:19
  37.0 22.8 %copy-start = (f32[128,14,2048]{2,0,1:T(8,128)S(1)}, f32[128,14,2048]{2,0,1:T(8,128)}, u32[]{:S(2)}) copy-start(f32[128,14,2048]{2,0,1:T(8,128)} %maximum_convert_fusion) | copy-start | bytes 44040196
Sparse Core Ops, SparseCore 0:
  8.9 427.4 all-gather.1
  452.5 31.0 reduce-scatter.3
where the time goes:
time: 493 us; the launch traced here: 492 us
  waiting for transfers between devices  373 us (76%)
  other arithmetic  47.1 us (10%)
  local copies, waits for them, and re-layouts  36.4 us (7%)
  matrix products  15.1 us (3%)
  between operations  13.4 us (3%)
  starting transfers between devices  6.47 us (1%)
    all_gather x1, waiting for transfers between devices, local(): lax.all_gather(modes, 'mode', axis=0, tiled=True)  332 us
    dot_general x1, other arithmetic, inner_rows(): lax.dot_general(left_flat, right_flat, (((1,), (1,)), ((), ())), preferre...  34.3 us
    slice x2, local copies, waits for them, and re-layouts, shifted(): return jnp.concatenate([field[..., offset:], zeros_part], axis=-1)  32.9 us
    reduce_scatter x1, waiting for transfers between devices, local(): lax.psum_scatter(partial_cols, 'space', scatter_dimension=0, tiled=True)  31.3 us
    dot_general x1, matrix products, inner_rows(): lax.dot_general(left_flat, right_flat, (((1,), (1,)), ((), ())), preferre...  15.1 us
    convert_element_type x1, other arithmetic, local(): padded = extended(modes, (('space', 1),), 1).astype(jnp.float32)  10.5 us
  transfers between devices with their start and end apart: 4, of which 4 were waited for; matrix products, arithmetic and copies ran while one was open for 17% of the time, Pallas kernels for 0%

commit v1 on v0

v1 whole, which is shorter than its diff:
```python
import functools
import math

import jax
import jax.numpy as jnp
from jax import lax
from jax.experimental import pallas as pl
from jax.experimental.pallas import tpu as pltpu
from jax.sharding import PartitionSpec as P

NZ = 64
LANES = 128
SUB = 16
BF = jnp.bfloat16
F32 = jnp.float32


def cyclic(devices, k):
    return [(i, (i + k) % devices) for i in range(devices)]


def product(left, right):
    return lax.dot_general(left, right, (((1,), (1,)), ((), ())), preferred_element_type=F32)


def phase_kernel(n_old, eps, steps, keep, velocity, w, wh, x, xp, xn, xd, xu, h, *refs):
    old = [refs[4 * i : 4 * i + 4] for i in range(n_old)]
    out = refs[4 * n_old :]
    if keep:
        a, ah = out[0], out[1]
        sums = out[2:]
    else:
        sums, (a, ah) = out[:-2], out[-2:]
    i = pl.program_id(0)
    count, tiles = x.shape[1], x.shape[2] // LANES
    v0, v1, v2 = velocity[0], velocity[1], velocity[2]
    lane = lax.broadcasted_iota(jnp.int32, (SUB, LANES), 1)
    low = lane < NZ
    at_end = (lane % NZ) == NZ - 1
    at_start = (lane % NZ) == 0

    def body(j, carry):
        rows = pl.ds(pl.multiple_of(j * SUB, SUB), SUB)

        def tile(ref, r, t):
            return ref[r, rows, t * LANES : (t + 1) * LANES].astype(F32)

        halo = h[0, rows, :].astype(F32)
        swapped = pltpu.roll(halo, NZ, 1)
        center = [[tile(x, r, t) for t in range(tiles)] for r in (0, 1)]
        tails = []
        for r in (0, 1):
            turned = [pltpu.roll(c, NZ, 1) for c in center[r]]
            tails.append((center[r][-1], turned[-1]))
            for t in range(tiles):
                c = center[r][t]
                if r == 0:
                    x_up = center[1][t]
                    x_down = jnp.where(i == 0, tile(xd, 0, t), tile(xp, 0, t))
                else:
                    x_up = jnp.where(i == steps - 1, tile(xu, 0, t), tile(xn, 0, t))
                    x_down = center[0][t]
                after = turned[t + 1] if t + 1 < tiles else (swapped if r == 0 else halo)
                before = turned[t - 1] if t > 0 else jnp.zeros_like(c)
                y_up = jnp.where(low, turned[t], after)
                y_down = jnp.where(low, before, turned[t])
                z_up = jnp.where(at_end, 0.0, pltpu.roll(c, LANES - 1, 1))
                z_down = jnp.where(at_start, 0.0, pltpu.roll(c, 1, 1))
                spread = x_up + x_down + y_up + y_down + z_up + z_down - 6.0 * c
                drift = v0 * (x_up - x_down) + v1 * (y_up - y_down) + v2 * (z_up - z_down)
                weight = w[r, :, t * LANES : (t + 1) * LANES]
                a[r, rows, t * LANES : (t + 1) * LANES] = (
                    weight * (eps * spread - 0.5 * drift)
                ).astype(BF)
        below = jnp.where(low, tails[0][1], tails[1][0])
        ah[0, rows, :] = (wh[0] * (eps * below + 0.5 * (v1 * below))).astype(BF)
        return carry

    lax.fori_loop(0, count // SUB, body, 0)

    @pl.when(i == 0)
    def _():
        for s in sums:
            s[...] = jnp.zeros_like(s)

    for o, (ox, oh, oa, oah) in enumerate(old):
        sums[2 * o][...] += product(x[0], oa[0]) + product(x[1], oa[1]) + product(h[0], oah[0])
        sums[2 * o + 1][...] += product(ox[0], a[0]) + product(ox[1], a[1]) + product(oh[0], ah[0])
    sums[2 * n_old][...] += product(x[0], a[0]) + product(x[1], a[1]) + product(h[0], ah[0])


def phase(velocity, w, wh, new, old, eps, keep):
    x, xd, xu, h = new
    rows, count, width = x.shape
    steps = rows // 2
    pair = lambda m: pl.BlockSpec((2, m, width), lambda i: (i, 0, 0))
    single = lambda f: pl.BlockSpec((1, count, width), lambda i: (f(i), 0, 0))
    halo = lambda m: pl.BlockSpec((1, m, LANES), lambda i: (i, 0, 0))
    specs = [
        pl.BlockSpec(memory_space=pltpu.SMEM),
        pl.BlockSpec((2, 1, width), lambda i: (i, 0, 0)),
        pl.BlockSpec((1, 1, LANES), lambda i: (i, 0, 0)),
        pair(count),
        single(lambda i: jnp.maximum(2 * i - 1, 0)),
        single(lambda i: jnp.minimum(2 * i + 2, rows - 1)),
        single(lambda i: 0),
        single(lambda i: 0),
        halo(count),
    ]
    args = [velocity, w, wh, x, x, x, xd, xu, h]
    sums = []
    for ox, oh, oa, oah in old:
        m = ox.shape[1]
        specs += [pair(m), halo(m), pair(m), halo(m)]
        args += [ox, oh, oa, oah]
        sums += [(count, m), (m, count)]
    sums.append((count, count))
    out_shape = [jax.ShapeDtypeStruct(s, F32) for s in sums]
    out_specs = [pl.BlockSpec(s, lambda i: (0, 0)) for s in sums]
    scratch = []
    if keep:
        out_shape = [
            jax.ShapeDtypeStruct(x.shape, BF),
            jax.ShapeDtypeStruct(h.shape, BF),
        ] + out_shape
        out_specs = [pair(count), halo(count)] + out_specs
    else:
        scratch = [pltpu.VMEM((2, count, width), BF), pltpu.VMEM((1, count, LANES), BF)]
    elements = rows * count * width
    pairs = sum(a * b for a, b in sums)
    outs = pl.pallas_call(
        functools.partial(phase_kernel, len(old), eps, steps, keep),
        grid=(steps,),
        in_specs=specs,
        out_specs=out_specs,
        out_shape=out_shape,
        scratch_shapes=scratch,
        compiler_params=pltpu.CompilerParams(vmem_limit_bytes=32 << 20),
        cost_estimate=pl.CostEstimate(
            flops=25 * elements + 2 * pairs * rows * width,
            bytes_accessed=6 * elements + 4 * sum(o[0].size for o in old) + 4 * pairs,
            transcendentals=0,
        ),
    )(*args)
    if keep:
        return (x, h, outs[0], outs[1]), outs[2:]
    return None, outs


def local(modes, phases, velocity):
    space, n = lax.axis_size("space"), lax.axis_size("mode")
    sp, q = lax.axis_index("space"), lax.axis_index("mode")
    count, rows, plane = modes.shape
    width = plane // n
    eps = 1.0 / math.sqrt(space * rows * plane)
    field = jnp.transpose(modes, (1, 0, 2))

    weight = jnp.where(phases == 0, 0.1, jnp.where(phases == 1, 1.0, 0.5)).astype(F32)
    w = lax.dynamic_slice_in_dim(weight, q * width, width, axis=1)[:, None, :]
    after = jnp.minimum((q + 1) * width, plane - NZ)
    wh = lax.dynamic_slice_in_dim(weight, after, NZ, axis=1).reshape(rows // 2, 1, LANES)

    def slab(owner):
        return lax.dynamic_slice_in_dim(field, owner * width, width, axis=2)

    def line(owner):
        start = jnp.minimum((owner + 1) * width, plane - NZ)
        part = lax.dynamic_slice_in_dim(field, start, NZ, axis=2)
        part = jnp.where(owner == n - 1, jnp.zeros_like(part), part)
        return jnp.concatenate([part[0::2], part[1::2]], axis=-1)

    order = [0, 1, 3, 2] if n == 4 else list(range(n))
    xs, hs = {}, {}
    for k in order:
        s, l = slab((q + k) % n), line((q + k) % n)
        xs[k] = lax.ppermute(s, "mode", cyclic(n, k)) if k else s
        hs[k] = lax.ppermute(l, "mode", cyclic(n, k)) if k else l
    groups = [[k] for k in order] if n == 4 else [order]
    up = [(i, i + 1) for i in range(space - 1)]
    down = [(i + 1, i) for i in range(space - 1)]
    old, found, names = [], {}, []
    for g, group in enumerate(groups):
        join = lambda parts: parts[0] if len(parts) == 1 else jnp.concatenate(parts, axis=1)
        x, h = join([xs[k] for k in group]), join([hs[k] for k in group])
        xd = lax.ppermute(x[rows - 1 :], "space", up)
        xu = lax.ppermute(x[:1], "space", down)
        kept, sums = phase(velocity, w, wh, (x, xd, xu, h), old, eps, g + 1 < len(groups))
        for o, name in enumerate(names):
            found[g, name], found[name, g] = sums[2 * o], sums[2 * o + 1]
        found[g, g] = sums[-1]
        names.append(g)
        old.append(kept)

    if n == 4:
        place = [order.index((n - d) % n) for d in range(n)]
        total = jnp.concatenate(
            [jnp.concatenate([found[a, b] for b in place], axis=1) for a in place], axis=0
        )
    else:
        only = found[0, 0].reshape(n, count, n, count)
        turn = jnp.array([(n - d) % n for d in range(n)])
        total = only[turn][:, :, turn].reshape(n * count, n * count)
    size = n * count
    share = size // space

    def piece(target):
        return lax.dynamic_slice_in_dim(total, (target * share - q * count) % size, share, axis=0)

    mine = piece(sp)
    for k in range(1, space):
        mine = mine + lax.ppermute(piece((sp + k) % space), "space", cyclic(space, k))
    result = mine[:, :count]
    for k in range(1, n):
        result = result + lax.ppermute(mine[:, k * count : (k + 1) * count], "mode", cyclic(n, k))
    return result * eps


def solution(mesh):
    placed = (P("mode", "space", None), P("space", None), P())
    return jax.shard_map(
        local, mesh=mesh, in_specs=placed, out_specs=P("space", "mode"), check_vma=False
    )
```

time: 493 us -> 236 us (0.48)
  waiting for transfers between devices: 373 us -> 87.7 us
  starting transfers between devices: 6.47 us -> 85.1 us
  Pallas kernels: 0 us -> 42.8 us
  other arithmetic: 47.1 us -> 6.21 us
  local copies, waits for them, and re-layouts: 36.4 us -> 9.82 us
  matrix products: 15.1 us -> 0 us
  between operations: 13.4 us -> 0.32 us
    all_gather x1 -> x0, waiting for transfers between devices: 332 us -> none  [local(): lax.all_gather(modes, 'mode', axis=0, tiled=True)]
    ppermute x2 -> x24, starting transfers between devices: 6.43 us -> 85.1 us  [the longest x3 39.6 us: local(): lax.ppermute(mine[:, k * count:(k + 1) * count], 'mode', cyclic(n, k))]
    ppermute x2 -> x24, waiting for transfers between devices: 9.15 us -> 87.7 us  [the longest x3 73 us: local(): xs[k] = lax.ppermute(s, 'mode', cyclic(n, k)) if k else s]
    pallas_call x0 -> x4, Pallas kernels: none -> 42.8 us  [phase(): pl.pallas_call(functools.partial(phase_kernel, len(old), eps, steps, keep...]
    dot_general x1 -> x0, other arithmetic: 34.3 us -> none  [inner_rows(): lax.dot_general(left_flat, right_flat, (((1,), (1,)), ((), ())), preferre...]
    slice x4 -> x7, local copies, waits for them, and re-layouts: 35.5 us -> 3.65 us  [the longest x4 2.72 us: local(): xu = lax.ppermute(x[:1], 'space', down)]
    reduce_scatter x1 -> x0, waiting for transfers between devices: 31.3 us -> none  [local(): lax.psum_scatter(partial_cols, 'space', scatter_dimension=0, tiled=True)]
    dot_general x1 -> x0, matrix products: 15.1 us -> none  [inner_rows(): lax.dot_general(left_flat, right_flat, (((1,), (1,)), ((), ())), preferre...]
  transfers between devices with their start and end apart: 4 -> 24, of which waited for: 4 -> 11; matrix products, arithmetic and copies ran while one was open for 17% -> 4% of each run, Pallas kernels for 0% -> 13%
where the time goes in v1:
time: 236 us; the launch traced here: 232 us
  waiting for transfers between devices  87.7 us (37%)
  starting transfers between devices  85.1 us (36%)
  Pallas kernels  42.8 us (18%)
  local copies, waits for them, and re-layouts  9.82 us (4%)
  other arithmetic  6.21 us (3%)
    ppermute x3, waiting for transfers between devices, local(): xs[k] = lax.ppermute(s, 'mode', cyclic(n, k)) if k else s  73 us
    pallas_call x4, Pallas kernels, phase(): pl.pallas_call(functools.partial(phase_kernel, len(old), eps, steps, keep...  42.8 us
    ppermute x3, starting transfers between devices, local(): lax.ppermute(mine[:, k * count:(k + 1) * count], 'mode', cyclic(n, k))  39.6 us
    ppermute x4, starting transfers between devices, local(): xd = lax.ppermute(x[rows - 1:], 'space', up)  17.8 us
    ppermute x7, starting transfers between devices, local(): lax.ppermute(piece((sp + k) % space), 'space', cyclic(space, k))  10.7 us
    ppermute x4, starting transfers between devices, local(): xu = lax.ppermute(x[:1], 'space', down)  9.77 us
    ppermute x3, starting transfers between devices, local(): xs[k] = lax.ppermute(s, 'mode', cyclic(n, k)) if k else s  5.57 us
    dynamic_slice x1, local copies, waits for them, and re-layouts, slab(): return lax.dynamic_slice_in_dim(field, owner * width, width, axis=2)  5.13 us
  transfers between devices with their start and end apart: 24, of which 11 were waited for; matrix products, arithmetic and copies ran while one was open for 4% of the time, Pallas kernels for 13%

profile of v1, /device:TPU:1, one launch (start us, length us, event | category | flops | bytes accessed | tf_op | source)
XLA Modules:
  0.0 231.9 jit_solution(10397828745652965419)
XLA Ops:
  0.0 5.1 %dynamic-slice_bitcast_fusion.2 = (bf16[12,128,512]{2,1,0:T(8,128)(2,1)}, bf16[12,128,512]{2,1,0:T(8,128)(2,1)}, bf16[12,128,512]{2,1,0:T(8,128)(2,1)S(1)}, bf16[12,128,512]{2,1,0:T(8,128)(2,1)}) fusion(bf16[128,12,2048]{2,0,1:T(8,128)(2,1)} %param.3, s32[]{:T(128)S(6)} %select_n.198, s32[]{:T(128)S(6)} %select_n.204, s32[]{:T(128)S(6)} %select_n.192, ...), kind=kLoop, calls=%fused_computation.2 | loop fusion | bytes 12582928 | tf_op jit(solution)/shard_map/dynamic_slice | solution.py:164
  5.1 2.1 collective-permute-start.6
  7.3 0.7 fusion.5
  8.0 3.9 %collective-permute-start = (bf16[1,128,512]{2,1,0:T(8,128)(2,1)}, bf16[1,128,512]{2,1,0:T(8,128)(2,1)S(1)}, u32[]{:S(2)}, u32[]{:S(2)}) collective-permute-start(bf16[1,128,512]{2,1,0:T(8,128)(2,1)} %get-tuple-element.62), channel_id=1, source_target_pairs={{0,4},{4,8},{8,12},{12,16},{16,20},{20,24},{24,28},{1,5},{5,9},{9,... | collective-permute-start | bytes 393224 | tf_op jit(solution)/shard_map/ppermute | solution.py:185
  11.9 1.9 collective-permute-start.1
  13.9 2.4 %collective-permute-start.10 = (bf16[12,128,512]{2,1,0:T(8,128)(2,1)}, bf16[12,128,512]{2,1,0:T(8,128)(2,1)}, u32[]{:S(2)}, u32[]{:S(2)}) collective-permute-start(bf16[12,128,512]{2,1,0:T(8,128)(2,1)} %get-tuple-element.56), channel_id=1, source_target_pairs={{0,2},{1,3},{2,0},{3,1},{4,6},{5,7},{6,4},{7,5},{8,10},{9,11},{10,... | collective-permute-start | bytes 4718600 | tf_op jit(solution)/shard_map/ppermute | solution.py:176
  16.2 1.1 collective-permute-start.2
  17.4 2.5 %select_bitcast_fusion.2 = (bf16[12,128,64]{2,1,0:T(8,128)(2,1)S(1)}, bf16[12,128,64]{2,1,0:T(8,128)(2,1)S(1)}, bf16[12,128,64]{2,1,0:T(8,128)(2,1)S(1)}, bf16[12,128,64]{2,1,0:T(8,128)(2,1)S(1)}) fusion(bf16[128,12,2048]{2,0,1:T(8,128)(2,1)} %param.3, s32[]{:T(128)S(6)} %select_n.200, pred[]{:T(512)S(6)} %eq.53, s32[]{:T(128)S(6)} %select_n.206, ...), kind=kLoop, calls=%fused_computation.7 | loop fusion | flops 393216 | bytes 1572884 | tf_op jit(solution)/shard_map/jit(_where)/select_n | solution.py:169
  19.9 0.1 fusion.9
  20.0 0.8 pad_maximum_fusion.2
  20.8 0.1 pad_maximum_fusion.h.refs_1_
  20.9 0.0 copy-start
  21.0 0.9 fusion.7
  21.8 0.8 pad_maximum_fusion.3
  22.6 0.8 constant_dynamic-slice_fusion.7
  23.4 0.1 reshape.3.wh
  23.5 1.1 pad_maximum_fusion.1
  24.7 0.4 collective-permute-start.7
  25.1 0.0 collective-permute-done.1.xu
  25.1 0.1 collective-permute-start.13
  25.2 8.8 %shard_map.37 = (bf16[12,128,512]{2,1,0:T(8,128)(2,1)S(1)}, bf16[6,128,128]{2,1,0:T(8,128)(2,1)S(1)}, f32[128,128]{1,0:T(8,128)S(1)}) custom-call(f32[3]{0:T(128)S(1)} %copy-done, f32[12,1,512]{2,1,0:T(1,128)S(1)} %broadcast_in_dim.18.w, f32[6,1,128]{2,1,0:T(1,128)S(1)} %reshape.3.wh, bf16[12,128,512]{2,1,0:T(8,128)(2,1)S(1)} %get-tuple-element.55.x.xp.xn.refs_0_, ...), custom_call_target="tpu_custom_call" | custom-call | flops 220987392 | bytes 4784128 | tf_op jit(solution)/shard_map/pallas_call | solution.py:131
  34.0 9.7 %collective-permute-done.6.x.xp.xn.refs_4_ = bf16[12,128,512]{2,1,0:T(8,128)(2,1)S(1)} collective-permute-done((bf16[12,128,512]{2,1,0:T(8,128)(2,1)}, bf16[12,128,512]{2,1,0:T(8,128)(2,1)S(1)}, u32[]{:S(2)}, u32[]{:S(2)}) %collective-permute-start.6) | collective-permute-done | bytes 1572896 | tf_op jit(solution)/shard_map/ppermute | solution.py:176
  43.7 1.1 collective-permute-start.5
  44.8 63.3 %collective-permute-done.2.x.xp.xn.refs_8_ = bf16[12,128,512]{2,1,0:T(8,128)(2,1)} collective-permute-done((bf16[12,128,512]{2,1,0:T(8,128)(2,1)}, bf16[12,128,512]{2,1,0:T(8,128)(2,1)}, u32[]{:S(2)}, u32[]{:S(2)}) %collective-permute-start.2) | collective-permute-done | bytes 1572896 | tf_op jit(solution)/shard_map/ppermute | solution.py:176
  108.1 5.7 %collective-permute-start.8 = (bf16[1,128,512]{2,1,0:T(8,128)(2,1)S(1)}, bf16[1,128,512]{2,1,0:T(8,128)(2,1)S(1)}, u32[]{:S(2)}, u32[]{:S(2)}) collective-permute-start(bf16[1,128,512]{2,1,0:T(8,128)(2,1)S(1)} %get-tuple-element.64), channel_id=1, source_target_pairs={{0,4},{4,8},{8,12},{12,16},{16,20},{20,24},{24,28},{1,5},{5,9},{9,... | collective-permute-start | bytes 393224 | tf_op jit(solution)/shard_map/ppermute | solution.py:185
  113.8 1.0 fusion.3
  114.8 0.6 collective-permute-done.7.h.refs_5_
  115.4 4.0 %collective-permute-start.9 = (bf16[1,128,512]{2,1,0:T(8,128)(2,1)S(1)}, bf16[1,128,512]{2,1,0:T(8,128)(2,1)S(1)}, u32[]{:S(2)}, u32[]{:S(2)}) collective-permute-start(bf16[1,128,512]{2,1,0:T(8,128)(2,1)S(1)} %get-tuple-element.63), channel_id=1, source_target_pairs={{4,0},{8,4},{12,8},{16,12},{20,16},{24,20},{28,24},{5,1},{9,5},{13... | collective-permute-start | bytes 393224 | tf_op jit(solution)/shard_map/ppermute | solution.py:186
  119.4 1.3 collective-permute-done.5.h.refs_9_
  120.7 4.5 %collective-permute-start.3 = (bf16[1,128,512]{2,1,0:T(8,128)(2,1)S(1)}, bf16[1,128,512]{2,1,0:T(8,128)(2,1)S(1)}, u32[]{:S(2)}, u32[]{:S(2)}) collective-permute-start(bf16[1,128,512]{2,1,0:T(8,128)(2,1)S(1)} %get-tuple-element.58), channel_id=1, source_target_pairs={{0,4},{4,8},{8,12},{12,16},{16,20},{20,24},{24,28},{1,5},{5,9},{9,... | collective-permute-start | bytes 393224 | tf_op jit(solution)/shard_map/ppermute | solution.py:185
  125.2 0.0 collective-permute-done.10.x.xp.xn
  125.2 1.9 collective-permute-start.4
  127.2 1.0 fusion.4
  128.2 3.6 %collective-permute-start.11 = (bf16[1,128,512]{2,1,0:T(8,128)(2,1)S(1)}, bf16[1,128,512]{2,1,0:T(8,128)(2,1)S(1)}, u32[]{:S(2)}, u32[]{:S(2)}) collective-permute-start(bf16[1,128,512]{2,1,0:T(8,128)(2,1)S(1)} %get-tuple-element.60), channel_id=1, source_target_pairs={{0,4},{4,8},{8,12},{12,16},{16,20},{20,24},{24,28},{1,5},{5,9},{9,... | collective-permute-start | bytes 393224 | tf_op jit(solution)/shard_map/ppermute | solution.py:185
  131.8 0.0 collective-permute-done.9.xu
  131.8 1.9 collective-permute-start.12
  133.7 9.6 %shard_map.38 = (bf16[12,128,512]{2,1,0:T(8,128)(2,1)S(1)}, bf16[6,128,128]{2,1,0:T(8,128)(2,1)S(1)}, f32[128,128]{1,0:T(8,128)S(1)}, f32[128,128]{1,0:T(8,128)S(1)}, f32[128,128]{1,0:T(8,128)S(1)}) custom-call(f32[3]{0:T(128)S(1)} %copy-done, f32[12,1,512]{2,1,0:T(1,128)S(1)} %broadcast_in_dim.18.w, f32[6,1,128]{2,1,0:T(1,128)S(1)} %reshape.3.wh, ...), custom_call_target="tpu_custom_call" | custom-call | flops 623640576 | bytes 8060928 | tf_op jit(solution)/shard_map/pallas_call | solution.py:131
  143.4 0.0 collective-permute-done.3.xd
  143.4 11.6 %shard_map.39 = (bf16[12,128,512]{2,1,0:T(8,128)(2,1)S(1)}, bf16[6,128,128]{2,1,0:T(8,128)(2,1)S(1)}, f32[128,128]{1,0:T(8,128)S(1)}, f32[128,128]{1,0:T(8,128)S...) custom-call(f32[3]{0:T(128)S(1)} %copy-done, f32[12,1,512]{2,1,0:T(1,128)S(1)} %broadcast_in_dim.18.w, ...), custom_call_target="tpu_custom_call" | custom-call | flops 1026293760 | bytes 11337728 | tf_op jit(solution)/shard_map/pallas_call | solution.py:131
  155.0 3.2 %collective-permute-done.13.h = bf16[6,128,128]{2,1,0:T(8,128)(2,1)S(1)} collective-permute-done((bf16[6,128,128]{2,1,0:T(8,128)(2,1)}, bf16[6,128,128]{2,1,0:T(8,128)(2,1)S(1)}, u32[]{:S(2)}, u32[]{:S(2)}) %collective-permute-start.13) | collective-permute-done | bytes 196640 | tf_op jit(solution)/shard_map/ppermute | solution.py:177
  158.2 0.0 collective-permute-done.11.xd
  158.2 0.0 collective-permute-done.12.xu
  158.2 12.8 %shard_map.40 = (f32[128,128]{1,0:T(8,128)S(1)}, f32[128,128]{1,0:T(8,128)S(1)}, f32[128,128]{1,0:T(8,128)S(1)}, f32[128,128]{1,0:T(8,128)S(1)}, f32[128,128]{1,...) custom-call(f32[3]{0:T(128)S(1)} %copy-done, f32[12,1,512]{2,1,0:T(1,128)S(1)} %broadcast_in_dim.18.w, ...), custom_call_target="tpu_custom_call" | custom-call | flops 1428946944 | bytes 14614528 | tf_op jit(solution)/shard_map/pallas_call | solution.py:131
  171.0 0.1 maximum_maximum_fusion
  171.1 0.1 constant_dynamic-slice_fusion.6
  171.2 0.4 collective-permute-start.20
  171.7 2.4 %collective-permute-start.19 = (f32[64,512]{1,0:T(8,128)S(1)}, f32[64,512]{1,0:T(8,128)S(1)}, u32[]{:S(2)}, u32[]{:S(2)}) collective-permute-start(f32[64,512]{1,0:T(8,128)S(1)} %get-tuple-element.67), channel_id=1, source_target_pairs={{0,24},{4,28},{8,0},{12,4},{16,8},{20,12},{24,16},{28,20},{1,25},{... | collective-permute-start | bytes 393224 | tf_op jit(solution)/shard_map/ppermute | solution.py:211
  174.0 1.4 collective-permute-start.18
  175.4 1.2 collective-permute-start.17
  176.7 0.0 collective-permute-start.16
  176.7 0.7 collective-permute-done.20
  177.4 1.9 collective-permute-start.15
  179.3 0.0 collective-permute-done.19
  179.3 3.4 %collective-permute-start.14 = (f32[64,512]{1,0:T(8,128)S(1)}, f32[64,512]{1,0:T(8,128)S(1)}, u32[]{:S(2)}, u32[]{:S(2)}) collective-permute-start(f32[64,512]{1,0:T(8,128)S(1)} %get-tuple-element.65), channel_id=1, source_target_pairs={{0,4},{4,8},{8,12},{12,16},{16,20},{20,24},{24,28},{28,0},{1,5},{5... | collective-permute-start | bytes 393224 | tf_op jit(solution)/shard_map/ppermute | solution.py:211
  182.7 2.6 %collective-permute-done.17 = f32[64,512]{1,0:T(8,128)S(1)} collective-permute-done((f32[64,512]{1,0:T(8,128)S(1)}, f32[64,512]{1,0:T(8,128)S(1)}, u32[]{:S(2)}, u32[]{:S(2)}) %collective-permute-start.17) | collective-permute-done | bytes 131104 | tf_op jit(solution)/shard_map/ppermute | solution.py:211
  185.3 1.4 collective-permute-done.16
  186.7 0.0 collective-permute-done.15
  186.7 0.1 add_add_fusion
  186.8 27.9 %collective-permute-start.23 = (f32[64,128]{1,0:T(8,128)S(1)}, f32[64,128]{1,0:T(8,128)S(1)}, u32[]{:S(2)}, u32[]{:S(2)}) collective-permute-start(f32[64,128]{1,0:T(8,128)S(1)} %get-tuple-element.81), channel_id=1, source_target_pairs={{0,3},{1,0},{2,1},{3,2},{4,7},{5,4},{6,5},{7,6},{8,11},{9,8},{10,9... | collective-permute-start | bytes 98312 | tf_op jit(solution)/shard_map/ppermute | solution.py:214
  214.8 11.7 %collective-permute-start.22 = (f32[64,128]{1,0:T(8,128)S(1)}, f32[64,128]{1,0:T(8,128)S(1)}, u32[]{:S(2)}, u32[]{:S(2)}) collective-permute-start(f32[64,128]{1,0:T(8,128)S(1)} %get-tuple-element.82), channel_id=1, source_target_pairs={{0,2},{1,3},{2,0},{3,1},{4,6},{5,7},{6,4},{7,5},{8,10},{9,11},{10,... | collective-permute-start | bytes 98312 | tf_op jit(solution)/shard_map/ppermute | solution.py:214
  226.5 0.1 collective-permute-done.23
  226.6 1.5 collective-permute-done.22
  228.1 3.2 %collective-permute-done.21 = f32[64,128]{1,0:T(8,128)S(1)} collective-permute-done((f32[64,128]{1,0:T(8,128)S(1)}, f32[64,128]{1,0:T(8,128)S(1)}, u32[]{:S(2)}, u32[]{:S(2)}) %collective-permute-start.21) | collective-permute-done | bytes 32800 | tf_op jit(solution)/shard_map/ppermute | solution.py:214
  231.3 0.6 fusion.2
  (16 shorter events, 0.1 us)
Async XLA Ops:
  0.0 17.3 %copy-start.2 = (s32[12,2048]{1,0:T(8,128)S(1)}, s32[12,2048]{1,0:T(8,128)}, u32[]{:S(2)}) copy-start(s32[12,2048]{1,0:T(8,128)} %param.4) | copy-start | bytes 294916
  5.1 38.6 %collective-permute-start.6 = (bf16[12,128,512]{2,1,0:T(8,128)(2,1)}, bf16[12,128,512]{2,1,0:T(8,128)(2,1)S(1)}, u32[]{:S(2)}, u32[]{:S(2)}) collective-permute-start(bf16[12,128,512]{2,1,0:T(8,128)(2,1)} %get-tuple-element.54), channel_id=1, source_target_pairs={{0,1},{1,2},{2,3},{3,0},{4,5},{5,6},{6,7},{7,4},{8,9},{9,10},{10,1... | collective-permute-start | bytes 4718600 | tf_op jit(solution)/shard_map/ppermute | solution.py:176
  8.0 16.7 %collective-permute-start = (bf16[1,128,512]{2,1,0:T(8,128)(2,1)}, bf16[1,128,512]{2,1,0:T(8,128)(2,1)S(1)}, u32[]{:S(2)}, u32[]{:S(2)}) collective-permute-start(bf16[1,128,512]{2,1,0:T(8,128)(2,1)} %get-tuple-element.62), channel_id=1, source_target_pairs={{0,4},{4,8},{8,12},{12,16},{16,20},{20,24},{24,28},{1,5},{5,9},{9,... | collective-permute-start | bytes 393224 | tf_op jit(solution)/shard_map/ppermute | solution.py:185
  11.9 13.2 %collective-permute-start.1 = (bf16[1,128,512]{2,1,0:T(8,128)(2,1)}, bf16[1,128,512]{2,1,0:T(8,128)(2,1)}, u32[]{:S(2)}, u32[]{:S(2)}) collective-permute-start(bf16[1,128,512]{2,1,0:T(8,128)(2,1)} %get-tuple-element.61), channel_id=1, source_target_pairs={{4,0},{8,4},{12,8},{16,12},{20,16},{24,20},{28,24},{5,1},{9,5},{13... | collective-permute-start | bytes 393224 | tf_op jit(solution)/shard_map/ppermute | solution.py:186
  13.9 111.4 %collective-permute-start.10 = (bf16[12,128,512]{2,1,0:T(8,128)(2,1)}, bf16[12,128,512]{2,1,0:T(8,128)(2,1)}, u32[]{:S(2)}, u32[]{:S(2)}) collective-permute-start(bf16[12,128,512]{2,1,0:T(8,128)(2,1)} %get-tuple-element.56), channel_id=1, source_target_pairs={{0,2},{1,3},{2,0},{3,1},{4,6},{5,7},{6,4},{7,5},{8,10},{9,11},{10,... | collective-permute-start | bytes 4718600 | tf_op jit(solution)/shard_map/ppermute | solution.py:176
  16.2 91.9 %collective-permute-start.2 = (bf16[12,128,512]{2,1,0:T(8,128)(2,1)}, bf16[12,128,512]{2,1,0:T(8,128)(2,1)}, u32[]{:S(2)}, u32[]{:S(2)}) collective-permute-start(bf16[12,128,512]{2,1,0:T(8,128)(2,1)} %get-tuple-element.53), channel_id=1, source_target_pairs={{0,3},{1,0},{2,1},{3,2},{4,7},{5,4},{6,5},{7,6},{8,11},{9,8},{10,9... | collective-permute-start | bytes 4718600 | tf_op jit(solution)/shard_map/ppermute | solution.py:176
  17.3 2.6 %copy-start.1 = (f32[12,2048]{1,0:T(8,128)}, f32[12,2048]{1,0:T(8,128)S(1)}, u32[]{:S(2)}) copy-start(f32[12,2048]{1,0:T(8,128)S(1)} %select_select_fusion) | copy-start | bytes 294916
  20.9 4.2 %copy-start = (f32[3]{0:T(128)S(1)}, f32[3]{0:T(128)}, u32[]{:S(2)}) copy-start(f32[3]{0:T(128)} %velocity.7) | copy-start | bytes 40
  24.7 90.7 %collective-permute-start.7 = (bf16[6,128,128]{2,1,0:T(8,128)(2,1)}, bf16[6,128,128]{2,1,0:T(8,128)(2,1)S(1)}, u32[]{:S(2)}, u32[]{:S(2)}) collective-permute-start(bf16[6,128,128]{2,1,0:T(8,128)(2,1)} %pad_maximum_fusion.2), channel_id=1, source_target_pairs={{0,1},{1,2},{2,3},{3,0},{4,5},{5,6},{6,7},{7,4},{8,9},{9,10},{10,1... | collective-permute-start | bytes 589832 | tf_op jit(solution)/shard_map/ppermute | solution.py:177
  25.1 133.1 %collective-permute-start.13 = (bf16[6,128,128]{2,1,0:T(8,128)(2,1)}, bf16[6,128,128]{2,1,0:T(8,128)(2,1)S(1)}, u32[]{:S(2)}, u32[]{:S(2)}) collective-permute-start(bf16[6,128,128]{2,1,0:T(8,128)(2,1)} %pad_maximum_fusion.3), channel_id=1, source_target_pairs={{0,2},{1,3},{2,0},{3,1},{4,6},{5,7},{6,4},{7,5},{8,10},{9,11},{10,... | collective-permute-start | bytes 589832 | tf_op jit(solution)/shard_map/ppermute | solution.py:177
  43.7 77.0 %collective-permute-start.5 = (bf16[6,128,128]{2,1,0:T(8,128)(2,1)S(1)}, bf16[6,128,128]{2,1,0:T(8,128)(2,1)S(1)}, u32[]{:S(2)}, u32[]{:S(2)}) collective-permute-start(bf16[6,128,128]{2,1,0:T(8,128)(2,1)S(1)} %pad_maximum_fusion.1), channel_id=1, source_target_pairs={{0,3},{1,0},{2,1},{3,2},{4,7},{5,4},{6,5},{7,6},{8,11},{9,8},{10,9... | collective-permute-start | bytes 589832 | tf_op jit(solution)/shard_map/ppermute | solution.py:177
  108.1 20.1 %collective-permute-start.8 = (bf16[1,128,512]{2,1,0:T(8,128)(2,1)S(1)}, bf16[1,128,512]{2,1,0:T(8,128)(2,1)S(1)}, u32[]{:S(2)}, u32[]{:S(2)}) collective-permute-start(bf16[1,128,512]{2,1,0:T(8,128)(2,1)S(1)} %get-tuple-element.64), channel_id=1, source_target_pairs={{0,4},{4,8},{8,12},{12,16},{16,20},{20,24},{24,28},{1,5},{5,9},{9,... | collective-permute-start | bytes 393224 | tf_op jit(solution)/shard_map/ppermute | solution.py:185
  115.4 16.4 %collective-permute-start.9 = (bf16[1,128,512]{2,1,0:T(8,128)(2,1)S(1)}, bf16[1,128,512]{2,1,0:T(8,128)(2,1)S(1)}, u32[]{:S(2)}, u32[]{:S(2)}) collective-permute-start(bf16[1,128,512]{2,1,0:T(8,128)(2,1)S(1)} %get-tuple-element.63), channel_id=1, source_target_pairs={{4,0},{8,4},{12,8},{16,12},{20,16},{24,20},{28,24},{5,1},{9,5},{13... | collective-permute-start | bytes 393224 | tf_op jit(solution)/shard_map/ppermute | solution.py:186
  120.7 22.7 %collective-permute-start.3 = (bf16[1,128,512]{2,1,0:T(8,128)(2,1)S(1)}, bf16[1,128,512]{2,1,0:T(8,128)(2,1)S(1)}, u32[]{:S(2)}, u32[]{:S(2)}) collective-permute-start(bf16[1,128,512]{2,1,0:T(8,128)(2,1)S(1)} %get-tuple-element.58), channel_id=1, source_target_pairs={{0,4},{4,8},{8,12},{12,16},{16,20},{20,24},{24,28},{1,5},{5,9},{9,... | collective-permute-start | bytes 393224 | tf_op jit(solution)/shard_map/ppermute | solution.py:185
  125.2 18.2 %collective-permute-start.4 = (bf16[1,128,512]{2,1,0:T(8,128)(2,1)S(1)}, bf16[1,128,512]{2,1,0:T(8,128)(2,1)S(1)}, u32[]{:S(2)}, u32[]{:S(2)}) collective-permute-start(bf16[1,128,512]{2,1,0:T(8,128)(2,1)S(1)} %get-tuple-element.57), channel_id=1, source_target_pairs={{4,0},{8,4},{12,8},{16,12},{20,16},{24,20},{28,24},{5,1},{9,5},{13... | collective-permute-start | bytes 393224 | tf_op jit(solution)/shard_map/ppermute | solution.py:186
  128.2 30.0 %collective-permute-start.11 = (bf16[1,128,512]{2,1,0:T(8,128)(2,1)S(1)}, bf16[1,128,512]{2,1,0:T(8,128)(2,1)S(1)}, u32[]{:S(2)}, u32[]{:S(2)}) collective-permute-start(bf16[1,128,512]{2,1,0:T(8,128)(2,1)S(1)} %get-tuple-element.60), channel_id=1, source_target_pairs={{0,4},{4,8},{8,12},{12,16},{16,20},{20,24},{24,28},{1,5},{5,9},{9,... | collective-permute-start | bytes 393224 | tf_op jit(solution)/shard_map/ppermute | solution.py:185
  131.8 26.4 %collective-permute-start.12 = (bf16[1,128,512]{2,1,0:T(8,128)(2,1)S(1)}, bf16[1,128,512]{2,1,0:T(8,128)(2,1)S(1)}, u32[]{:S(2)}, u32[]{:S(2)}) collective-permute-start(bf16[1,128,512]{2,1,0:T(8,128)(2,1)S(1)} %get-tuple-element.59), channel_id=1, source_target_pairs={{4,0},{8,4},{12,8},{16,12},{20,16},{24,20},{28,24},{5,1},{9,5},{13... | collective-permute-start | bytes 393224 | tf_op jit(solution)/shard_map/ppermute | solution.py:186
  171.2 6.1 %collective-permute-start.20 = (f32[64,512]{1,0:T(8,128)S(1)}, f32[64,512]{1,0:T(8,128)S(1)}, u32[]{:S(2)}, u32[]{:S(2)}) collective-permute-start(f32[64,512]{1,0:T(8,128)S(1)} %get-tuple-element.66), channel_id=1, source_target_pairs={{0,28},{4,0},{8,4},{12,8},{16,12},{20,16},{24,20},{28,24},{1,29},{... | collective-permute-start | bytes 393224 | tf_op jit(solution)/shard_map/ppermute | solution.py:211
  171.7 7.6 %collective-permute-start.19 = (f32[64,512]{1,0:T(8,128)S(1)}, f32[64,512]{1,0:T(8,128)S(1)}, u32[]{:S(2)}, u32[]{:S(2)}) collective-permute-start(f32[64,512]{1,0:T(8,128)S(1)} %get-tuple-element.67), channel_id=1, source_target_pairs={{0,24},{4,28},{8,0},{12,4},{16,8},{20,12},{24,16},{28,20},{1,25},{... | collective-permute-start | bytes 393224 | tf_op jit(solution)/shard_map/ppermute | solution.py:211
  174.0 8.6 %collective-permute-start.18 = (f32[64,512]{1,0:T(8,128)S(1)}, f32[64,512]{1,0:T(8,128)S(1)}, u32[]{:S(2)}, u32[]{:S(2)}) collective-permute-start(f32[64,512]{1,0:T(8,128)S(1)} %get-tuple-element.68), channel_id=1, source_target_pairs={{0,20},{4,24},{8,28},{12,0},{16,4},{20,8},{24,12},{28,16},{1,21},{... | collective-permute-start | bytes 393224 | tf_op jit(solution)/shard_map/ppermute | solution.py:211
  175.4 9.9 %collective-permute-start.17 = (f32[64,512]{1,0:T(8,128)S(1)}, f32[64,512]{1,0:T(8,128)S(1)}, u32[]{:S(2)}, u32[]{:S(2)}) collective-permute-start(f32[64,512]{1,0:T(8,128)S(1)} %get-tuple-element.69), channel_id=1, source_target_pairs={{0,16},{4,20},{8,24},{12,28},{16,0},{20,4},{24,8},{28,12},{1,17},{... | collective-permute-start | bytes 393224 | tf_op jit(solution)/shard_map/ppermute | solution.py:211
  176.7 10.0 %collective-permute-start.16 = (f32[64,512]{1,0:T(8,128)S(1)}, f32[64,512]{1,0:T(8,128)S(1)}, u32[]{:S(2)}, u32[]{:S(2)}) collective-permute-start(f32[64,512]{1,0:T(8,128)S(1)} %get-tuple-element.70), channel_id=1, source_target_pairs={{0,12},{4,16},{8,20},{12,24},{16,28},{20,0},{24,4},{28,8},{1,13},{... | collective-permute-start | bytes 393224 | tf_op jit(solution)/shard_map/ppermute | solution.py:211
  177.4 9.3 %collective-permute-start.15 = (f32[64,512]{1,0:T(8,128)S(1)}, f32[64,512]{1,0:T(8,128)S(1)}, u32[]{:S(2)}, u32[]{:S(2)}) collective-permute-start(f32[64,512]{1,0:T(8,128)S(1)} %get-tuple-element.71), channel_id=1, source_target_pairs={{0,8},{4,12},{8,16},{12,20},{16,24},{20,28},{24,0},{28,4},{1,9},{5... | collective-permute-start | bytes 393224 | tf_op jit(solution)/shard_map/ppermute | solution.py:211
  179.3 7.4 %collective-permute-start.14 = (f32[64,512]{1,0:T(8,128)S(1)}, f32[64,512]{1,0:T(8,128)S(1)}, u32[]{:S(2)}, u32[]{:S(2)}) collective-permute-start(f32[64,512]{1,0:T(8,128)S(1)} %get-tuple-element.65), channel_id=1, source_target_pairs={{0,4},{4,8},{8,12},{12,16},{16,20},{20,24},{24,28},{28,0},{1,5},{5... | collective-permute-start | bytes 393224 | tf_op jit(solution)/shard_map/ppermute | solution.py:211
  186.8 39.8 %collective-permute-start.23 = (f32[64,128]{1,0:T(8,128)S(1)}, f32[64,128]{1,0:T(8,128)S(1)}, u32[]{:S(2)}, u32[]{:S(2)}) collective-permute-start(f32[64,128]{1,0:T(8,128)S(1)} %get-tuple-element.81), channel_id=1, source_target_pairs={{0,3},{1,0},{2,1},{3,2},{4,7},{5,4},{6,5},{7,6},{8,11},{9,8},{10,9... | collective-permute-start | bytes 98312 | tf_op jit(solution)/shard_map/ppermute | solution.py:214
  214.8 13.3 %collective-permute-start.22 = (f32[64,128]{1,0:T(8,128)S(1)}, f32[64,128]{1,0:T(8,128)S(1)}, u32[]{:S(2)}, u32[]{:S(2)}) collective-permute-start(f32[64,128]{1,0:T(8,128)S(1)} %get-tuple-element.82), channel_id=1, source_target_pairs={{0,2},{1,3},{2,0},{3,1},{4,6},{5,7},{6,4},{7,5},{8,10},{9,11},{10,... | collective-permute-start | bytes 98312 | tf_op jit(solution)/shard_map/ppermute | solution.py:214
  226.4 4.8 %collective-permute-start.21 = (f32[64,128]{1,0:T(8,128)S(1)}, f32[64,128]{1,0:T(8,128)S(1)}, u32[]{:S(2)}, u32[]{:S(2)}) collective-permute-start(f32[64,128]{1,0:T(8,128)S(1)} %get-tuple-element.80), channel_id=1, source_target_pairs={{0,1},{1,2},{2,3},{3,0},{4,5},{5,6},{6,7},{7,4},{8,9},{9,10},{10,1... | collective-permute-start | bytes 98312 | tf_op jit(solution)/shard_map/ppermute | solution.py:214

commit v2 on v0

v2 whole, which is shorter than its diff:
```python
import functools
import math

import jax
import jax.numpy as jnp
from jax import lax
from jax.experimental import pallas as pl
from jax.experimental.pallas import tpu as pltpu
from jax.sharding import PartitionSpec as P

NZ = 64
LANES = 128
SUB = 16
BF = jnp.bfloat16
F32 = jnp.float32
VMEM = pltpu.VMEM


def product(left, right):
    return lax.dot_general(left, right, (((1,), (1,)), ((), ())), preferred_element_type=F32)


def apply_rows(i, eps, velocity, w, wh, xs, h, a, tiles, rows, off, count, flip):
    span = rows + 2
    xp, xm = eps - 0.5 * velocity[0], eps + 0.5 * velocity[0]
    yp, ym = eps - 0.5 * velocity[1], eps + 0.5 * velocity[1]
    zp, zm = eps - 0.5 * velocity[2], eps + 0.5 * velocity[2]
    lane = lax.broadcasted_iota(jnp.int32, (SUB, LANES), 1)
    low = lane < NZ
    zps = jnp.where(lane % NZ == NZ - 1, 0.0, zp)
    zms = jnp.where(lane % NZ == 0, 0.0, zm)
    own = jnp.where(low, yp, ym)
    other = jnp.where(low, ym, yp)
    at_end = jnp.where(flip == 0, 1.0, 0.0)
    at_start = 1.0 - at_end

    def body(j, carry):
        start = pl.multiple_of(j * SUB, SUB)
        source = pl.ds(start, SUB)
        target = pl.ds(pl.multiple_of(j * SUB + off, SUB), SUB)
        halo = h(i, source).astype(F32)
        ends = (pltpu.roll(halo, NZ, 1), halo)
        starts = (halo, pltpu.roll(halo, NZ, 1))
        center = [
            [xs[t * span + 2 * i + r, source, :].astype(F32) for t in range(tiles)] for r in range(4)
        ]
        firsts, lasts = [], []
        for r in (0, 1):
            mid = center[r + 1]
            turned = [pltpu.roll(c, NZ, 1) for c in mid]
            lasts.append(turned[-1] if r == 0 else mid[-1])
            firsts.append(mid[0] if r == 0 else turned[0])
            for t in range(tiles):
                c = mid[t]
                behind = turned[t + 1] if t + 1 < tiles else at_end * ends[r]
                before = turned[t - 1] if t > 0 else at_start * starts[r]
                value = xp * center[r + 2][t] + xm * center[r][t]
                value = value + own * turned[t] + other * jnp.where(low, before, behind)
                value = value + zps * pltpu.roll(c, LANES - 1, 1) + zms * pltpu.roll(c, 1, 1)
                value = (value - (6.0 * eps) * c) * w[2 * i + r, :, t * LANES : (t + 1) * LANES]
                a[t * rows + 2 * i + r, target, :] = value.astype(BF)
        last = jnp.where(low, lasts[0], lasts[1])
        first = jnp.where(low, firsts[0], firsts[1])
        side = at_end * ym * last + at_start * yp * first
        a[tiles * rows + i, target, :] = (wh[i] * side).astype(BF)
        return carry

    lax.fori_loop(0, count // SUB, body, 0)


def phase_kernel(cfg, *refs):
    refs = list(refs)
    d, off, count, whole = cfg["d"], cfg["off"], cfg["count"], cfg["whole"]
    rows, tiles = cfg["rows"], cfg["tiles"]
    steps, end, mine, span = rows // 2, off + count, slice(off, off + count), rows + 2
    last, part = cfg["last"], count < whole
    take = lambda k: [refs.pop(0) for _ in range(k)]
    order, velocity, w, wh, xd, xu = take(6)
    parts = take(cfg["n_parts"])
    old = [take(2) for _ in range(cfg["n_old"])]
    prev = take(2) if cfg["prev"] else None
    gin = take(1)[0] if cfg["gin"] else None
    xo = take(1)[0] if part and not last else None
    a = None if last else take(1)[0]
    (gout,) = take(1)
    if last:
        (a,) = take(1)
    xs, t2 = take(2)
    t1 = take(1)[0] if cfg["t1"] else None
    g = take(1)[0] if last else gout

    edge = cfg["edge"]
    if part:
        rim, inner = parts[0], parts[-1]
        deep = rows - 2
        base = tiles * deep + (off // count) * (2 * tiles + rows // 2)
        halo_of = lambda i, at: rim[base + 2 * tiles + i, at, :]
        inside = slice(0, count)
    else:
        inside = mine
        halo_of = lambda i, at: parts[0][tiles * rows + i, at, :]
    for t in range(tiles):
        xs[t * span] = xd[edge + t]
        xs[t * span + rows + 1] = xu[edge + t]
        if part:
            xs[t * span + 1] = rim[base + 2 * t]
            xs[t * span + rows] = rim[base + 2 * t + 1]
            xs[t * span + 2 : t * span + rows] = inner[t * deep : (t + 1) * deep]
        else:
            xs[t * span + 1 : t * span + rows + 1] = parts[0][t * rows : (t + 1) * rows]
    t2[...] = jnp.zeros_like(t2)
    if t1 is not None:
        t1[...] = jnp.zeros_like(t1)
    if part:
        a[...] = jnp.zeros_like(a) if prev is None or last else prev[1][...]

    def padded(value, before=None):
        pieces = [value]
        if off:
            pieces.insert(0, jnp.zeros((off, LANES), BF) if before is None else before)
        if end < whole:
            pieces.append(jnp.zeros((whole - end, LANES), BF))
        return pieces[0] if len(pieces) == 1 else jnp.concatenate(pieces, axis=0)

    def body(i, carry):
        flip = order[1]
        apply_rows(
            i, cfg["eps"], velocity, w, wh, xs, halo_of, a, tiles, rows, off, count, flip
        )
        picks = [t * rows + 2 * i + r for r in (0, 1) for t in range(tiles)]
        picks.append(tiles * rows + i)
        wide = lambda ref: jnp.concatenate([ref[k] for k in picks], axis=1)
        new = [xs[t * span + 2 * i + r + 1] for r in (0, 1) for t in range(tiles)]
        new.append(halo_of(i, inside))
        if part:
            before = [None if prev is None else prev[0][k, :off, :] for k in picks]
            both = [padded(v, u) for v, u in zip(new, before)]
            if xo is not None:
                for k, v in zip(picks, both):
                    xo[k] = v
        else:
            both = new
        fresh = [padded(v) for v in new]
        mark = [padded(a[k, mine, :]) for k in picks]
        tall = [wide(ox) for ox, _ in old] + [jnp.concatenate(both, axis=1)]
        t2[...] += product(jnp.concatenate(tall, axis=0), jnp.concatenate(mark, axis=1))
        tall = [wide(oa) for _, oa in old] + ([wide(prev[1])] if prev is not None else [])
        if tall:
            t1[...] += product(jnp.concatenate(tall, axis=0), jnp.concatenate(fresh, axis=1))
        return carry

    lax.fori_loop(0, steps, body, 0)

    g[...] = jnp.zeros_like(g) if gin is None else gin[...]
    block = lambda k: slice(k * whole, (k + 1) * whole)
    names = [*cfg["old"], d]
    for k, o in enumerate(names):
        g[block(o), block(d)] += t2[block(k), :]
    for k, o in enumerate(names if prev is not None else names[:-1]):
        g[block(d), block(o)] += t1[block(k), :].T
    if last:
        q = order[0]
        n, space = cfg["n"], cfg["space"]
        share = gout.shape[1]
        per = whole // share
        for s in range(space):
            first = pl.multiple_of(((s // per) ^ q) * whole + (s % per) * share, share)
            for z in range(n):
                start = pl.multiple_of((z ^ q) * whole, whole)
                gout[s * n + z] = g[pl.ds(first, share), pl.ds(start, whole)].astype(BF)


def phase(cfg, order, velocity, w, wh, xd, xu, parts, old, prev, gin):
    rows, tiles, whole, count = cfg["rows"], cfg["tiles"], cfg["whole"], cfg["count"]
    size, last, part = cfg["n_blocks"] * whole, cfg["last"], count < whole
    kept = jax.ShapeDtypeStruct((tiles * rows + rows // 2, whole, LANES), BF)
    args = [order, velocity, w, wh, xd, xu, *parts]
    for group in [*old, *([prev] if prev is not None else [])]:
        args += list(group)
    if gin is not None:
        args.append(gin)
    scratch = []
    if last:
        gshape = jax.ShapeDtypeStruct((cfg["space"] * cfg["n"], size // cfg["space"], whole), BF)
        out_shape = [gshape]
        scratch.append(VMEM(kept.shape, BF))
    else:
        out_shape = [kept] * (2 if part else 1) + [jax.ShapeDtypeStruct((size, size), F32)]
    seconds = len(old) + (prev is not None)
    scratch.append(VMEM((tiles * (rows + 2), count, LANES), BF))
    scratch.append(VMEM(((len(old) + 1) * whole, whole), F32))
    if seconds:
        scratch.append(VMEM((seconds * whole, whole), F32))
    if last:
        scratch.append(VMEM((size, size), F32))
    elements = rows * count * tiles * LANES
    cfg = dict(cfg, n_parts=len(parts), n_old=len(old), prev=prev is not None, gin=gin is not None, t1=bool(seconds))
    vmem = pl.BlockSpec(memory_space=VMEM)
    smem = pl.BlockSpec(memory_space=pltpu.SMEM)
    outs = pl.pallas_call(
        functools.partial(phase_kernel, cfg),
        in_specs=[smem, smem] + [vmem] * (len(args) - 2),
        out_specs=[vmem] * len(out_shape),
        out_shape=out_shape,
        scratch_shapes=scratch,
        compiler_params=pltpu.CompilerParams(vmem_limit_bytes=cfg["vmem"] << 20),
        cost_estimate=pl.CostEstimate(
            flops=20 * elements + 4 * size * elements,
            bytes_accessed=6 * elements,
            transcendentals=0,
        ),
    )(*args)
    if last:
        return None, outs[0]
    return (outs[0] if part else parts[0], outs[-2]), outs[-1]


def pack_kernel(jobs, n, rows, tiles, order, field, *refs):
    outs = refs[: len(jobs)]
    line, packed, sem, line_sem, out_sem = refs[len(jobs) :]
    q, flip = order[0], order[1]
    copies, halos = [], []
    for k, (d, kind, a, b) in enumerate(jobs):
        owner = q ^ d
        base = owner * tiles * LANES
        cut = lambda t: pl.ds(pl.multiple_of(base + t * LANES, LANES), LANES)
        deep = rows - 2
        for t in range(tiles):
            if kind == "full":
                copies.append((field.at[:, :, cut(t)], outs[k].at[t * rows : (t + 1) * rows]))
                continue
            copies.append((field.at[1 : rows - 1, a:b, cut(t)], outs[k].at[t * deep : (t + 1) * deep]))
            if kind == "rim":
                for c in (0, 1):
                    first = tiles * deep + c * (2 * tiles + rows // 2)
                    half = slice(c * (b - a), (c + 1) * (b - a))
                    copies.append((field.at[0, half, cut(t)], outs[k].at[first + 2 * t]))
                    copies.append((field.at[rows - 1, half, cut(t)], outs[k].at[first + 2 * t + 1]))
        if kind == "full":
            halos.append((k, owner, rows * tiles, slice(0, line.shape[2])))
        elif kind == "rim":
            for c in (0, 1):
                first = tiles * deep + c * (2 * tiles + rows // 2) + 2 * tiles
                halos.append((k, owner, first, slice(c * (b - a), (c + 1) * (b - a))))
    copies = [pltpu.make_async_copy(src, dst, sem.at[m]) for m, (src, dst) in enumerate(copies)]
    lines = []
    for m, (k, owner, _, _) in enumerate(halos):
        at = jnp.where(flip == 0, jnp.minimum((owner + 1) * tiles, n * tiles - 1),
                       jnp.maximum(owner * tiles - 1, 0))
        at = pl.ds(pl.multiple_of(at * LANES, LANES), LANES)
        lines.append(pltpu.make_async_copy(field.at[:, :, at], line.at[m], line_sem.at[m]))
        lines[-1].start()
    for c in copies:
        c.start()
    stores = []
    for m, (k, owner, first, modes) in enumerate(halos):
        lines[m].wait()
        low = lax.broadcasted_iota(jnp.int32, line.shape[2:], 1) < NZ
        none = jnp.where(flip == 0, owner == n - 1, owner == 0)
        for i in range(rows // 2):
            one, two = line[m, 2 * i].astype(F32), line[m, 2 * i + 1].astype(F32)
            front = jnp.where(low, one, pltpu.roll(two, NZ, 1))
            back = jnp.where(low, pltpu.roll(one, NZ, 1), two)
            value = jnp.where(flip == 0, front, back)
            packed[m, i] = jnp.where(none, 0.0, value).astype(BF)
        stores.append(
            pltpu.make_async_copy(
                packed.at[m, :, modes], outs[k].at[first : first + rows // 2], out_sem.at[m]
            )
        )
        stores[-1].start()
    for c in copies + stores:
        c.wait()


def pack(jobs, n, tiles, order, field):
    rows, count, _ = field.shape
    shapes, pieces, lines = [], 0, 0
    for d, kind, a, b in jobs:
        if kind == "full":
            shapes.append((tiles * rows + rows // 2, count, LANES))
            pieces += tiles
            lines += 1
        elif kind == "rim":
            shapes.append((tiles * (rows - 2) + 2 * (tiles * 2 + rows // 2), b - a, LANES))
            pieces += 5 * tiles
            lines += 2
        else:
            shapes.append((tiles * (rows - 2), b - a, LANES))
            pieces += tiles
    anywhere = pl.BlockSpec(memory_space=pltpu.HBM)
    lines = max(lines, 1)
    return pl.pallas_call(
        functools.partial(pack_kernel, jobs, n, rows, tiles),
        in_specs=[pl.BlockSpec(memory_space=pltpu.SMEM), anywhere],
        out_specs=[anywhere] * len(jobs),
        out_shape=[jax.ShapeDtypeStruct(s, BF) for s in shapes],
        scratch_shapes=[
            VMEM((lines, rows, count, LANES), BF),
            VMEM((lines, rows // 2, count, LANES), BF),
            pltpu.SemaphoreType.DMA((pieces,)),
            pltpu.SemaphoreType.DMA((lines,)),
            pltpu.SemaphoreType.DMA((lines,)),
        ],
        compiler_params=pltpu.CompilerParams(vmem_limit_bytes=16 << 20),
    )(order, field)


def spread_out(total, n, space, q, count):
    share = n * count // space
    out = []
    for s in range(space):
        start = ((s * share) // count ^ q) * count + (s * share) % count
        rows = lax.dynamic_slice_in_dim(total, start, share, axis=0)
        out += [lax.dynamic_slice_in_dim(rows, (z ^ q) * count, count, axis=1) for z in range(n)]
    return jnp.stack(out)


def after(value, token):
    return lax.optimization_barrier((value, token))[0]


def local(modes, phases, velocity):
    space, n = lax.axis_size("space"), lax.axis_size("mode")
    sp, q = lax.axis_index("space"), lax.axis_index("mode")
    count, rows, plane = modes.shape
    width = plane // n
    tiles = width // LANES
    eps = 1.0 / math.sqrt(space * rows * plane)
    field = jnp.transpose(modes, (1, 0, 2))
    flip = sp & 1

    weight = jnp.where(phases == 0, 0.1, jnp.where(phases == 1, 1.0, 0.5)).astype(F32)
    w = lax.dynamic_slice_in_dim(weight, q * width, width, axis=1)[:, None, :]

    def line_start(owner):
        end = jnp.minimum((owner + 1) * width, plane - NZ)
        return jnp.where(flip == 0, end, jnp.maximum(owner * width - NZ, 0))

    wh = lax.dynamic_slice_in_dim(weight, line_start(q), NZ, axis=1).reshape(rows // 2, 1, LANES)

    def slab(source, owner):
        return lax.dynamic_slice_in_dim(source, owner * width, width, axis=2)

    def line(source, owner):
        part = lax.dynamic_slice_in_dim(source, line_start(owner), NZ, axis=2)
        none = jnp.where(flip == 0, owner == n - 1, owner == 0)
        part = jnp.where(none, jnp.zeros_like(part), part)
        return jnp.concatenate([part[0::2], part[1::2]], axis=-1)

    up = [(i, i + 1) for i in range(space - 1)]
    down = [(i + 1, i) for i in range(space - 1)]

    def edges(first, last):
        return lax.ppermute(last, "space", up), lax.ppermute(first, "space", down)

    def swap(part, d):
        return lax.ppermute(part, "mode", [(i, i ^ d) for i in range(n)])

    order = jnp.stack([q, flip])
    base = dict(rows=rows, tiles=tiles, eps=eps, n=n, space=space, last=False, off=0, d=0, vmem=16, edge=0)
    if n != 4:
        xs, hs = [slab(field, q)], [line(field, q)]
        for d in range(1, n):
            xs.append(swap(slab(field, q ^ d), d))
            hs.append(swap(line(field, q ^ d), d))
        x, h = jnp.concatenate(xs, axis=1), jnp.concatenate(hs, axis=1)
        cfg = dict(base, whole=n * count, count=n * count, n_blocks=1, old=[], vmem=40)
        xd, xu = edges(x[:1], x[rows - 1 :])
        x = jnp.concatenate([x, h], axis=0)
        _, total = phase(cfg, order, velocity, w, wh, xd, xu, [x], [], None, None)
        tiles = spread_out(total, n, space, q, count)
    else:
        half = count // 2
        p3, p1 = pack([(3, "full", 0, 0), (1, "full", 0, 0)], n, tiles, order, field)
        x3, x1 = swap(p3, 3), swap(p1, 1)
        jobs = [(2, "rim", 0, half), (2, "inner", half, count), (0, "full", 0, 0)]
        p2, p2b, x0 = pack(jobs, n, tiles, order, after(field, p1))
        front, back = swap(p2, 2), swap(p2b, 2)
        pick = lambda x, r: [x[t * rows + r][None] for t in range(tiles)]
        join = lambda pieces: jnp.concatenate(pieces, axis=0)
        base = dict(base, whole=count, n_blocks=n)
        full = dict(base, count=count)
        xd, xu = edges(join(pick(x0, 0)), join(pick(x0, rows - 1)))
        kept, g = phase(dict(full, old=[]), order, velocity, w, wh, xd, xu, [x0], [], None, None)
        names, old = [0], [kept]
        x3 = after(x3, g)
        xd, xu = edges(
            join(pick(x3, 0) + pick(x1, 0)), join(pick(x3, rows - 1) + pick(x1, rows - 1))
        )
        for k, (d, x) in enumerate(((3, x3), (1, x1))):
            cfg = dict(full, d=d, old=list(names), edge=k * tiles)
            kept, g = phase(cfg, order, velocity, w, wh, xd, xu, [x], old, None, g)
            names, old = [*names, d], [*old, kept]
        front = after(front, g)
        start, step = tiles * (rows - 2), 2 * tiles + rows // 2
        rims = [front[start + c * step : start + c * step + 2 * tiles] for c in (0, 1)]
        xd, xu = edges(join([r[::2] for r in rims]), join([r[1::2] for r in rims]))
        part = dict(base, d=2, count=half, old=names)
        kept, g = phase(part, order, velocity, w, wh, xd, xu, [front], old, None, g)
        back = after(back, g)
        part = dict(part, off=half, edge=tiles, last=True)
        _, g = phase(part, order, velocity, w, wh, xd, xu, [front, back], old, kept, g)
        tiles = g
    arrived = lax.all_to_all(tiles, ("space", "mode"), split_axis=0, concat_axis=0, tiled=True)
    return jnp.sum(arrived.astype(F32), axis=0) * eps


def solution(mesh):
    placed = (P("mode", "space", None), P("space", None), P())
    return jax.shard_map(
        local, mesh=mesh, in_specs=placed, out_specs=P("space", "mode"), check_vma=False
    )
```

time: 493 us -> 201 us (0.41)
  waiting for transfers between devices: 373 us -> 87.3 us
  Pallas kernels: 0 us -> 51.5 us
  other arithmetic: 47.1 us -> 3.07 us
  local copies, waits for them, and re-layouts: 36.4 us -> 13.4 us
  blocking collectives: 0 us -> 19.8 us
  starting transfers between devices: 6.47 us -> 24.2 us
  matrix products: 15.1 us -> 0 us
  between operations: 13.4 us -> 0.22 us
    all_gather x1 -> x0, waiting for transfers between devices: 332 us -> none  [local(): lax.all_gather(modes, 'mode', axis=0, tiled=True)]
    ppermute x2 -> x10, waiting for transfers between devices: 9.15 us -> 87.3 us  [the longest x4 80.1 us: swap(): return lax.ppermute(part, 'mode', [(i, i ^ d) for i in range(n)])]
    pallas_call x0 -> x7, Pallas kernels: none -> 51.5 us  [the longest x5 46 us: phase(): pl.pallas_call(functools.partial(phase_kernel, cfg), in_specs=[smem, smem...]
    slice x4 -> x3, local copies, waits for them, and re-layouts: 35.5 us -> 1.02 us  [the longest x1 0.99 us: local(): front[start + c * step:start + c * step + 2 * tiles]]
    dot_general x1 -> x0, other arithmetic: 34.3 us -> none  [inner_rows(): lax.dot_general(left_flat, right_flat, (((1,), (1,)), ((), ())), preferre...]
    reduce_scatter x1 -> x0, waiting for transfers between devices: 31.3 us -> none  [local(): lax.psum_scatter(partial_cols, 'space', scatter_dimension=0, tiled=True)]
    all_to_all x0 -> x1, blocking collectives: none -> 19.8 us  [local(): lax.all_to_all(tiles, ('space', 'mode'), split_axis=0, concat_axis=0, til...]
    ppermute x2 -> x10, starting transfers between devices: 6.43 us -> 24.2 us  [the longest x6 18.7 us: edges(): return (lax.ppermute(last, 'space', up), lax.ppermute(first, 'space', down))]
  transfers between devices with their start and end apart: 4 -> 10, of which waited for: 4 -> 6; matrix products, arithmetic and copies ran while one was open for 17% -> 5% of each run, Pallas kernels for 0% -> 20%
where the time goes in v2:
time: 201 us; the launch traced here: 200 us
  waiting for transfers between devices  87.3 us (43%)
  Pallas kernels  51.5 us (26%)
  starting transfers between devices  24.2 us (12%)
  blocking collectives  19.8 us (10%)
  local copies, waits for them, and re-layouts  13.4 us (7%)
  other arithmetic  3.07 us (2%)
    ppermute x4, waiting for transfers between devices, swap(): return lax.ppermute(part, 'mode', [(i, i ^ d) for i in range(n)])  80.1 us
    pallas_call x5, Pallas kernels, phase(): pl.pallas_call(functools.partial(phase_kernel, cfg), in_specs=[smem, smem...  46 us
    all_to_all x1, blocking collectives, local(): lax.all_to_all(tiles, ('space', 'mode'), split_axis=0, concat_axis=0, til...  19.8 us
    ppermute x6, starting transfers between devices, edges(): return (lax.ppermute(last, 'space', up), lax.ppermute(first, 'space', down))  18.7 us
    unnamed x19, local copies, waits for them, and re-layouts  7.48 us
    ppermute x6, waiting for transfers between devices, edges(): return (lax.ppermute(last, 'space', up), lax.ppermute(first, 'space', down))  7.23 us
    pallas_call x2, Pallas kernels, pack(): pl.pallas_call(functools.partial(pack_kernel, jobs, n, rows, tiles), in_s...  5.53 us
    ppermute x4, starting transfers between devices, swap(): return lax.ppermute(part, 'mode', [(i, i ^ d) for i in range(n)])  5.48 us
  transfers between devices with their start and end apart: 10, of which 6 were waited for; matrix products, arithmetic and copies ran while one was open for 5% of the time, Pallas kernels for 20%

profile of v2, /device:TPU:1, one launch (start us, length us, event | category | flops | bytes accessed | tf_op | source)
XLA Modules:
  0.0 199.6 jit_solution(11084301307138424612)
XLA Ops:
  0.0 0.1 pad_add_fusion.order.refs_0_
  0.1 0.0 copy-start
  0.1 2.8 %copy-done = bf16[128,12,2048]{2,0,1:T(8,128)(2,1)S(1)} copy-done((bf16[128,12,2048]{2,0,1:T(8,128)(2,1)S(1)}, bf16[128,12,2048]{2,0,1:T(8,128)(2,1)}, u32[]{:S(2)}) %copy-start) | copy-done | bytes 6291480
  2.9 2.7 %shard_map.37 = (bf16[54,128,128]{2,1,0:T(8,128)(2,1)}, bf16[54,128,128]{2,1,0:T(8,128)(2,1)}) custom-call(s32[2]{0:T(128)S(1)} %pad_add_fusion.order.refs_0_, bf16[12,128,2048]{2,1,0:T(8,128)(2,1)S(1)} %bitcast.3), custom_call_target="tpu_custom_call" | custom-call | tf_op jit(solution)/shard_map/pallas_call | solution.py:293
  5.6 4.2 %collective-permute-start.1 = (bf16[54,128,128]{2,1,0:T(8,128)(2,1)}, bf16[54,128,128]{2,1,0:T(8,128)(2,1)S(1)}, u32[]{:S(2)}, u32[]{:S(2)}) collective-permute-start(bf16[54,128,128]{2,1,0:T(8,128)(2,1)} %get-tuple-element.26), channel_id=1, source_target_pairs={{0,3},{1,2},{2,1},{3,0},{4,7},{5,6},{6,5},{7,4},{8,11},{9,10},{10,... | collective-permute-start | bytes 5308424 | tf_op jit(solution)/shard_map/ppermute | solution.py:358
  9.8 0.0 copy-start.2
  9.8 0.0 collective-permute-start.4
  9.8 2.8 %shard_map.38 = (bf16[68,64,128]{2,1,0:T(8,128)(2,1)}, bf16[40,64,128]{2,1,0:T(8,128)(2,1)S(1)}, bf16[54,128,128]{2,1,0:T(8,128)(2,1)S(1)}) custom-call(s32[2]{0:T(128)S(1)} %pad_add_fusion.order.refs_0_, bf16[12,128,2048]{2,1,0:T(8,128)(2,1)S(1)} %bitcast.4), custom_call_target="tpu_custom_call" | custom-call | tf_op jit(solution)/shard_map/pallas_call | solution.py:293
  12.6 0.0 copy-start.3
  12.6 0.9 copy-done.3
  13.6 0.7 pad_maximum_fusion
  14.2 4.0 %collective-permute-start.2 = (bf16[4,128,128]{2,1,0:T(8,128)(2,1)}, bf16[4,128,128]{2,1,0:T(8,128)(2,1)}, u32[]{:S(2)}, u32[]{:S(2)}) collective-permute-start(bf16[4,128,128]{2,1,0:T(8,128)(2,1)} %pad_maximum_fusion), channel_id=1, source_target_pairs={{0,4},{4,8},{8,12},{12,16},{16,20},{20,24},{24,28},{1,5},{5,9},{9,... | collective-permute-start | bytes 393224 | tf_op jit(solution)/shard_map/ppermute | solution.py:355
  18.2 0.7 pad_maximum_fusion.1
  18.9 1.9 collective-permute-start.3
  20.8 0.6 collective-permute-start
  21.3 0.9 select_select_fusion
  22.3 0.0 copy-start.5
  22.3 0.6 copy-done.5
  22.9 0.6 constant_dynamic-slice_fusion.1
  23.5 1.4 broadcast_in_dim.18.refs_2_
  24.9 1.4 constant_dynamic-slice_fusion
  26.3 0.8 reshape.3.refs_3_
  27.1 0.0 collective-permute-done.2.refs_4_
  27.1 0.0 collective-permute-done.3.refs_5_
  27.1 0.0 copy-done.2
  27.1 0.0 copy-start.1
  27.1 0.7 copy-done.1
  27.8 0.0 copy-start.4
  27.8 8.0 %shard_map.39 = (bf16[54,128,128]{2,1,0:T(8,128)(2,1)S(1)}, f32[512,512]{1,0:T(8,128)S(1)}) custom-call(s32[2]{0:T(128)S(1)} %pad_add_fusion.order.refs_0_, f32[3]{0:T(128)S(1)} %copy-done.2, f32[12,1,512]{2,1,0:T(1,128)S(1)} %copy-done.1, f32[6,1,128]{2,1,0:T(1,128)S(1)} %reshape.3.refs_3_, bf16[4,128,128]{2,1,0:T(8,128)(2,1)} %collective-permute-done.2.refs_4_, ...), custom_call_target="tpu_custom_call" | custom-call | flops 1626341376 | bytes 4718592 | tf_op jit(solution)/shard_map/pallas_call | solution.py:200
  35.9 12.6 %collective-permute-done.1.refs_6_.refs_9_.refs_10_ = bf16[54,128,128]{2,1,0:T(8,128)(2,1)S(1)} collective-permute-done((bf16[54,128,128]{2,1,0:T(8,128)(2,1)}, bf16[54,128,128]{2,1,0:T(8,128)(2,1)S(1)}, u32[]{:S(2)}, u32[]{:S(2)}) %collective-permute-start.1) | collective-permute-done | bytes 1769504 | tf_op jit(solution)/shard_map/ppermute | solution.py:358
  48.5 39.7 %collective-permute-done.4.refs_6_.refs_11_.refs_12_ = bf16[54,128,128]{2,1,0:T(8,128)(2,1)} collective-permute-done((bf16[54,128,128]{2,1,0:T(8,128)(2,1)}, bf16[54,128,128]{2,1,0:T(8,128)(2,1)}, u32[]{:S(2)}, u32[]{:S(2)}) %collective-permute-start.4) | collective-permute-done | bytes 1769504 | tf_op jit(solution)/shard_map/ppermute | solution.py:358
  88.2 0.8 constant_dynamic-update-slice_fusion.11
  89.0 0.8 constant_dynamic-update-slice_fusion.10
  89.7 0.8 constant_dynamic-update-slice_fusion.9
  90.5 0.8 constant_dynamic-update-slice_fusion.8
  91.3 2.5 %collective-permute-start.6 = (bf16[8,128,128]{2,1,0:T(8,128)(2,1)S(1)}, bf16[8,128,128]{2,1,0:T(8,128)(2,1)S(1)}, u32[]{:S(2)}, u32[]{:S(2)}) collective-permute-start(bf16[8,128,128]{2,1,0:T(8,128)(2,1)S(1)} %get-tuple-element.41), channel_id=1, source_target_pairs={{4,0},{8,4},{12,8},{16,12},{20,16},{24,20},{28,24},{5,1},{9,5},{13... | collective-permute-start | bytes 786440 | tf_op jit(solution)/shard_map/ppermute | solution.py:355
  93.8 3.1 %collective-permute-start.5 = (bf16[8,128,128]{2,1,0:T(8,128)(2,1)S(1)}, bf16[8,128,128]{2,1,0:T(8,128)(2,1)S(1)}, u32[]{:S(2)}, u32[]{:S(2)}) collective-permute-start(bf16[8,128,128]{2,1,0:T(8,128)(2,1)S(1)} %get-tuple-element.42), channel_id=1, source_target_pairs={{0,4},{4,8},{8,12},{12,16},{16,20},{20,24},{24,28},{1,5},{5,9},{9,... | collective-permute-start | bytes 786440 | tf_op jit(solution)/shard_map/ppermute | solution.py:355
  96.9 0.0 copy-done.4
  96.9 0.7 collective-permute-start.9
  97.6 1.8 collective-permute-done.6.refs_5_
  99.4 0.8 collective-permute-done.5.refs_4_
  100.2 8.6 %shard_map.40 = (bf16[54,128,128]{2,1,0:T(8,128)(2,1)S(1)}, f32[512,512]{1,0:T(8,128)S(1)}) custom-call(s32[2]{0:T(128)S(1)} %pad_add_fusion.order.refs_0_, f32[3]{0:T(128)S(1)} %copy-done.2, f32[12,1,512]{2,1,0:T(1,128)S(1)} %copy-done.1, f32[6,1,128]{2,1,0:T(1,128)S(1)} %reshape.3.refs_3_, bf16[8,128,128]{2,1,0:T(8,128)(2,1)S(1)} %collective-permute-done.5.refs_4_, ...), custom_call_target="tpu_custom_call" | custom-call | flops 1626341376 | bytes 4718592 | tf_op jit(solution)/shard_map/pallas_call | solution.py:200
  108.8 10.5 %shard_map.41 = (bf16[54,128,128]{2,1,0:T(8,128)(2,1)S(1)}, f32[512,512]{1,0:T(8,128)S(1)}) custom-call(s32[2]{0:T(128)S(1)} %pad_add_fusion.order.refs_0_, f32[3]{0:T(128)S(1)} %copy-done.2, f32[12,1,512]{2,1,0:T(1,128)S(1)} %copy-done.1, f32[6,1,128]{2,1,0:T(1,128)S(1)} %reshape.3.refs_3_, bf16[8,128,128]{2,1,0:T(8,128)(2,1)S(1)} %collective-permute-done.5.refs_4_, ...), custom_call_target="tpu_custom_call" | custom-call | flops 1626341376 | bytes 4718592 | tf_op jit(solution)/shard_map/pallas_call | solution.py:200
  119.3 27.9 %collective-permute-done.refs_6_ = bf16[68,64,128]{2,1,0:T(8,128)(2,1)} collective-permute-done((bf16[68,64,128]{2,1,0:T(8,128)(2,1)}, bf16[68,64,128]{2,1,0:T(8,128)(2,1)}, u32[]{:S(2)}, u32[]{:S(2)}) %collective-permute-start) | collective-permute-done | bytes 1114144 | tf_op jit(solution)/shard_map/ppermute | solution.py:358
  147.2 1.0 fusion.1
  148.2 5.3 %collective-permute-start.7 = (bf16[8,64,128]{2,1,0:T(8,128)(2,1)S(1)}, bf16[8,64,128]{2,1,0:T(8,128)(2,1)S(1)}, u32[]{:S(2)}, u32[]{:S(2)}) collective-permute-start(bf16[8,64,128]{2,1,0:T(8,128)(2,1)S(1)} %pad_maximum_fusion.2), channel_id=1, source_target_pairs={{0,4},{4,8},{8,12},{12,16},{16,20},{20,24},{24,28},{1,5},{5,9},{9,... | collective-permute-start | bytes 393224 | tf_op jit(solution)/shard_map/ppermute | solution.py:355
  153.6 1.9 collective-permute-start.8
  155.5 0.0 collective-permute-done.7.refs_4_
  155.5 4.6 %collective-permute-done.8.refs_5_ = bf16[8,64,128]{2,1,0:T(8,128)(2,1)S(1)} collective-permute-done((bf16[8,64,128]{2,1,0:T(8,128)(2,1)S(1)}, bf16[8,64,128]{2,1,0:T(8,128)(2,1)S(1)}, u32[]{:S(2)}, u32[]{:S(2)}) %collective-permute-start.8) | collective-permute-done | bytes 131104 | tf_op jit(solution)/shard_map/ppermute | solution.py:355
  160.2 9.1 %shard_map.42 = (bf16[54,128,128]{2,1,0:T(8,128)(2,1)S(1)}, bf16[54,128,128]{2,1,0:T(8,128)(2,1)S(1)}, f32[512,512]{1,0:T(8,128)S(1)}) custom-call(s32[2]{0:T(128)S(1)} %pad_add_fusion.order.refs_0_, f32[3]{0:T(128)S(1)} %copy-done.2, f32[12,1,512]{2,1,0:T(1,128)S(1)} %copy-done.1, f32[6,1,128]{2,1,0:T(1,128)S(1)} %reshape.3.refs_3_, ...), custom_call_target="tpu_custom_call" | custom-call | flops 813170688 | bytes 2359296 | tf_op jit(solution)/shard_map/pallas_call | solution.py:200
  169.3 0.0 collective-permute-done.9.refs_7_
  169.3 9.8 %shard_map.43 = bf16[32,64,128]{2,1,0:T(8,128)(2,1)S(1)} custom-call(s32[2]{0:T(128)S(1)} %pad_add_fusion.order.refs_0_, f32[3]{0:T(128)S(1)} %copy-done.2, f32[12,1,512]{2,1,0:T(1,128)S(1)} %copy-done.1, f32[6,1,128]{2,1,0:T(1,128)S(1)} %reshape.3.refs_3_, bf16[8,64,128]{2,1,0:T(8,128)(2,1)S(1)} %collective-permute-done.7.refs_4_, ...), custom_call_target="tpu_custom_call" | custom-call | flops 813170688 | bytes 2359296 | tf_op jit(solution)/shard_map/pallas_call | solution.py:200
  179.1 19.8 %all_to_all.5 = bf16[32,64,128]{2,1,0:T(8,128)(2,1)S(1)} all-to-all(bf16[32,64,128]{2,1,0:T(8,128)(2,1)S(1)} %shard_map.43), channel_id=1, replica_groups=mesh['space'=8,'mode'=4] {'space','mode'}, dimensions={0} | all-to-all | bytes 1048576 | tf_op jit(solution)/shard_map/all_to_all | solution.py:405
  198.9 0.1 convert_reduce_fusion
  199.0 0.6 broadcast_multiply_fusion
  (8 shorter events, 0.1 us)
Async XLA Ops:
  0.1 2.8 %copy-start = (bf16[128,12,2048]{2,0,1:T(8,128)(2,1)S(1)}, bf16[128,12,2048]{2,0,1:T(8,128)(2,1)}, u32[]{:S(2)}) copy-start(bf16[128,12,2048]{2,0,1:T(8,128)(2,1)} %param.3) | copy-start | bytes 18874372
  5.6 42.8 %collective-permute-start.1 = (bf16[54,128,128]{2,1,0:T(8,128)(2,1)}, bf16[54,128,128]{2,1,0:T(8,128)(2,1)S(1)}, u32[]{:S(2)}, u32[]{:S(2)}) collective-permute-start(bf16[54,128,128]{2,1,0:T(8,128)(2,1)} %get-tuple-element.26), channel_id=1, source_target_pairs={{0,3},{1,2},{2,1},{3,0},{4,7},{5,6},{6,5},{7,4},{8,11},{9,10},{10,... | collective-permute-start | bytes 5308424 | tf_op jit(solution)/shard_map/ppermute | solution.py:358
  9.8 17.3 %copy-start.2 = (f32[3]{0:T(128)S(1)}, f32[3]{0:T(128)}, u32[]{:S(2)}) copy-start(f32[3]{0:T(128)} %refs_1_.9) | copy-start | bytes 40
  9.8 78.4 %collective-permute-start.4 = (bf16[54,128,128]{2,1,0:T(8,128)(2,1)}, bf16[54,128,128]{2,1,0:T(8,128)(2,1)}, u32[]{:S(2)}, u32[]{:S(2)}) collective-permute-start(bf16[54,128,128]{2,1,0:T(8,128)(2,1)} %get-tuple-element.23), channel_id=1, source_target_pairs={{0,1},{1,0},{2,3},{3,2},{4,5},{5,4},{6,7},{7,6},{8,9},{9,8},{10,11... | collective-permute-start | bytes 5308424 | tf_op jit(solution)/shard_map/ppermute | solution.py:358
  12.6 0.9 copy-start.3
  14.2 12.9 %collective-permute-start.2 = (bf16[4,128,128]{2,1,0:T(8,128)(2,1)}, bf16[4,128,128]{2,1,0:T(8,128)(2,1)}, u32[]{:S(2)}, u32[]{:S(2)}) collective-permute-start(bf16[4,128,128]{2,1,0:T(8,128)(2,1)} %pad_maximum_fusion), channel_id=1, source_target_pairs={{0,4},{4,8},{8,12},{12,16},{16,20},{20,24},{24,28},{1,5},{5,9},{9,... | collective-permute-start | bytes 393224 | tf_op jit(solution)/shard_map/ppermute | solution.py:355
  18.9 8.2 %collective-permute-start.3 = (bf16[4,128,128]{2,1,0:T(8,128)(2,1)}, bf16[4,128,128]{2,1,0:T(8,128)(2,1)}, u32[]{:S(2)}, u32[]{:S(2)}) collective-permute-start(bf16[4,128,128]{2,1,0:T(8,128)(2,1)} %pad_maximum_fusion.1), channel_id=1, source_target_pairs={{4,0},{8,4},{12,8},{16,12},{20,16},{24,20},{28,24},{5,1},{9,5},{13... | collective-permute-start | bytes 393224 | tf_op jit(solution)/shard_map/ppermute | solution.py:355
  20.8 126.4 %collective-permute-start = (bf16[68,64,128]{2,1,0:T(8,128)(2,1)}, bf16[68,64,128]{2,1,0:T(8,128)(2,1)}, u32[]{:S(2)}, u32[]{:S(2)}) collective-permute-start(bf16[68,64,128]{2,1,0:T(8,128)(2,1)} %get-tuple-element.25), channel_id=1, source_target_pairs={{0,2},{1,3},{2,0},{3,1},{4,6},{5,7},{6,4},{7,5},{8,10},{9,11},{10,... | collective-permute-start | bytes 3342344 | tf_op jit(solution)/shard_map/ppermute | solution.py:358
  22.3 0.7 copy-start.5
  27.1 0.7 copy-start.1
  27.8 69.1 %copy-start.4 = (bf16[40,64,128]{2,1,0:T(8,128)(2,1)S(1)}, bf16[40,64,128]{2,1,0:T(8,128)(2,1)}, u32[]{:S(2)}) copy-start(bf16[40,64,128]{2,1,0:T(8,128)(2,1)} %copy-done.3) | copy-start | bytes 1966084
  91.3 8.1 %collective-permute-start.6 = (bf16[8,128,128]{2,1,0:T(8,128)(2,1)S(1)}, bf16[8,128,128]{2,1,0:T(8,128)(2,1)S(1)}, u32[]{:S(2)}, u32[]{:S(2)}) collective-permute-start(bf16[8,128,128]{2,1,0:T(8,128)(2,1)S(1)} %get-tuple-element.41), channel_id=1, source_target_pairs={{4,0},{8,4},{12,8},{16,12},{20,16},{24,20},{28,24},{5,1},{9,5},{13... | collective-permute-start | bytes 786440 | tf_op jit(solution)/shard_map/ppermute | solution.py:355
  93.8 6.4 %collective-permute-start.5 = (bf16[8,128,128]{2,1,0:T(8,128)(2,1)S(1)}, bf16[8,128,128]{2,1,0:T(8,128)(2,1)S(1)}, u32[]{:S(2)}, u32[]{:S(2)}) collective-permute-start(bf16[8,128,128]{2,1,0:T(8,128)(2,1)S(1)} %get-tuple-element.42), channel_id=1, source_target_pairs={{0,4},{4,8},{8,12},{12,16},{16,20},{20,24},{24,28},{1,5},{5,9},{9,... | collective-permute-start | bytes 786440 | tf_op jit(solution)/shard_map/ppermute | solution.py:355
  96.9 72.4 %collective-permute-start.9 = (bf16[40,64,128]{2,1,0:T(8,128)(2,1)S(1)}, bf16[40,64,128]{2,1,0:T(8,128)(2,1)S(1)}, u32[]{:S(2)}, u32[]{:S(2)}) collective-permute-start(bf16[40,64,128]{2,1,0:T(8,128)(2,1)S(1)} %copy-done.4), channel_id=1, source_target_pairs={{0,2},{1,3},{2,0},{3,1},{4,6},{5,7},{6,4},{7,5},{8,10},{9,11},{10,... | collective-permute-start | bytes 1966088 | tf_op jit(solution)/shard_map/ppermute | solution.py:358
  148.2 7.3 %collective-permute-start.7 = (bf16[8,64,128]{2,1,0:T(8,128)(2,1)S(1)}, bf16[8,64,128]{2,1,0:T(8,128)(2,1)S(1)}, u32[]{:S(2)}, u32[]{:S(2)}) collective-permute-start(bf16[8,64,128]{2,1,0:T(8,128)(2,1)S(1)} %pad_maximum_fusion.2), channel_id=1, source_target_pairs={{0,4},{4,8},{8,12},{12,16},{16,20},{20,24},{24,28},{1,5},{5,9},{9,... | collective-permute-start | bytes 393224 | tf_op jit(solution)/shard_map/ppermute | solution.py:355
  153.6 6.6 %collective-permute-start.8 = (bf16[8,64,128]{2,1,0:T(8,128)(2,1)S(1)}, bf16[8,64,128]{2,1,0:T(8,128)(2,1)S(1)}, u32[]{:S(2)}, u32[]{:S(2)}) collective-permute-start(bf16[8,64,128]{2,1,0:T(8,128)(2,1)S(1)} %pad_maximum_fusion.3), channel_id=1, source_target_pairs={{4,0},{8,4},{12,8},{16,12},{20,16},{24,20},{28,24},{5,1},{9,5},{13... | collective-permute-start | bytes 393224 | tf_op jit(solution)/shard_map/ppermute | solution.py:355

commit v3 on v2

v3 whole, which is shorter than its diff:
```python
import functools
import math

import jax
import jax.numpy as jnp
from jax import lax
from jax.experimental import pallas as pl
from jax.experimental.pallas import tpu as pltpu
from jax.sharding import PartitionSpec as P

NZ = 64
LANES = 128
SUB = 16
PACK_VMEM = 16
BF = jnp.bfloat16
F32 = jnp.float32
VMEM = pltpu.VMEM


def product(left, right):
    return lax.dot_general(left, right, (((1,), (1,)), ((), ())), preferred_element_type=F32)


def apply_rows(i, eps, velocity, w, xs, a, tiles, rows, off, count):
    span = rows + 2
    xp, xm = eps - 0.5 * velocity[0], eps + 0.5 * velocity[0]
    yp, ym = eps - 0.5 * velocity[1], eps + 0.5 * velocity[1]
    zp, zm = eps - 0.5 * velocity[2], eps + 0.5 * velocity[2]
    lane = lax.broadcasted_iota(jnp.int32, (SUB, LANES), 1)
    low = lane < NZ
    zps = jnp.where(lane % NZ == NZ - 1, 0.0, zp)
    zms = jnp.where(lane % NZ == 0, 0.0, zm)
    own = jnp.where(low, yp, ym)
    other = jnp.where(low, ym, yp)

    def body(j, carry):
        source = pl.ds(pl.multiple_of(j * SUB, SUB), SUB)
        target = pl.ds(pl.multiple_of(j * SUB + off, SUB), SUB)
        center = [
            [xs[t * span + 2 * i + r, source, :].astype(F32) for t in range(tiles)] for r in range(4)
        ]
        for r in (0, 1):
            mid = center[r + 1]
            turned = [pltpu.roll(c, NZ, 1) for c in mid]
            for t in range(tiles):
                c = mid[t]
                behind = turned[t + 1] if t + 1 < tiles else jnp.zeros_like(c)
                before = turned[t - 1] if t > 0 else jnp.zeros_like(c)
                value = xp * center[r + 2][t] + xm * center[r][t]
                value = value + own * turned[t] + other * jnp.where(low, before, behind)
                value = value + zps * pltpu.roll(c, LANES - 1, 1) + zms * pltpu.roll(c, 1, 1)
                value = (value - (6.0 * eps) * c) * w[2 * i + r, :, t * LANES : (t + 1) * LANES]
                a[t * rows + 2 * i + r, target, :] = value.astype(BF)
        return carry

    lax.fori_loop(0, count // SUB, body, 0)


def phase_kernel(cfg, *refs):
    refs = list(refs)
    d, off, count, whole = cfg["d"], cfg["off"], cfg["count"], cfg["whole"]
    rows, tiles = cfg["rows"], cfg["tiles"]
    steps, end, mine, span = rows // 2, off + count, slice(off, off + count), rows + 2
    last, part = cfg["last"], count < whole
    take = lambda k: [refs.pop(0) for _ in range(k)]
    order, velocity, w = take(3)
    parts = take(cfg["n_parts"])
    old = [take(2) for _ in range(cfg["n_old"])]
    prev = take(2) if cfg["prev"] else None
    gin = take(1)[0] if cfg["gin"] else None
    xo = take(1)[0] if part and not last else None
    a = None if last else take(1)[0]
    (gout,) = take(1)
    if last:
        (a,) = take(1)
    xs, t2 = take(2)
    t1 = take(1)[0] if cfg["t1"] else None
    g = gout
    loads = []
    if old or prev is not None:
        held, sem = take(2)
        sources = [v for pair in old for v in pair] + list(prev or [])
        for k, v in enumerate(sources):
            loads.append(pltpu.make_async_copy(v, held.at[k], sem.at[k]))
            loads[-1].start()
        old = [(held.at[2 * k], held.at[2 * k + 1]) for k in range(len(old))]
        if prev is not None:
            prev = (held.at[2 * len(old)], held.at[2 * len(old) + 1])

    if part:
        rim, inner = parts[0], parts[-1]
        deep = rows - 2
        begin = inner.shape[0] - (tiles - 2) * deep
        base = (off // count) * (2 * tiles + 2 * deep)
        sides = (base + 2 * tiles, base + 2 * tiles + deep)
    for t in range(tiles):
        xs[t * span] = jnp.zeros_like(xs[0])
        xs[t * span + rows + 1] = jnp.zeros_like(xs[0])
        if part:
            xs[t * span + 1] = rim[base + t]
            xs[t * span + rows] = rim[base + tiles + t]
            if t in (0, tiles - 1):
                first = sides[t // (tiles - 1)]
                xs[t * span + 2 : t * span + rows] = rim[first : first + deep]
            else:
                xs[t * span + 2 : t * span + rows] = inner[begin + (t - 1) * deep : begin + t * deep]
        else:
            xs[t * span + 1 : t * span + rows + 1] = parts[0][t * rows : (t + 1) * rows]
    t2[...] = jnp.zeros_like(t2)
    if t1 is not None:
        t1[...] = jnp.zeros_like(t1)
    def padded(value, before=None):
        pieces = [value]
        if off:
            pieces.insert(0, jnp.zeros((off, LANES), BF) if before is None else before)
        if end < whole:
            pieces.append(jnp.zeros((whole - end, LANES), BF))
        return pieces[0] if len(pieces) == 1 else jnp.concatenate(pieces, axis=0)

    def stencil(i, carry):
        apply_rows(i, cfg["eps"], velocity, w, xs, a, tiles, rows, off, count)
        return carry

    lax.fori_loop(0, steps, stencil, 0)
    for c in loads:
        c.wait()

    def body(i, carry):
        picks = [t * rows + 2 * i + r for r in (0, 1) for t in range(tiles)]
        wide = lambda ref: jnp.concatenate([ref[k] for k in picks], axis=1)
        new = [xs[t * span + 2 * i + r + 1] for r in (0, 1) for t in range(tiles)]
        if part:
            before = [None if prev is None else prev[0][k, :off, :] for k in picks]
            both = [padded(v, u) for v, u in zip(new, before)]
            if xo is not None:
                for k, v in zip(picks, both):
                    xo[k] = v
        else:
            both = new
        fresh = [padded(v) for v in new]
        mark = [padded(a[k, mine, :]) for k in picks]
        if part and not last:
            rest = slice(0, off) if off else slice(end, whole)
            for k in picks:
                a[k, rest, :] = jnp.zeros((whole - count, LANES), BF) if prev is None else prev[1][k, rest, :]
        tall = [wide(ox) for ox, _ in old] + [jnp.concatenate(both, axis=1)]
        t2[...] += product(jnp.concatenate(tall, axis=0), jnp.concatenate(mark, axis=1))
        tall = [wide(oa) for _, oa in old] + ([wide(prev[1])] if prev is not None else [])
        if tall:
            t1[...] += product(jnp.concatenate(tall, axis=0), jnp.concatenate(fresh, axis=1))
        return carry

    lax.fori_loop(0, steps, body, 0)

    g[...] = jnp.zeros_like(g) if gin is None else gin[...]
    block = lambda k: slice(k * whole, (k + 1) * whole)
    names = [*cfg["old"], d]
    for k, o in enumerate(names):
        g[block(o), block(d)] += t2[block(k), :]
    for k, o in enumerate(names if prev is not None else names[:-1]):
        g[block(d), block(o)] += t1[block(k), :].T


def phase(cfg, order, velocity, w, parts, old, prev, gin):
    rows, tiles, whole, count = cfg["rows"], cfg["tiles"], cfg["whole"], cfg["count"]
    size, last, part = cfg["n_blocks"] * whole, cfg["last"], count < whole
    kept = jax.ShapeDtypeStruct((tiles * rows, whole, LANES), BF)
    args = [order, velocity, w, *parts]
    first = len(args)
    for group in [*old, *([prev] if prev is not None else [])]:
        args += list(group)
    loaded = len(args) - first
    if gin is not None:
        args.append(gin)
    scratch = []
    if last:
        out_shape = []
        scratch.append(VMEM(kept.shape, BF))
    else:
        out_shape = [kept] * (2 if part else 1)
    out_shape.append(jax.ShapeDtypeStruct((size, size), F32))
    seconds = len(old) + (prev is not None)
    scratch.append(VMEM((tiles * (rows + 2), count, LANES), BF))
    scratch.append(VMEM(((len(old) + 1) * whole, whole), F32))
    if seconds:
        scratch.append(VMEM((seconds * whole, whole), F32))
    if loaded:
        scratch += [VMEM((loaded, *kept.shape), BF), pltpu.SemaphoreType.DMA((loaded,))]
    elements = rows * count * tiles * LANES
    cfg = dict(cfg, n_parts=len(parts), n_old=len(old), prev=prev is not None, gin=gin is not None, t1=bool(seconds))
    vmem = pl.BlockSpec(memory_space=VMEM)
    smem = pl.BlockSpec(memory_space=pltpu.SMEM)
    outs = pl.pallas_call(
        functools.partial(phase_kernel, cfg),
        in_specs=[smem, smem]
        + [pl.BlockSpec(memory_space=pl.ANY) if first <= k < first + loaded else vmem for k in range(2, len(args))],
        out_specs=[vmem] * len(out_shape),
        out_shape=out_shape,
        scratch_shapes=scratch,
        compiler_params=pltpu.CompilerParams(vmem_limit_bytes=cfg["vmem"] << 20),
        cost_estimate=pl.CostEstimate(flops=1, bytes_accessed=1, transcendentals=0),
    )(*args)
    if last:
        return None, outs[0]
    return (outs[0] if part else parts[0], outs[-2]), outs[-1]


def line_kernel(rows, tiles, flip, *refs):
    ins, (near, far, near_row, far_row) = refs[:-4], refs[-4:]
    deep = rows - 2

    def tile_row(ref, row, t, c):
        if c is None:
            return ref[t * rows + row].astype(F32)
        base = c * (2 * tiles + 2 * deep)
        if row in (0, rows - 1):
            return ref[base + (tiles if row else 0) + t].astype(F32)
        return ref[base + 2 * tiles + (deep if t else 0) + row - 1].astype(F32)

    parts = []
    for ref in ins:
        parts += [(ref, None)] if ref.shape[0] == tiles * rows else [(ref, 0), (ref, 1)]
    keep = flip[0] == 0
    start = 0
    for ref, c in parts:
        size = ref.shape[1]
        low = lax.broadcasted_iota(jnp.int32, (size, LANES), 1) < NZ
        modes = slice(start, start + size)
        start += size
        for t in range(tiles):
            near_row[t, modes, :] = tile_row(ref, 0, t, c).astype(BF)
            far_row[t, modes, :] = tile_row(ref, rows - 1, t, c).astype(BF)
        for i in range(rows // 2):
            one, two = tile_row(ref, 2 * i, 0, c), tile_row(ref, 2 * i + 1, 0, c)
            first = jnp.where(low, one, pltpu.roll(two, NZ, 1))
            one, two = tile_row(ref, 2 * i, tiles - 1, c), tile_row(ref, 2 * i + 1, tiles - 1, c)
            final = jnp.where(low, pltpu.roll(one, NZ, 1), two)
            near[i, modes, :] = jnp.where(keep, first, final).astype(BF)
            far[i, modes, :] = jnp.where(keep, final, first).astype(BF)


def lines_of(arrays, rows, tiles, flip):
    modes = sum(v.shape[1] * (1 if v.shape[0] == tiles * rows else 2) for v in arrays)
    vmem = pl.BlockSpec(memory_space=VMEM)
    shape = jax.ShapeDtypeStruct((rows // 2, modes, LANES), BF)
    return pl.pallas_call(
        functools.partial(line_kernel, rows, tiles),
        in_specs=[pl.BlockSpec(memory_space=pltpu.SMEM)] + [vmem] * len(arrays),
        out_specs=[vmem] * 4,
        out_shape=[shape] * 2 + [jax.ShapeDtypeStruct((tiles, modes, LANES), BF)] * 2,
        compiler_params=pltpu.CompilerParams(vmem_limit_bytes=12 << 20),
        cost_estimate=pl.CostEstimate(flops=1, bytes_accessed=1, transcendentals=0),
    )(flip.reshape(1), *arrays)


def border_kernel(eps, groups, space, n, order, velocity, wn, wh, wr, wx, gin, *refs):
    count = len(groups)
    here, there = refs[:count], refs[count : 2 * count]
    own, over = refs[2 * count : 3 * count], refs[3 * count : 4 * count]
    g, out = refs[-1], refs[4 * count]
    xp, xm = eps - 0.5 * velocity[0], eps + 0.5 * velocity[0]
    yp, ym = eps - 0.5 * velocity[1], eps + 0.5 * velocity[1]
    toward = jnp.where(order[1] == 0, yp, ym)
    back = jnp.where(order[1] == 0, ym, yp)
    blocks = sum(len(names) for names in groups)
    size = g.shape[0] // blocks

    def find(refs, d, i):
        for names, ref in zip(groups, refs):
            if d in names:
                k = names.index(d)
                return ref[i, k * size : (k + 1) * size, :]

    def every(refs, i):
        return jnp.concatenate([find(refs, d, i) for d in range(blocks)], axis=0)

    left, right = [], []
    for k in range(wn.shape[0]):
        mine = every(here, k)
        if blocks == 4:
            near = order[2] == 1
            other = [
                jnp.where(near, find(there, d ^ 1, k).astype(F32), find(there, d ^ 3, k).astype(F32))
                for d in range(blocks)
            ]
            other = jnp.concatenate(other, axis=0)
        else:
            other = every(there, k).astype(F32)
        left += [mine, other.astype(BF)]
        right += [(wn[k] * (toward * other)).astype(BF), (wh[k] * (back * mine.astype(F32))).astype(BF)]
    for t in range(wr.shape[0]):
        mine, other = every(own, t), every(over, t)
        left += [mine, other]
        right += [
            (wr[t] * (xp * other.astype(F32))).astype(BF),
            (wx[t] * (xm * mine.astype(F32))).astype(BF),
        ]
    total = gin[...]
    for k in range(0, len(left), 4):
        total = total + product(
            jnp.concatenate(left[k : k + 4], axis=1), jnp.concatenate(right[k : k + 4], axis=1)
        )
    g[...] = total
    if blocks == n:
        q = order[0]
        share = out.shape[1]
        per = size // share
        for s in range(space):
            first = pl.multiple_of(((s // per) ^ q) * size + (s % per) * share, share)
            for z in range(n):
                start = pl.multiple_of((z ^ q) * size, size)
                out[s * n + z] = g[pl.ds(first, share), pl.ds(start, size)].astype(out.dtype)
    else:
        out[...] = total


def border(eps, groups, order, velocity, weights, gin, here, there, own, over, space, n):
    vmem = pl.BlockSpec(memory_space=VMEM)
    smem = pl.BlockSpec(memory_space=pltpu.SMEM)
    blocks = sum(len(names) for names in groups)
    shape = jax.ShapeDtypeStruct(gin.shape, F32)
    if blocks == n:
        size = gin.shape[0]
        shape = jax.ShapeDtypeStruct((space * n, size // space, size // n), BF)
    args = [order, velocity, *weights, gin, *here, *there, *own, *over]
    return pl.pallas_call(
        functools.partial(border_kernel, eps, groups, space, n),
        in_specs=[smem, smem] + [vmem] * (len(args) - 2),
        out_specs=vmem,
        out_shape=shape,
        scratch_shapes=[VMEM(gin.shape, F32)],
        compiler_params=pltpu.CompilerParams(vmem_limit_bytes=16 << 20),
        cost_estimate=pl.CostEstimate(flops=1, bytes_accessed=1, transcendentals=0),
    )(*args)


def pack_kernel(jobs, rows, tiles, order, field, *refs):
    outs, sem = refs[:-1], refs[-1]
    q = order[0]
    deep = rows - 2
    copies = []
    for k, (d, kind, a, b) in enumerate(jobs):
        base = (q ^ d) * tiles * LANES
        cut = lambda t: pl.ds(pl.multiple_of(base + t * LANES, LANES), LANES)
        for t in range(tiles):
            if kind == "full":
                copies.append((field.at[:, :, cut(t)], outs[k].at[t * rows : (t + 1) * rows]))
                continue
            inside = slice(1, rows - 1)
            if t not in (0, tiles - 1):
                begin = 2 * (2 * tiles + 2 * deep) if kind == "rim" else 0
                to = slice(begin + (t - 1) * deep, begin + t * deep)
                copies.append((field.at[inside, a:b, cut(t)], outs[k].at[to]))
            if kind == "rim":
                for c in (0, 1):
                    first = c * (2 * tiles + 2 * deep)
                    half = slice(c * (b - a), (c + 1) * (b - a))
                    copies.append((field.at[0, half, cut(t)], outs[k].at[first + t]))
                    copies.append((field.at[rows - 1, half, cut(t)], outs[k].at[first + tiles + t]))
                    if t in (0, tiles - 1):
                        to = first + 2 * tiles + (deep if t else 0)
                        copies.append((field.at[inside, half, cut(t)], outs[k].at[to : to + deep]))
    copies = [pltpu.make_async_copy(src, dst, sem.at[m]) for m, (src, dst) in enumerate(copies)]
    for c in copies:
        c.start()
    for c in copies:
        c.wait()


def pack(jobs, tiles, order, field):
    rows, count, _ = field.shape
    deep = rows - 2
    shapes, pieces = [], 0
    for d, kind, a, b in jobs:
        if kind == "full":
            shapes.append((tiles * rows, count, LANES))
            pieces += tiles
        else:
            length = (tiles - 2) * deep
            pieces += tiles - 2
            if kind == "rim":
                length += 2 * (2 * tiles + 2 * deep)
                pieces += 4 * tiles + 4
            shapes.append((length, b - a, LANES))
    anywhere = pl.BlockSpec(memory_space=pl.ANY)
    return pl.pallas_call(
        functools.partial(pack_kernel, jobs, rows, tiles),
        in_specs=[pl.BlockSpec(memory_space=pltpu.SMEM), anywhere],
        out_specs=[anywhere] * len(jobs),
        out_shape=[jax.ShapeDtypeStruct(s, BF) for s in shapes],
        scratch_shapes=[pltpu.SemaphoreType.DMA((pieces,))],
        compiler_params=pltpu.CompilerParams(vmem_limit_bytes=PACK_VMEM << 20),
    )(order, field)


def first_kernel(owners, rows, tiles, order, field, *refs):
    count = len(owners)
    outs, (stage, into, out_of) = refs[:count], refs[count:]
    loads, stores = [], []
    for k, d in enumerate(owners):
        wide = pl.ds(pl.multiple_of((order[0] ^ d) * tiles * LANES, LANES), tiles * LANES)
        loads.append(pltpu.make_async_copy(field.at[:, :, wide], stage.at[k], into.at[k]))
        loads[-1].start()
    for k in range(count):
        loads[k].wait()
        for t in range(tiles):
            lanes = slice(t * LANES, (t + 1) * LANES)
            to = outs[k].at[t * rows : (t + 1) * rows]
            stores.append(
                pltpu.make_async_copy(stage.at[k, :, :, lanes], to, out_of.at[k * tiles + t])
            )
            stores[-1].start()
    for c in stores:
        c.wait()


def first_pack(owners, tiles, order, field):
    rows, count, _ = field.shape
    shape = jax.ShapeDtypeStruct((tiles * rows, count, LANES), BF)
    anywhere = pl.BlockSpec(memory_space=pl.ANY)
    return pl.pallas_call(
        functools.partial(first_kernel, owners, rows, tiles),
        in_specs=[pl.BlockSpec(memory_space=pltpu.SMEM), anywhere],
        out_specs=[anywhere] * len(owners),
        out_shape=[shape] * len(owners),
        scratch_shapes=[
            VMEM((len(owners), rows, count, tiles * LANES), BF),
            pltpu.SemaphoreType.DMA((len(owners),)),
            pltpu.SemaphoreType.DMA((len(owners) * tiles,)),
        ],
        compiler_params=pltpu.CompilerParams(vmem_limit_bytes=60 << 20),
    )(order, field)


def spread_out(total, n, space, q, count):
    share = n * count // space
    out = []
    for s in range(space):
        start = ((s * share) // count ^ q) * count + (s * share) % count
        rows = lax.dynamic_slice_in_dim(total, start, share, axis=0)
        out += [lax.dynamic_slice_in_dim(rows, (z ^ q) * count, count, axis=1) for z in range(n)]
    return jnp.stack(out)


def after(value, token):
    return lax.optimization_barrier((value, token))[0]


def local(modes, phases, velocity):
    space, n = lax.axis_size("space"), lax.axis_size("mode")
    sp, q = lax.axis_index("space"), lax.axis_index("mode")
    count, rows, plane = modes.shape
    width = plane // n
    tiles = width // LANES
    eps = 1.0 / math.sqrt(space * rows * plane)
    field = jnp.transpose(modes, (1, 0, 2))
    flip = sp & 1

    weight = jnp.where(phases == 0, 0.1, jnp.where(phases == 1, 1.0, 0.5)).astype(F32)
    w = lax.dynamic_slice_in_dim(weight, q * width, width, axis=1)[:, None, :]

    near = jnp.where(flip == 0, jnp.minimum((q + 1) * width, plane - NZ), jnp.maximum(q * width - NZ, 0))
    mine = jnp.where(flip == 0, (q + 1) * width - NZ, q * width)
    wh, wn = [
        lax.dynamic_slice_in_dim(weight, v, NZ, axis=1).reshape(rows // 2, 1, LANES)
        for v in (near, mine)
    ]

    def slab(source, owner):
        return lax.dynamic_slice_in_dim(source, owner * width, width, axis=2)

    ahead = [(i + 1, i) for i in range(space - 1)]
    above = lambda v: lax.ppermute(v, "space", ahead)
    cut = lambda v: lax.dynamic_slice_in_dim(v, q * width, width, axis=1).reshape(tiles, 1, LANES)
    weights = (wn, wh, cut(weight[rows - 1 :]), cut(above(weight[:1])))

    def swap(part, d):
        return lax.ppermute(part, "mode", [(i, i ^ d) for i in range(n)])

    relay = [(s * n + i, s * n + i - 1 + 2 * (s & 1)) for s in range(space) for i in range(n)]
    relay = [(i, j) for i, j in relay if i // n == j // n and j >= 0]
    beside = lambda v: lax.ppermute(v, ("space", "mode"), relay)
    partner = jnp.clip(q + 1 - 2 * flip, 0, n - 1) ^ q
    order = jnp.stack([q, flip, partner])
    base = dict(rows=rows, tiles=tiles, eps=eps, n=n, space=space, last=False, off=0, d=0, vmem=24)
    if n != 4:
        xs = [slab(field, q)] + [swap(slab(field, q ^ d), d) for d in range(1, n)]
        x = jnp.concatenate(xs, axis=1)
        cfg = dict(base, whole=n * count, count=n * count, n_blocks=1, old=[], vmem=40)
        x = jnp.concatenate([x[:, :, t * LANES : (t + 1) * LANES] for t in range(tiles)], axis=0)
        _, total = phase(cfg, order, velocity, w, [x], [], None, None)
        send, here, send_row, own = lines_of([x], rows, tiles, flip)
        there = beside(send).reshape(rows // 2, n, count, LANES)
        there = there[:, jnp.arange(n) ^ partner].reshape(send.shape)
        total = border(eps, [[0]], order, velocity, weights, total, [here], [there], [own], [above(send_row)], space, n)
        tiles = spread_out(total, n, space, q, count)
    else:
        half = count // 2
        p1, p3 = first_pack((1, 3), tiles, order, field)
        x1, x3 = swap(p1, 1), swap(p3, 3)
        jobs = [(0, "full", 0, 0), (2, "rim", 0, half), (2, "inner", half, count)]
        x0, p2, p2b = pack(jobs, tiles, order, after(field, p3))
        front, back = swap(p2, 2), swap(p2b, 2)
        base = dict(base, whole=count, n_blocks=n)
        names, old, g, met = [], [], None, []

        def meet(*arrays):
            send, here, row, own = lines_of(arrays, rows, tiles, flip)
            met.append((here, beside(send), own, above(row)))

        x0 = after(x0, weights)
        for d, x in ((0, x0), (1, x1), (3, x3)):
            if names:
                x = after(x, g)
            if d == 3:
                meet(x0, x1, x)
            cfg = dict(base, count=count, d=d, old=list(names))
            kept, g = phase(cfg, order, velocity, w, [x], old, None, g)
            names, old = [*names, d], [*old, kept]
        front = after(front, (g, met[-1][3]))
        meet(front)
        part = dict(base, d=2, count=half, old=names)
        kept, g = phase(part, order, velocity, w, [front], old, None, g)
        back = after(back, (g, met[-1][3]))
        part = dict(part, off=half, last=True)
        _, g = phase(part, order, velocity, w, [front, back], old, kept, g)
        met = [list(v) for v in zip(*met)]
        g = border(eps, [[0, 1, 3], [2]], order, velocity, weights, g, *met, space, n)
        tiles = g
    arrived = lax.all_to_all(tiles, ("space", "mode"), split_axis=0, concat_axis=0, tiled=True)
    return jnp.sum(arrived.astype(F32), axis=0) * eps


def solution(mesh):
    placed = (P("mode", "space", None), P("space", None), P())
    return jax.shard_map(
        local, mesh=mesh, in_specs=placed, out_specs=P("space", "mode"), check_vma=False
    )
```

time: 201 us -> 187 us (0.930)
  waiting for transfers between devices: 87.3 us -> 53.3 us
  starting transfers between devices: 24.2 us -> 48.7 us
  local copies, waits for them, and re-layouts: 13.4 us -> 5.92 us
  Pallas kernels: 51.5 us -> 56.2 us
    ppermute x4, waiting for transfers between devices: 80.1 us -> 52.4 us  [swap(): return lax.ppermute(part, 'mode', [(i, i ^ d) for i in range(n)])]
    ppermute x6 -> x5, starting transfers between devices: 18.7 us -> 42.6 us  [the longest x2 30.2 us: local(): beside = lambda v: lax.ppermute(v, ('space', 'mode'), relay)]
    pallas_call x2 -> x5, Pallas kernels: 5.53 us -> 12 us  [the longest x1 3.95 us: first_pack(): pl.pallas_call(functools.partial(first_kernel, owners, rows, tiles), in_s...]
    ppermute x6 -> x5, waiting for transfers between devices: 7.23 us -> 0.91 us  [the longest x3 0.9 us: local(): above = lambda v: lax.ppermute(v, 'space', ahead)]
    unnamed x19 -> x10, local copies, waits for them, and re-layouts: 7.48 us -> 3.44 us
  transfers between devices with their start and end apart: 10 -> 9, of which waited for: 6 -> 4; matrix products, arithmetic and copies ran while one was open for 5% -> 1% of each run, Pallas kernels for 20% -> 27%
where the time goes in v3:
time: 187 us; the launch traced here: 186 us
  Pallas kernels  56.2 us (30%)
  waiting for transfers between devices  53.3 us (29%)
  starting transfers between devices  48.7 us (26%)
  blocking collectives  20.2 us (11%)
  local copies, waits for them, and re-layouts  5.92 us (3%)
    ppermute x4, waiting for transfers between devices, swap(): return lax.ppermute(part, 'mode', [(i, i ^ d) for i in range(n)])  52.4 us
    pallas_call x5, Pallas kernels, phase(): pl.pallas_call(functools.partial(phase_kernel, cfg), in_specs=[smem, smem...  44.2 us
    ppermute x2, starting transfers between devices, local(): beside = lambda v: lax.ppermute(v, ('space', 'mode'), relay)  30.2 us
    all_to_all x1, blocking collectives, local(): lax.all_to_all(tiles, ('space', 'mode'), split_axis=0, concat_axis=0, til...  20.2 us
    ppermute x3, starting transfers between devices, local(): above = lambda v: lax.ppermute(v, 'space', ahead)  12.4 us
    ppermute x4, starting transfers between devices, swap(): return lax.ppermute(part, 'mode', [(i, i ^ d) for i in range(n)])  6.11 us
    pallas_call x1, Pallas kernels, first_pack(): pl.pallas_call(functools.partial(first_kernel, owners, rows, tiles), in_s...  3.95 us
  transfers between devices with their start and end apart: 9, of which 4 were waited for; matrix products, arithmetic and copies ran while one was open for 1% of the time, Pallas kernels for 27%

profile of v3, /device:TPU:1, one launch (start us, length us, event | category | flops | bytes accessed | tf_op | source)
XLA Modules:
  0.0 186.0 jit_solution(3059157538291110845)
XLA Ops:
  0.0 0.6 pad_add_fusion.order.refs_0_
  0.6 0.0 copy-start.1
  0.6 4.0 %shard_map.37 = (bf16[48,128,128]{2,1,0:T(8,128)(2,1)}, bf16[48,128,128]{2,1,0:T(8,128)(2,1)}) custom-call(s32[3]{0:T(128)} %pad_add_fusion.order.refs_0_, bf16[12,128,2048]{2,1,0:T(8,128)(2,1)} %bitcast.8), custom_call_target="tpu_custom_call" | custom-call | tf_op jit(solution)/shard_map/pallas_call | solution.py:421
  4.6 2.2 %collective-permute-start.3 = (bf16[48,128,128]{2,1,0:T(8,128)(2,1)}, bf16[48,128,128]{2,1,0:T(8,128)(2,1)S(1)}, u32[]{:S(2)}, u32[]{:S(2)}) collective-permute-start(bf16[48,128,128]{2,1,0:T(8,128)(2,1)} %get-tuple-element.36), channel_id=1, source_target_pairs={{0,1},{1,0},{2,3},{3,2},{4,5},{5,4},{6,7},{7,6},{8,9},{9,8},{10,11... | collective-permute-start | bytes 4718600 | tf_op jit(solution)/shard_map/ppermute | solution.py:478
  6.8 2.2 %collective-permute-start.2 = (bf16[48,128,128]{2,1,0:T(8,128)(2,1)}, bf16[48,128,128]{2,1,0:T(8,128)(2,1)}, u32[]{:S(2)}, u32[]{:S(2)}) collective-permute-start(bf16[48,128,128]{2,1,0:T(8,128)(2,1)} %get-tuple-element.33), channel_id=1, source_target_pairs={{0,3},{1,2},{2,1},{3,0},{4,7},{5,6},{6,5},{7,4},{8,11},{9,10},{10,... | collective-permute-start | bytes 4718600 | tf_op jit(solution)/shard_map/ppermute | solution.py:478
  9.0 0.0 copy-done.1
  9.0 0.0 copy-start
  9.0 2.8 %copy-done = bf16[128,12,2048]{2,0,1:T(8,128)(2,1)S(1)} copy-done((bf16[128,12,2048]{2,0,1:T(8,128)(2,1)S(1)}, bf16[128,12,2048]{2,0,1:T(8,128)(2,1)}, u32[]{:S(2)}) %copy-start) | copy-done | bytes 6291480
  11.8 0.0 copy-start.4
  11.8 0.0 copy-start.2
  11.8 2.3 %shard_map.38 = (bf16[48,128,128]{2,1,0:T(8,128)(2,1)S(1)}, bf16[76,64,128]{2,1,0:T(8,128)(2,1)}, bf16[20,64,128]{2,1,0:T(8,128)(2,1)S(1)}) custom-call(s32[3]{0:T(128)S(1)} %copy-done.1, bf16[12,128,2048]{2,1,0:T(8,128)(2,1)S(1)} %bitcast.9), custom_call_target="tpu_custom_call" | custom-call | tf_op jit(solution)/shard_map/pallas_call | solution.py:386
  14.1 0.2 collective-permute-start.1
  14.2 0.0 copy-done.4
  14.3 0.0 copy-start.3
  14.3 0.6 copy-done.3
  14.9 3.1 %collective-permute-start = (f32[1,2048]{1,0:T(1,128)S(1)}, f32[1,2048]{1,0:T(1,128)}, u32[]{:S(2)}, u32[]{:S(2)}) collective-permute-start(f32[1,2048]{1,0:T(1,128)S(1)} %get-tuple-element.61), channel_id=1, source_target_pairs={{4,0},{8,4},{12,8},{16,12},{20,16},{24,20},{28,24},{5,1},{9,5},{13... | collective-permute-start | bytes 24584 | tf_op jit(solution)/shard_map/ppermute | solution.py:473
  18.1 0.9 constant_dynamic-slice_fusion.1
  19.0 0.8 constant_dynamic-slice_fusion
  19.7 0.1 reshape.15.wh
  19.8 0.1 reshape.14.wn
  19.9 0.9 collective-permute-done
  20.8 0.7 dynamic-slice_bitcast_fusion.wx
  21.5 0.0 copy-done.2
  21.5 7.3 %shard_map.39 = (bf16[48,128,128]{2,1,0:T(8,128)(2,1)S(1)}, f32[512,512]{1,0:T(8,128)S(1)}) custom-call(s32[3]{0:T(128)S(1)} %copy-done.1, f32[3]{0:T(128)S(1)} %copy-done.2, f32[12,1,512]{2,1,0:T(1,128)S(1)} %broadcast_in_dim.18.refs_2_, bf16[48,128,128]{2,1,0:T(8,128)(2,1)S(1)} %get-tuple-element.38.refs_3_.refs_4_.refs_0_.refs_5_), custom_call_target="tpu_custom_call" | custom-call | flops 1 | bytes 1 | tf_op jit(solution)/shard_map/pallas_call | solution.py:193
  28.8 12.3 %collective-permute-done.3.refs_3_.refs_6_.refs_1_.refs_7_ = bf16[48,128,128]{2,1,0:T(8,128)(2,1)S(1)} collective-permute-done((bf16[48,128,128]{2,1,0:T(8,128)(2,1)}, bf16[48,128,128]{2,1,0:T(8,128)(2,1)S(1)}, u32[]{:S(2)}, u32[]{:S(2)}) %collective-permute-start.3) | collective-permute-done | bytes 1572896 | tf_op jit(solution)/shard_map/ppermute | solution.py:478
  41.1 8.5 %shard_map.40 = (bf16[48,128,128]{2,1,0:T(8,128)(2,1)S(1)}, f32[512,512]{1,0:T(8,128)S(1)}) custom-call(s32[3]{0:T(128)S(1)} %copy-done.1, f32[3]{0:T(128)S(1)} %copy-done.2, f32[12,1,512]{2,1,0:T(1,128)S(1)} %broadcast_in_dim.18.refs_2_, bf16[48,128,128]{2,1,0:T(8,128)(2,1)S(1)} %collective-permute-done.3.refs_3_.refs_6_.refs_1_.refs_7_, ...), custom_call_target="tpu_custom_call" | custom-call | flops 1 | bytes 1 | tf_op jit(solution)/shard_map/pallas_call | solution.py:193
  49.6 27.2 %collective-permute-done.2.refs_3_.refs_2_.refs_8_.refs_9_ = bf16[48,128,128]{2,1,0:T(8,128)(2,1)} collective-permute-done((bf16[48,128,128]{2,1,0:T(8,128)(2,1)}, bf16[48,128,128]{2,1,0:T(8,128)(2,1)}, u32[]{:S(2)}, u32[]{:S(2)}) %collective-permute-start.2) | collective-permute-done | bytes 1572896 | tf_op jit(solution)/shard_map/ppermute | solution.py:478
  76.9 2.0 %shard_map.42 = (bf16[6,384,128]{2,1,0:T(8,128)(2,1)S(1)}, bf16[6,384,128]{2,1,0:T(8,128)(2,1)S(1)}, bf16[4,384,128]{2,1,0:T(8,128)(2,1)S(1)}, bf16[4,384,128]{2,1,0:T(8,128)(2,1)S(1)}) custom-call(s32[1]{0:T(128)} %bitcast.1.flip, bf16[48,128,128]{2,1,0:T(8,128)(2,1)S(1)} %get-tuple-element.38.refs_3_.refs_4_.refs_0_.refs_5_, ...), custom_call_target="tpu_custom_call" | custom-call | flops 1 | bytes 1 | tf_op jit(solution)/shard_map/pallas_call | solution.py:246
  78.9 4.7 %collective-permute-start.4 = (bf16[4,384,128]{2,1,0:T(8,128)(2,1)S(1)}, bf16[4,384,128]{2,1,0:T(8,128)(2,1)S(1)}, u32[]{:S(2)}, u32[]{:S(2)}) collective-permute-start(bf16[4,384,128]{2,1,0:T(8,128)(2,1)S(1)} %get-tuple-element.46), channel_id=1, source_target_pairs={{4,0},{8,4},{12,8},{16,12},{20,16},{24,20},{28,24},{5,1},{9,5},{13... | collective-permute-start | bytes 1179656 | tf_op jit(solution)/shard_map/ppermute | solution.py:473
  83.6 28.9 %collective-permute-start.7 = (bf16[6,384,128]{2,1,0:T(8,128)(2,1)S(1)}, bf16[6,384,128]{2,1,0:T(8,128)(2,1)S(1)}, u32[]{:S(2)}, u32[]{:S(2)}) collective-permute-start(bf16[6,384,128]{2,1,0:T(8,128)(2,1)S(1)} %get-tuple-element.57), channel_id=1, source_target_pairs={{1,0},{2,1},{3,2},{4,5},{5,6},{6,7},{9,8},{10,9},{11,10},{12,13},{... | collective-permute-start | bytes 1769480 | tf_op jit(solution)/shard_map/ppermute | solution.py:482
  112.5 1.5 collective-permute-start.5
  114.0 10.4 %shard_map.41 = (bf16[48,128,128]{2,1,0:T(8,128)(2,1)S(1)}, f32[512,512]{1,0:T(8,128)S(1)}) custom-call(s32[3]{0:T(128)S(1)} %copy-done.1, f32[3]{0:T(128)S(1)} %copy-done.2, f32[12,1,512]{2,1,0:T(1,128)S(1)} %broadcast_in_dim.18.refs_2_, bf16[48,128,128]{2,1,0:T(8,128)(2,1)} %collective-permute-done.2.refs_3_.refs_2_.refs_8_.refs_9_, ...), custom_call_target="tpu_custom_call" | custom-call | flops 1 | bytes 1 | tf_op jit(solution)/shard_map/pallas_call | solution.py:193
  124.5 12.9 %collective-permute-done.1.refs_3_.refs_0_ = bf16[76,64,128]{2,1,0:T(8,128)(2,1)} collective-permute-done((bf16[76,64,128]{2,1,0:T(8,128)(2,1)}, bf16[76,64,128]{2,1,0:T(8,128)(2,1)}, u32[]{:S(2)}, u32[]{:S(2)}) %collective-permute-start.1) | collective-permute-done | bytes 1245216 | tf_op jit(solution)/shard_map/ppermute | solution.py:478
  137.4 0.0 collective-permute-done.4.refs_6_
  137.4 1.5 shard_map.44
  138.9 1.3 collective-permute-start.8
  140.2 4.6 %collective-permute-start.6 = (bf16[4,128,128]{2,1,0:T(8,128)(2,1)S(1)}, bf16[4,128,128]{2,1,0:T(8,128)(2,1)S(1)}, u32[]{:S(2)}, u32[]{:S(2)}) collective-permute-start(bf16[4,128,128]{2,1,0:T(8,128)(2,1)S(1)} %get-tuple-element.51), channel_id=1, source_target_pairs={{4,0},{8,4},{12,8},{16,12},{20,16},{24,20},{28,24},{5,1},{9,5},{13... | collective-permute-start | bytes 393224 | tf_op jit(solution)/shard_map/ppermute | solution.py:473
  144.8 8.6 %shard_map.43 = (bf16[48,128,128]{2,1,0:T(8,128)(2,1)S(1)}, bf16[48,128,128]{2,1,0:T(8,128)(2,1)S(1)}, f32[512,512]{1,0:T(8,128)S(1)}) custom-call(s32[3]{0:T(128)S(1)} %copy-done.1, f32[3]{0:T(128)S(1)} %copy-done.2, f32[12,1,512]{2,1,0:T(1,128)S(1)} %broadcast_in_dim.18.refs_2_, bf16[76,64,128]{2,1,0:T(8,128)(2,1)} %collective-permute-done.1.refs_3_.refs_0_, ...), custom_call_target="tpu_custom_call" | custom-call | flops 1 | bytes 1 | tf_op jit(solution)/shard_map/pallas_call | solution.py:193
  153.4 0.0 collective-permute-done.5.refs_4_
  153.4 0.0 collective-permute-done.6.refs_7_
  153.5 9.3 %shard_map.45.gin = f32[512,512]{1,0:T(8,128)S(1)} custom-call(s32[3]{0:T(128)S(1)} %copy-done.1, f32[3]{0:T(128)S(1)} %copy-done.2, f32[12,1,512]{2,1,0:T(1,128)S(1)} %broadcast_in_dim.18.refs_2_, bf16[76,64,128]{2,1,0:T(8,128)(2,1)} %collective-permute-done.1.refs_3_.refs_0_, bf16[20,64,128]{2,1,0:T(8,128)(2,1)S(1)} %collective-permute-done.5.refs_4_, ...), custom_call_target="tpu_custom_call" | custom-call | flops 1 | bytes 1 | tf_op jit(solution)/shard_map/pallas_call | solution.py:193
  162.8 0.0 collective-permute-done.7.refs_2_
  162.8 0.0 collective-permute-done.8.refs_3_
  162.8 2.3 %shard_map.46 = bf16[32,64,128]{2,1,0:T(8,128)(2,1)S(1)} custom-call(s32[3]{0:T(128)S(1)} %copy-done.1, f32[3]{0:T(128)S(1)} %copy-done.2, f32[6,1,128]{2,1,0:T(1,128)S(1)} %reshape.14.wn, f32[6,1,128]{2,1,0:T(1,128)S(1)} %reshape.15.wh, f32[4,1,128]{2,1,0:T(1,128)S(1)} %dynamic-slice_bitcast_fusion.1.wr, f32[4,1,128]{2,1,0:T(1,128)S(1)} %dynamic-slice_bitcast_fusion.wx, ...), custom_call_target="tpu_custom_call" | custom-call | flops 1 | bytes 1 | tf_op jit(solution)/shard_map/pallas_call | solution.py:326
  165.1 20.2 %all_to_all.5 = bf16[32,64,128]{2,1,0:T(8,128)(2,1)S(1)} all-to-all(bf16[32,64,128]{2,1,0:T(8,128)(2,1)S(1)} %shard_map.46), channel_id=1, replica_groups=mesh['space'=8,'mode'=4] {'space','mode'}, dimensions={0} | all-to-all | bytes 1048576 | tf_op jit(solution)/shard_map/all_to_all | solution.py:530
  185.3 0.1 convert_reduce_fusion
  185.3 0.6 broadcast_multiply_fusion
  (4 shorter events, 0.1 us)
Async XLA Ops:
  0.6 8.4 %copy-start.1 = (s32[3]{0:T(128)S(1)}, s32[3]{0:T(128)}, u32[]{:S(2)}) copy-start(s32[3]{0:T(128)} %pad_add_fusion.order.refs_0_) | copy-start | bytes 40
  4.6 36.5 %collective-permute-start.3 = (bf16[48,128,128]{2,1,0:T(8,128)(2,1)}, bf16[48,128,128]{2,1,0:T(8,128)(2,1)S(1)}, u32[]{:S(2)}, u32[]{:S(2)}) collective-permute-start(bf16[48,128,128]{2,1,0:T(8,128)(2,1)} %get-tuple-element.36), channel_id=1, source_target_pairs={{0,1},{1,0},{2,3},{3,2},{4,5},{5,4},{6,7},{7,6},{8,9},{9,8},{10,11... | collective-permute-start | bytes 4718600 | tf_op jit(solution)/shard_map/ppermute | solution.py:478
  6.8 70.1 %collective-permute-start.2 = (bf16[48,128,128]{2,1,0:T(8,128)(2,1)}, bf16[48,128,128]{2,1,0:T(8,128)(2,1)}, u32[]{:S(2)}, u32[]{:S(2)}) collective-permute-start(bf16[48,128,128]{2,1,0:T(8,128)(2,1)} %get-tuple-element.33), channel_id=1, source_target_pairs={{0,3},{1,2},{2,1},{3,0},{4,7},{5,6},{6,5},{7,4},{8,11},{9,10},{10,... | collective-permute-start | bytes 4718600 | tf_op jit(solution)/shard_map/ppermute | solution.py:478
  9.0 2.8 %copy-start = (bf16[128,12,2048]{2,0,1:T(8,128)(2,1)S(1)}, bf16[128,12,2048]{2,0,1:T(8,128)(2,1)}, u32[]{:S(2)}) copy-start(bf16[128,12,2048]{2,0,1:T(8,128)(2,1)} %param.3) | copy-start | bytes 18874372
  11.8 2.5 %copy-start.4 = (s32[12,2048]{1,0:T(8,128)S(1)}, s32[12,2048]{1,0:T(8,128)}, u32[]{:S(2)}) copy-start(s32[12,2048]{1,0:T(8,128)} %param.4) | copy-start | bytes 294916
  11.8 9.7 %copy-start.2 = (f32[3]{0:T(128)S(1)}, f32[3]{0:T(128)}, u32[]{:S(2)}) copy-start(f32[3]{0:T(128)} %velocity.1) | copy-start | bytes 40
  14.1 123.3 %collective-permute-start.1 = (bf16[76,64,128]{2,1,0:T(8,128)(2,1)}, bf16[76,64,128]{2,1,0:T(8,128)(2,1)}, u32[]{:S(2)}, u32[]{:S(2)}) collective-permute-start(bf16[76,64,128]{2,1,0:T(8,128)(2,1)} %get-tuple-element.35), channel_id=1, source_target_pairs={{0,2},{1,3},{2,0},{3,1},{4,6},{5,7},{6,4},{7,5},{8,10},{9,11},{10,... | collective-permute-start | bytes 3735560 | tf_op jit(solution)/shard_map/ppermute | solution.py:478
  14.3 0.7 copy-start.3
  14.9 5.9 %collective-permute-start = (f32[1,2048]{1,0:T(1,128)S(1)}, f32[1,2048]{1,0:T(1,128)}, u32[]{:S(2)}, u32[]{:S(2)}) collective-permute-start(f32[1,2048]{1,0:T(1,128)S(1)} %get-tuple-element.61), channel_id=1, source_target_pairs={{4,0},{8,4},{12,8},{16,12},{20,16},{24,20},{28,24},{5,1},{9,5},{13... | collective-permute-start | bytes 24584 | tf_op jit(solution)/shard_map/ppermute | solution.py:473
  78.9 58.5 %collective-permute-start.4 = (bf16[4,384,128]{2,1,0:T(8,128)(2,1)S(1)}, bf16[4,384,128]{2,1,0:T(8,128)(2,1)S(1)}, u32[]{:S(2)}, u32[]{:S(2)}) collective-permute-start(bf16[4,384,128]{2,1,0:T(8,128)(2,1)S(1)} %get-tuple-element.46), channel_id=1, source_target_pairs={{4,0},{8,4},{12,8},{16,12},{20,16},{24,20},{28,24},{5,1},{9,5},{13... | collective-permute-start | bytes 1179656 | tf_op jit(solution)/shard_map/ppermute | solution.py:473
  83.6 79.2 %collective-permute-start.7 = (bf16[6,384,128]{2,1,0:T(8,128)(2,1)S(1)}, bf16[6,384,128]{2,1,0:T(8,128)(2,1)S(1)}, u32[]{:S(2)}, u32[]{:S(2)}) collective-permute-start(bf16[6,384,128]{2,1,0:T(8,128)(2,1)S(1)} %get-tuple-element.57), channel_id=1, source_target_pairs={{1,0},{2,1},{3,2},{4,5},{5,6},{6,7},{9,8},{10,9},{11,10},{12,13},{... | collective-permute-start | bytes 1769480 | tf_op jit(solution)/shard_map/ppermute | solution.py:482
  112.5 41.0 %collective-permute-start.5 = (bf16[20,64,128]{2,1,0:T(8,128)(2,1)S(1)}, bf16[20,64,128]{2,1,0:T(8,128)(2,1)S(1)}, u32[]{:S(2)}, u32[]{:S(2)}) collective-permute-start(bf16[20,64,128]{2,1,0:T(8,128)(2,1)S(1)} %get-tuple-element.48), channel_id=1, source_target_pairs={{0,2},{1,3},{2,0},{3,1},{4,6},{5,7},{6,4},{7,5},{8,10},{9,11},{10,... | collective-permute-start | bytes 983048 | tf_op jit(solution)/shard_map/ppermute | solution.py:478
  138.9 23.9 %collective-permute-start.8 = (bf16[6,128,128]{2,1,0:T(8,128)(2,1)S(1)}, bf16[6,128,128]{2,1,0:T(8,128)(2,1)S(1)}, u32[]{:S(2)}, u32[]{:S(2)}) collective-permute-start(bf16[6,128,128]{2,1,0:T(8,128)(2,1)S(1)} %get-tuple-element.58), channel_id=1, source_target_pairs={{1,0},{2,1},{3,2},{4,5},{5,6},{6,7},{9,8},{10,9},{11,10},{12,13},{... | collective-permute-start | bytes 589832 | tf_op jit(solution)/shard_map/ppermute | solution.py:482
  140.2 13.2 %collective-permute-start.6 = (bf16[4,128,128]{2,1,0:T(8,128)(2,1)S(1)}, bf16[4,128,128]{2,1,0:T(8,128)(2,1)S(1)}, u32[]{:S(2)}, u32[]{:S(2)}) collective-permute-start(bf16[4,128,128]{2,1,0:T(8,128)(2,1)S(1)} %get-tuple-element.51), channel_id=1, source_target_pairs={{4,0},{8,4},{12,8},{16,12},{20,16},{24,20},{28,24},{5,1},{9,5},{13... | collective-permute-start | bytes 393224 | tf_op jit(solution)/shard_map/ppermute | solution.py:473

commit v4 on v3

--- a/solution.py
+++ b/solution.py
@@ -58,45 +58,34 @@
 
 def phase_kernel(cfg, *refs):
     refs = list(refs)
-    d, off, count, whole = cfg["d"], cfg["off"], cfg["count"], cfg["whole"]
+    take = lambda k: [refs.pop(0) for _ in range(k)]
+    d, count, whole, index = cfg["d"], cfg["count"], cfg["whole"], cfg["index"]
     rows, tiles = cfg["rows"], cfg["tiles"]
-    steps, end, mine, span = rows // 2, off + count, slice(off, off + count), rows + 2
-    last, part = cfg["last"], count < whole
-    take = lambda k: [refs.pop(0) for _ in range(k)]
+    steps, span = rows // 2, rows + 2
     order, velocity, w = take(3)
     parts = take(cfg["n_parts"])
     old = [take(2) for _ in range(cfg["n_old"])]
-    prev = take(2) if cfg["prev"] else None
+    prev = take(2) if index == 1 else None
     gin = take(1)[0] if cfg["gin"] else None
-    xo = take(1)[0] if part and not last else None
-    a = None if last else take(1)[0]
-    (gout,) = take(1)
-    if last:
+    xo = take(1)[0] if index == 0 else None
+    a = take(1)[0] if index != 1 else None
+    gout = take(1)[0] if index != 0 else None
+    if index == 1:
         (a,) = take(1)
-    xs, t2 = take(2)
-    t1 = take(1)[0] if cfg["t1"] else None
-    g = gout
-    loads = []
-    if old or prev is not None:
-        held, sem = take(2)
-        sources = [v for pair in old for v in pair] + list(prev or [])
-        for k, v in enumerate(sources):
-            loads.append(pltpu.make_async_copy(v, held.at[k], sem.at[k]))
-            loads[-1].start()
-        old = [(held.at[2 * k], held.at[2 * k + 1]) for k in range(len(old))]
-        if prev is not None:
-            prev = (held.at[2 * len(old)], held.at[2 * len(old) + 1])
-
-    if part:
+    xs = take(1)[0]
+    t2 = take(1)[0] if index != 0 else None
+    t1 = take(1)[0] if old and index != 0 else None
+
+    if index is not None:
         rim, inner = parts[0], parts[-1]
         deep = rows - 2
         begin = inner.shape[0] - (tiles - 2) * deep
-        base = (off // count) * (2 * tiles + 2 * deep)
+        base = index * (2 * tiles + 2 * deep)
         sides = (base + 2 * tiles, base + 2 * tiles + deep)
     for t in range(tiles):
         xs[t * span] = jnp.zeros_like(xs[0])
         xs[t * span + rows + 1] = jnp.zeros_like(xs[0])
-        if part:
+        if index is not None:
             xs[t * span + 1] = rim[base + t]
             xs[t * span + rows] = rim[base + tiles + t]
             if t in (0, tiles - 1):
@@ -106,108 +95,81 @@
                 xs[t * span + 2 : t * span + rows] = inner[begin + (t - 1) * deep : begin + t * deep]
         else:
             xs[t * span + 1 : t * span + rows + 1] = parts[0][t * rows : (t + 1) * rows]
+
+    def stencil(i, carry):
+        apply_rows(i, cfg["eps"], velocity, w, xs, a, tiles, rows, 0, count)
+        return carry
+
+    lax.fori_loop(0, steps, stencil, 0)
+    if index == 0:
+        for t in range(tiles):
+            xo[t * rows : (t + 1) * rows] = xs[t * span + 1 : t * span + rows + 1]
+        return
+
     t2[...] = jnp.zeros_like(t2)
     if t1 is not None:
         t1[...] = jnp.zeros_like(t1)
-    def padded(value, before=None):
-        pieces = [value]
-        if off:
-            pieces.insert(0, jnp.zeros((off, LANES), BF) if before is None else before)
-        if end < whole:
-            pieces.append(jnp.zeros((whole - end, LANES), BF))
-        return pieces[0] if len(pieces) == 1 else jnp.concatenate(pieces, axis=0)
-
-    def stencil(i, carry):
-        apply_rows(i, cfg["eps"], velocity, w, xs, a, tiles, rows, off, count)
+
+    def body(i, carry):
+        pairs = [(r, t) for r in (0, 1) for t in range(tiles)]
+        picks = [t * rows + 2 * i + r for r, t in pairs]
+        join = lambda pieces: jnp.concatenate(pieces, axis=1)
+        wide = lambda ref: join([ref[k] for k in picks])
+        new = join([xs[t * span + 2 * i + r + 1] for r, t in pairs])
+        mark = wide(a)
+        if prev is not None:
+            new = jnp.concatenate([wide(prev[0]), new], axis=0)
+            mark = jnp.concatenate([wide(prev[1]), mark], axis=0)
+        t2[...] += product(jnp.concatenate([wide(ox) for ox, _ in old] + [new], axis=0), mark)
+        if old:
+            t1[...] += product(jnp.concatenate([wide(oa) for _, oa in old], axis=0), new)
         return carry
 
-    lax.fori_loop(0, steps, stencil, 0)
-    for c in loads:
-        c.wait()
-
-    def body(i, carry):
-        picks = [t * rows + 2 * i + r for r in (0, 1) for t in range(tiles)]
-        wide = lambda ref: jnp.concatenate([ref[k] for k in picks], axis=1)
-        new = [xs[t * span + 2 * i + r + 1] for r in (0, 1) for t in range(tiles)]
-        if part:
-            before = [None if prev is None else prev[0][k, :off, :] for k in picks]
-            both = [padded(v, u) for v, u in zip(new, before)]
-            if xo is not None:
-                for k, v in zip(picks, both):
-                    xo[k] = v
-        else:
-            both = new
-        fresh = [padded(v) for v in new]
-        mark = [padded(a[k, mine, :]) for k in picks]
-        if part and not last:
-            rest = slice(0, off) if off else slice(end, whole)
-            for k in picks:
-                a[k, rest, :] = jnp.zeros((whole - count, LANES), BF) if prev is None else prev[1][k, rest, :]
-        tall = [wide(ox) for ox, _ in old] + [jnp.concatenate(both, axis=1)]
-        t2[...] += product(jnp.concatenate(tall, axis=0), jnp.concatenate(mark, axis=1))
-        tall = [wide(oa) for _, oa in old] + ([wide(prev[1])] if prev is not None else [])
-        if tall:
-            t1[...] += product(jnp.concatenate(tall, axis=0), jnp.concatenate(fresh, axis=1))
-        return carry
-
     lax.fori_loop(0, steps, body, 0)
 
-    g[...] = jnp.zeros_like(g) if gin is None else gin[...]
+    gout[...] = jnp.zeros_like(gout) if gin is None else gin[...]
     block = lambda k: slice(k * whole, (k + 1) * whole)
-    names = [*cfg["old"], d]
-    for k, o in enumerate(names):
-        g[block(o), block(d)] += t2[block(k), :]
-    for k, o in enumerate(names if prev is not None else names[:-1]):
-        g[block(d), block(o)] += t1[block(k), :].T
+    for k, o in enumerate([*cfg["old"], d]):
+        gout[block(o), block(d)] += t2[block(k), :]
+        if o != d:
+            gout[block(d), block(o)] += t1[block(k), :].T
 
 
 def phase(cfg, order, velocity, w, parts, old, prev, gin):
     rows, tiles, whole, count = cfg["rows"], cfg["tiles"], cfg["whole"], cfg["count"]
-    size, last, part = cfg["n_blocks"] * whole, cfg["last"], count < whole
-    kept = jax.ShapeDtypeStruct((tiles * rows, whole, LANES), BF)
+    size, index = cfg["n_blocks"] * whole, cfg["index"]
+    kept = jax.ShapeDtypeStruct((tiles * rows, count, LANES), BF)
+    total = jax.ShapeDtypeStruct((size, size), F32)
     args = [order, velocity, w, *parts]
-    first = len(args)
     for group in [*old, *([prev] if prev is not None else [])]:
         args += list(group)
-    loaded = len(args) - first
     if gin is not None:
         args.append(gin)
-    scratch = []
-    if last:
-        out_shape = []
-        scratch.append(VMEM(kept.shape, BF))
-    else:
-        out_shape = [kept] * (2 if part else 1)
-    out_shape.append(jax.ShapeDtypeStruct((size, size), F32))
-    seconds = len(old) + (prev is not None)
+    out_shape = {None: [kept, total], 0: [kept, kept], 1: [total]}[index]
+    scratch = [VMEM(kept.shape, BF)] if index == 1 else []
     scratch.append(VMEM((tiles * (rows + 2), count, LANES), BF))
-    scratch.append(VMEM(((len(old) + 1) * whole, whole), F32))
-    if seconds:
-        scratch.append(VMEM((seconds * whole, whole), F32))
-    if loaded:
-        scratch += [VMEM((loaded, *kept.shape), BF), pltpu.SemaphoreType.DMA((loaded,))]
-    elements = rows * count * tiles * LANES
-    cfg = dict(cfg, n_parts=len(parts), n_old=len(old), prev=prev is not None, gin=gin is not None, t1=bool(seconds))
+    if index != 0:
+        scratch.append(VMEM(((len(old) + 1) * whole, whole), F32))
+        if old:
+            scratch.append(VMEM((len(old) * whole, whole), F32))
+    cfg = dict(cfg, n_parts=len(parts), n_old=len(old), gin=gin is not None)
     vmem = pl.BlockSpec(memory_space=VMEM)
     smem = pl.BlockSpec(memory_space=pltpu.SMEM)
-    outs = pl.pallas_call(
+    return pl.pallas_call(
         functools.partial(phase_kernel, cfg),
-        in_specs=[smem, smem]
-        + [pl.BlockSpec(memory_space=pl.ANY) if first <= k < first + loaded else vmem for k in range(2, len(args))],
+        in_specs=[smem, smem] + [vmem] * (len(args) - 2),
         out_specs=[vmem] * len(out_shape),
         out_shape=out_shape,
         scratch_shapes=scratch,
         compiler_params=pltpu.CompilerParams(vmem_limit_bytes=cfg["vmem"] << 20),
         cost_estimate=pl.CostEstimate(flops=1, bytes_accessed=1, transcendentals=0),
     )(*args)
-    if last:
-        return None, outs[0]
-    return (outs[0] if part else parts[0], outs[-2]), outs[-1]
-
-
-def line_kernel(rows, tiles, flip, *refs):
+
+
+def line_kernel(rows, tiles, choice, order, *refs):
     ins, (near, far, near_row, far_row) = refs[:-4], refs[-4:]
     deep = rows - 2
+    keep = order[1] == 0
 
     def tile_row(ref, row, t, c):
         if c is None:
@@ -217,47 +179,106 @@
             return ref[base + (tiles if row else 0) + t].astype(F32)
         return ref[base + 2 * tiles + (deep if t else 0) + row - 1].astype(F32)
 
-    parts = []
-    for ref in ins:
-        parts += [(ref, None)] if ref.shape[0] == tiles * rows else [(ref, 0), (ref, 1)]
-    keep = flip[0] == 0
+    def parts_of(ref):
+        return [(ref, None)] if ref.shape[0] == tiles * rows else [(ref, 0), (ref, 1)]
+
+    def line(ref, c, i, first):
+        t = 0 if first else tiles - 1
+        low = lax.broadcasted_iota(jnp.int32, (ref.shape[1], LANES), 1) < NZ
+        one, two = tile_row(ref, 2 * i, t, c), tile_row(ref, 2 * i + 1, t, c)
+        if first:
+            return jnp.where(low, one, pltpu.roll(two, NZ, 1))
+        return jnp.where(low, pltpu.roll(one, NZ, 1), two)
+
     start = 0
-    for ref, c in parts:
-        size = ref.shape[1]
-        low = lax.broadcasted_iota(jnp.int32, (size, LANES), 1) < NZ
-        modes = slice(start, start + size)
-        start += size
-        for t in range(tiles):
-            near_row[t, modes, :] = tile_row(ref, 0, t, c).astype(BF)
-            far_row[t, modes, :] = tile_row(ref, rows - 1, t, c).astype(BF)
-        for i in range(rows // 2):
-            one, two = tile_row(ref, 2 * i, 0, c), tile_row(ref, 2 * i + 1, 0, c)
-            first = jnp.where(low, one, pltpu.roll(two, NZ, 1))
-            one, two = tile_row(ref, 2 * i, tiles - 1, c), tile_row(ref, 2 * i + 1, tiles - 1, c)
-            final = jnp.where(low, pltpu.roll(one, NZ, 1), two)
-            near[i, modes, :] = jnp.where(keep, first, final).astype(BF)
-            far[i, modes, :] = jnp.where(keep, final, first).astype(BF)
-
-
-def lines_of(arrays, rows, tiles, flip):
-    modes = sum(v.shape[1] * (1 if v.shape[0] == tiles * rows else 2) for v in arrays)
+    for ref in ins[: choice[2]]:
+        for ref, c in parts_of(ref):
+            modes = slice(start, start + ref.shape[1])
+            start += ref.shape[1]
+            for t in range(tiles):
+                near_row[t, modes, :] = tile_row(ref, 0, t, c).astype(BF)
+                far_row[t, modes, :] = tile_row(ref, rows - 1, t, c).astype(BF)
+            for i in range(rows // 2):
+                value = jnp.where(keep, line(ref, c, i, False), line(ref, c, i, True))
+                far[i, modes, :] = value.astype(BF)
+
+    def send(ref):
+        start = 0
+        for ref, c in parts_of(ref):
+            modes = slice(start, start + ref.shape[1])
+            start += ref.shape[1]
+            for i in range(rows // 2):
+                value = jnp.where(keep, line(ref, c, i, True), line(ref, c, i, False))
+                near[i, modes, :] = value.astype(BF)
+
+    if choice[0] == choice[1]:
+        send(ins[choice[0]])
+    else:
+        pl.when(order[2] == 1)(lambda: send(ins[choice[0]]))
+        pl.when(order[2] != 1)(lambda: send(ins[choice[1]]))
+
+
+def lines_of(arrays, rows, tiles, order, choice):
+    size = lambda v: v.shape[1] * (1 if v.shape[0] == tiles * rows else 2)
+    modes = sum(size(v) for v in arrays[: choice[2]])
     vmem = pl.BlockSpec(memory_space=VMEM)
-    shape = jax.ShapeDtypeStruct((rows // 2, modes, LANES), BF)
+    lines = lambda m: jax.ShapeDtypeStruct((rows // 2, m, LANES), BF)
+    row = jax.ShapeDtypeStruct((tiles, modes, LANES), BF)
     return pl.pallas_call(
-        functools.partial(line_kernel, rows, tiles),
+        functools.partial(line_kernel, rows, tiles, choice),
         in_specs=[pl.BlockSpec(memory_space=pltpu.SMEM)] + [vmem] * len(arrays),
         out_specs=[vmem] * 4,
-        out_shape=[shape] * 2 + [jax.ShapeDtypeStruct((tiles, modes, LANES), BF)] * 2,
+        out_shape=[lines(size(arrays[choice[0]])), lines(modes), row, row],
         compiler_params=pltpu.CompilerParams(vmem_limit_bytes=12 << 20),
         cost_estimate=pl.CostEstimate(flops=1, bytes_accessed=1, transcendentals=0),
-    )(flip.reshape(1), *arrays)
-
-
-def border_kernel(eps, groups, space, n, order, velocity, wn, wh, wr, wx, gin, *refs):
+    )(order, *arrays)
+
+
+def halo_kernel(n, tiles, order, field, *refs):
+    outs, (line, sem) = refs[:2], refs[2:]
+    q, flip = order[0], order[1]
+    copies = []
+    for d in (0, 1):
+        owner = q ^ d
+        at = jnp.where(
+            flip == 0,
+            jnp.minimum((owner + 1) * tiles, n * tiles - 1),
+            jnp.maximum(owner * tiles - 1, 0),
+        )
+        at = pl.ds(pl.multiple_of(at * LANES, LANES), LANES)
+        copies.append(pltpu.make_async_copy(field.at[:, :, at], line.at[d], sem.at[d]))
+        copies[-1].start()
+    low = lax.broadcasted_iota(jnp.int32, line.shape[2:], 1) < NZ
+    for d in (0, 1):
+        copies[d].wait()
+        owner = q ^ d
+        none = jnp.where(flip == 0, owner == n - 1, owner == 0)
+        for i in range(line.shape[1] // 2):
+            one, two = line[d, 2 * i].astype(F32), line[d, 2 * i + 1].astype(F32)
+            front = jnp.where(low, one, pltpu.roll(two, NZ, 1))
+            back = jnp.where(low, pltpu.roll(one, NZ, 1), two)
+            value = jnp.where(flip == 0, front, back)
+            outs[d][i] = jnp.where(none, 0.0, value).astype(BF)
+
+
+def halos_of(n, tiles, order, field):
+    rows, count, _ = field.shape
+    shape = jax.ShapeDtypeStruct((rows // 2, count, LANES), BF)
+    return pl.pallas_call(
+        functools.partial(halo_kernel, n, tiles),
+        in_specs=[pl.BlockSpec(memory_space=pltpu.SMEM), pl.BlockSpec(memory_space=pl.ANY)],
+        out_specs=[pl.BlockSpec(memory_space=VMEM)] * 2,
+        out_shape=[shape] * 2,
+        scratch_shapes=[VMEM((2, rows, count, LANES), BF), pltpu.SemaphoreType.DMA((2,))],
+        compiler_params=pltpu.CompilerParams(vmem_limit_bytes=12 << 20),
+        cost_estimate=pl.CostEstimate(flops=1, bytes_accessed=1, transcendentals=0),
+    )(order, field)
+
+
+def border_kernel(eps, groups, beyond, space, n, order, velocity, wn, wh, wr, wx, gin, *refs):
     count = len(groups)
-    here, there = refs[:count], refs[count : 2 * count]
-    own, over = refs[2 * count : 3 * count], refs[3 * count : 4 * count]
-    g, out = refs[-1], refs[4 * count]
+    here, own, over = refs[:count], refs[count : 2 * count], refs[2 * count : 3 * count]
+    there, (out, g) = refs[3 * count : -2], refs[-2:]
     xp, xm = eps - 0.5 * velocity[0], eps + 0.5 * velocity[0]
     yp, ym = eps - 0.5 * velocity[1], eps + 0.5 * velocity[1]
     toward = jnp.where(order[1] == 0, yp, ym)
@@ -265,27 +286,19 @@
     blocks = sum(len(names) for names in groups)
     size = g.shape[0] // blocks
 
-    def find(refs, d, i):
+    def find(refs, d, i, groups=groups):
         for names, ref in zip(groups, refs):
             if d in names:
                 k = names.index(d)
                 return ref[i, k * size : (k + 1) * size, :]
 
-    def every(refs, i):
-        return jnp.concatenate([find(refs, d, i) for d in range(blocks)], axis=0)
+    def every(refs, i, groups=groups):
+        return jnp.concatenate([find(refs, d, i, groups) for d in range(blocks)], axis=0)
 
     left, right = [], []
     for k in range(wn.shape[0]):
         mine = every(here, k)
-        if blocks == 4:
-            near = order[2] == 1
-            other = [
-                jnp.where(near, find(there, d ^ 1, k).astype(F32), find(there, d ^ 3, k).astype(F32))
-                for d in range(blocks)
-            ]
-            other = jnp.concatenate(other, axis=0)
-        else:
-            other = every(there, k).astype(F32)
+        other = every(there, k, beyond).astype(F32)
         left += [mine, other.astype(BF)]
         right += [(wn[k] * (toward * other)).astype(BF), (wh[k] * (back * mine.astype(F32))).astype(BF)]
     for t in range(wr.shape[0]):
@@ -314,7 +327,7 @@
         out[...] = total
 
 
-def border(eps, groups, order, velocity, weights, gin, here, there, own, over, space, n):
+def border(eps, groups, beyond, order, velocity, weights, gin, here, own, over, there, space, n):
     vmem = pl.BlockSpec(memory_space=VMEM)
     smem = pl.BlockSpec(memory_space=pltpu.SMEM)
     blocks = sum(len(names) for names in groups)
@@ -322,9 +335,9 @@
     if blocks == n:
         size = gin.shape[0]
         shape = jax.ShapeDtypeStruct((space * n, size // space, size // n), BF)
-    args = [order, velocity, *weights, gin, *here, *there, *own, *over]
+    args = [order, velocity, *weights, gin, *here, *own, *over, *there]
     return pl.pallas_call(
-        functools.partial(border_kernel, eps, groups, space, n),
+        functools.partial(border_kernel, eps, groups, beyond, space, n),
         in_specs=[smem, smem] + [vmem] * (len(args) - 2),
         out_specs=vmem,
         out_shape=shape,
@@ -480,19 +493,23 @@
     relay = [(s * n + i, s * n + i - 1 + 2 * (s & 1)) for s in range(space) for i in range(n)]
     relay = [(i, j) for i, j in relay if i // n == j // n and j >= 0]
     beside = lambda v: lax.ppermute(v, ("space", "mode"), relay)
-    partner = jnp.clip(q + 1 - 2 * flip, 0, n - 1) ^ q
+    source = jnp.clip(q + 1 - 2 * flip, 0, n - 1) ^ q
+    partner = jnp.clip(q - 1 + 2 * flip, 0, n - 1) ^ q
     order = jnp.stack([q, flip, partner])
-    base = dict(rows=rows, tiles=tiles, eps=eps, n=n, space=space, last=False, off=0, d=0, vmem=24)
+    base = dict(rows=rows, tiles=tiles, eps=eps, n=n, space=space, index=None, d=0, vmem=12)
     if n != 4:
         xs = [slab(field, q)] + [swap(slab(field, q ^ d), d) for d in range(1, n)]
         x = jnp.concatenate(xs, axis=1)
         cfg = dict(base, whole=n * count, count=n * count, n_blocks=1, old=[], vmem=40)
         x = jnp.concatenate([x[:, :, t * LANES : (t + 1) * LANES] for t in range(tiles)], axis=0)
         _, total = phase(cfg, order, velocity, w, [x], [], None, None)
-        send, here, send_row, own = lines_of([x], rows, tiles, flip)
+        send, here, send_row, own = lines_of([x], rows, tiles, order, (0, 0, 1))
         there = beside(send).reshape(rows // 2, n, count, LANES)
-        there = there[:, jnp.arange(n) ^ partner].reshape(send.shape)
-        total = border(eps, [[0]], order, velocity, weights, total, [here], [there], [own], [above(send_row)], space, n)
+        there = there[:, jnp.arange(n) ^ source].reshape(send.shape)
+        total = border(
+            eps, [[0]], [[0]], order, velocity, weights, total,
+            [here], [own], [above(send_row)], [there], space, n,
+        )
         tiles = spread_out(total, n, space, q, count)
     else:
         half = count // 2
@@ -502,30 +519,37 @@
         x0, p2, p2b = pack(jobs, tiles, order, after(field, p3))
         front, back = swap(p2, 2), swap(p2b, 2)
         base = dict(base, whole=count, n_blocks=n)
-        names, old, g, met = [], [], None, []
-
-        def meet(*arrays):
-            send, here, row, own = lines_of(arrays, rows, tiles, flip)
-            met.append((here, beside(send), own, above(row)))
+        names, old, g = [], [], None
+
+        halo, halo1 = halos_of(n, tiles, order, after(field, p2b))
+        there, met = [halo, swap(halo1, 1)], []
+
+        def meet(arrays, choice):
+            send, here, row, own = lines_of(arrays, rows, tiles, order, choice)
+            met.append((here, own, above(row)))
+            there.append(beside(send))
 
         x0 = after(x0, weights)
         for d, x in ((0, x0), (1, x1), (3, x3)):
             if names:
                 x = after(x, g)
             if d == 3:
-                meet(x0, x1, x)
+                meet([x0, x1, x], (2, 1, 3))
             cfg = dict(base, count=count, d=d, old=list(names))
             kept, g = phase(cfg, order, velocity, w, [x], old, None, g)
-            names, old = [*names, d], [*old, kept]
-        front = after(front, (g, met[-1][3]))
-        meet(front)
-        part = dict(base, d=2, count=half, old=names)
-        kept, g = phase(part, order, velocity, w, [front], old, None, g)
-        back = after(back, (g, met[-1][3]))
-        part = dict(part, off=half, last=True)
-        _, g = phase(part, order, velocity, w, [front, back], old, kept, g)
+            names, old = [*names, d], [*old, (x, kept)]
+        front = after(front, (g, met[-1][2]))
+        meet([front, x0], (0, 1, 1))
+        part = dict(base, d=2, count=half, old=names, index=0)
+        kept = phase(part, order, velocity, w, [front], [], None, None)
+        back = after(back, (kept[1], met[-1][2]))
+        part = dict(part, index=1)
+        (g,) = phase(part, order, velocity, w, [front, back], old, kept, g)
         met = [list(v) for v in zip(*met)]
-        g = border(eps, [[0, 1, 3], [2]], order, velocity, weights, g, *met, space, n)
+        g = border(
+            eps, [[0, 1, 3], [2]], [[0], [1], [2], [3]], order, velocity, weights, g,
+            *met, there, space, n,
+        )
         tiles = g
     arrived = lax.all_to_all(tiles, ("space", "mode"), split_axis=0, concat_axis=0, tiled=True)
     return jnp.sum(arrived.astype(F32), axis=0) * eps

time: 187 us -> 181 us (0.968)
  Pallas kernels: 56.2 us -> 51.6 us
  waiting for transfers between devices: 53.3 us -> 51.3 us
    ppermute x4 -> x5, starting transfers between devices: 6.11 us -> 33.2 us  [swap(): return lax.ppermute(part, 'mode', [(i, i ^ d) for i in range(n)])]
    ppermute x2, starting transfers between devices: 30.2 us -> 4.66 us  [local(): beside = lambda v: lax.ppermute(v, ('space', 'mode'), relay)]
    pallas_call x5, Pallas kernels: 44.2 us -> 38.1 us  [phase(): pl.pallas_call(functools.partial(phase_kernel, cfg), in_specs=[smem, smem...]
    ppermute x4 -> x5, waiting for transfers between devices: 52.4 us -> 50.4 us  [swap(): return lax.ppermute(part, 'mode', [(i, i ^ d) for i in range(n)])]
    pallas_call x3 -> x4, Pallas kernels: 5.82 us -> 7.19 us  [the longest x2 3.79 us: lines_of(): pl.pallas_call(functools.partial(line_kernel, rows, tiles, choice), in_sp...]
  transfers between devices with their start and end apart: 9 -> 10, of which waited for: 4 -> 4; matrix products, arithmetic and copies ran while one was open for 1% -> 1% of each run, Pallas kernels for 27% -> 25%
where the time goes in v4:
time: 181 us
  Pallas kernels  51.6 us (29%)
  waiting for transfers between devices  51.3 us (28%)
  starting transfers between devices  50.3 us (28%)
  blocking collectives  20.2 us (11%)
  local copies, waits for them, and re-layouts  5.93 us (3%)
    ppermute x5, waiting for transfers between devices, swap(): return lax.ppermute(part, 'mode', [(i, i ^ d) for i in range(n)])  50.4 us
    pallas_call x5, Pallas kernels, phase(): pl.pallas_call(functools.partial(phase_kernel, cfg), in_specs=[smem, smem...  38.1 us
    ppermute x5, starting transfers between devices, swap(): return lax.ppermute(part, 'mode', [(i, i ^ d) for i in range(n)])  33.2 us
    all_to_all x1, blocking collectives, local(): lax.all_to_all(tiles, ('space', 'mode'), split_axis=0, concat_axis=0, til...  20.2 us
    ppermute x3, starting transfers between devices, local(): above = lambda v: lax.ppermute(v, 'space', ahead)  12.4 us
    ppermute x2, starting transfers between devices, local(): beside = lambda v: lax.ppermute(v, ('space', 'mode'), relay)  4.66 us
    pallas_call x1, Pallas kernels, first_pack(): pl.pallas_call(functools.partial(first_kernel, owners, rows, tiles), in_s...  3.96 us
    pallas_call x2, Pallas kernels, lines_of(): pl.pallas_call(functools.partial(line_kernel, rows, tiles, choice), in_sp...  3.79 us
  transfers between devices with their start and end apart: 10, of which 4 were waited for; matrix products, arithmetic and copies ran while one was open for 1% of the time, Pallas kernels for 25%

profile of v4, /device:TPU:1, one launch (start us, length us, event | category | flops | bytes accessed | tf_op | source)
XLA Modules:
  0.0 180.9 jit_solution(9228686639278285196)
XLA Ops:
  0.0 0.6 pad_add_fusion.order.refs_0_
  0.6 0.0 copy-start.1
  0.6 4.0 %shard_map.37 = (bf16[48,128,128]{2,1,0:T(8,128)(2,1)}, bf16[48,128,128]{2,1,0:T(8,128)(2,1)}) custom-call(s32[3]{0:T(128)} %pad_add_fusion.order.refs_0_, bf16[12,128,2048]{2,1,0:T(8,128)(2,1)} %bitcast.8), custom_call_target="tpu_custom_call" | custom-call | tf_op jit(solution)/shard_map/pallas_call | solution.py:434
  4.6 2.2 %collective-permute-start.3 = (bf16[48,128,128]{2,1,0:T(8,128)(2,1)}, bf16[48,128,128]{2,1,0:T(8,128)(2,1)S(1)}, u32[]{:S(2)}, u32[]{:S(2)}) collective-permute-start(bf16[48,128,128]{2,1,0:T(8,128)(2,1)} %get-tuple-element.38), channel_id=1, source_target_pairs={{0,1},{1,0},{2,3},{3,2},{4,5},{5,4},{6,7},{7,6},{8,9},{9,8},{10,11... | collective-permute-start | bytes 4718600 | tf_op jit(solution)/shard_map/ppermute | solution.py:491
  6.8 2.2 %collective-permute-start.2 = (bf16[48,128,128]{2,1,0:T(8,128)(2,1)}, bf16[48,128,128]{2,1,0:T(8,128)(2,1)}, u32[]{:S(2)}, u32[]{:S(2)}) collective-permute-start(bf16[48,128,128]{2,1,0:T(8,128)(2,1)} %get-tuple-element.35), channel_id=1, source_target_pairs={{0,3},{1,2},{2,1},{3,0},{4,7},{5,6},{6,5},{7,4},{8,11},{9,10},{10,... | collective-permute-start | bytes 4718600 | tf_op jit(solution)/shard_map/ppermute | solution.py:491
  9.0 0.0 copy-done.1
  9.0 0.0 copy-start
  9.0 2.8 %copy-done = bf16[128,12,2048]{2,0,1:T(8,128)(2,1)S(1)} copy-done((bf16[128,12,2048]{2,0,1:T(8,128)(2,1)S(1)}, bf16[128,12,2048]{2,0,1:T(8,128)(2,1)}, u32[]{:S(2)}) %copy-start) | copy-done | bytes 6291480
  11.8 0.0 copy-start.4
  11.8 0.0 copy-start.2
  11.8 2.3 %shard_map.38 = (bf16[48,128,128]{2,1,0:T(8,128)(2,1)S(1)}, bf16[76,64,128]{2,1,0:T(8,128)(2,1)}, bf16[20,64,128]{2,1,0:T(8,128)(2,1)S(1)}) custom-call(s32[3]{0:T(128)S(1)} %copy-done.1, bf16[12,128,2048]{2,1,0:T(8,128)(2,1)S(1)} %bitcast.9), custom_call_target="tpu_custom_call" | custom-call | tf_op jit(solution)/shard_map/pallas_call | solution.py:399
  14.1 0.2 collective-permute-start.1
  14.2 0.0 copy-done.4
  14.3 0.0 copy-start.3
  14.3 0.6 copy-done.3
  14.9 3.1 %collective-permute-start = (f32[1,2048]{1,0:T(1,128)S(1)}, f32[1,2048]{1,0:T(1,128)}, u32[]{:S(2)}, u32[]{:S(2)}) collective-permute-start(f32[1,2048]{1,0:T(1,128)S(1)} %get-tuple-element.65), channel_id=1, source_target_pairs={{4,0},{8,4},{12,8},{16,12},{20,16},{24,20},{28,24},{5,1},{9,5},{13... | collective-permute-start | bytes 24584 | tf_op jit(solution)/shard_map/ppermute | solution.py:486
  18.1 0.9 constant_dynamic-slice_fusion.1
  19.0 0.8 constant_dynamic-slice_fusion
  19.7 0.1 reshape.12.wn
  19.8 0.1 reshape.13.wh
  19.9 0.9 collective-permute-done
  20.8 0.7 dynamic-slice_bitcast_fusion.wx
  21.5 0.0 copy-done.2
  21.5 0.0 slice-start
  21.5 7.3 %shard_map.39 = (bf16[48,128,128]{2,1,0:T(8,128)(2,1)S(1)}, f32[512,512]{1,0:T(8,128)S(1)}) custom-call(s32[3]{0:T(128)S(1)} %copy-done.1, f32[3]{0:T(128)S(1)} %copy-done.2, f32[12,1,512]{2,1,0:T(1,128)S(1)} %broadcast_in_dim.18.refs_2_, bf16[48,128,128]{2,1,0:T(8,128)(2,1)S(1)} %get-tuple-element.40.refs_3_.refs_4_.refs_0_.refs_1_.refs_5_), custom_call_target="tpu_custom_call" | custom-call | flops 1 | bytes 1 | tf_op jit(solution)/shard_map/pallas_call | solution.py:158
  28.8 12.3 %collective-permute-done.3.refs_3_.refs_6_.refs_1_.refs_7_ = bf16[48,128,128]{2,1,0:T(8,128)(2,1)S(1)} collective-permute-done((bf16[48,128,128]{2,1,0:T(8,128)(2,1)}, bf16[48,128,128]{2,1,0:T(8,128)(2,1)S(1)}, u32[]{:S(2)}, u32[]{:S(2)}) %collective-permute-start.3) | collective-permute-done | bytes 1572896 | tf_op jit(solution)/shard_map/ppermute | solution.py:491
  41.1 0.0 slice-start.1
  41.1 8.3 %shard_map.40 = (bf16[48,128,128]{2,1,0:T(8,128)(2,1)S(1)}, f32[512,512]{1,0:T(8,128)S(1)}) custom-call(s32[3]{0:T(128)S(1)} %copy-done.1, f32[3]{0:T(128)S(1)} %copy-done.2, f32[12,1,512]{2,1,0:T(1,128)S(1)} %broadcast_in_dim.18.refs_2_, bf16[48,128,128]{2,1,0:T(8,128)(2,1)S(1)} %collective-permute-done.3.refs_3_.refs_6_.refs_1_.refs_7_, ...), custom_call_target="tpu_custom_call" | custom-call | flops 1 | bytes 1 | tf_op jit(solution)/shard_map/pallas_call | solution.py:158
  49.4 27.5 %collective-permute-done.2.refs_3_.refs_2_.refs_9_ = bf16[48,128,128]{2,1,0:T(8,128)(2,1)} collective-permute-done((bf16[48,128,128]{2,1,0:T(8,128)(2,1)}, bf16[48,128,128]{2,1,0:T(8,128)(2,1)}, u32[]{:S(2)}, u32[]{:S(2)}) %collective-permute-start.2) | collective-permute-done | bytes 1572896 | tf_op jit(solution)/shard_map/ppermute | solution.py:491
  76.8 2.1 %shard_map.42 = (bf16[6,128,128]{2,1,0:T(8,128)(2,1)S(1)}, bf16[6,384,128]{2,1,0:T(8,128)(2,1)S(1)}, bf16[4,384,128]{2,1,0:T(8,128)(2,1)S(1)}, bf16[4,384,128]{2,1,0:T(8,128)(2,1)S(1)}) custom-call(s32[3]{0:T(128)S(1)} %copy-done.1, bf16[48,128,128]{2,1,0:T(8,128)(2,1)S(1)} %get-tuple-element.40.refs_3_.refs_4_.refs_0_.refs_1_.refs_5_, ...), custom_call_target="tpu_custom_call" | custom-call | flops 1 | bytes 1 | tf_op jit(solution)/shard_map/pallas_call | solution.py:227
  79.0 4.7 %collective-permute-start.4 = (bf16[4,384,128]{2,1,0:T(8,128)(2,1)S(1)}, bf16[4,384,128]{2,1,0:T(8,128)(2,1)S(1)}, u32[]{:S(2)}, u32[]{:S(2)}) collective-permute-start(bf16[4,384,128]{2,1,0:T(8,128)(2,1)S(1)} %get-tuple-element.48), channel_id=1, source_target_pairs={{4,0},{8,4},{12,8},{16,12},{20,16},{24,20},{28,24},{5,1},{9,5},{13... | collective-permute-start | bytes 1179656 | tf_op jit(solution)/shard_map/ppermute | solution.py:486
  83.6 28.5 %collective-permute-start.5 = (bf16[20,64,128]{2,1,0:T(8,128)(2,1)S(1)}, bf16[20,64,128]{2,1,0:T(8,128)(2,1)S(1)}, u32[]{:S(2)}, u32[]{:S(2)}) collective-permute-start(bf16[20,64,128]{2,1,0:T(8,128)(2,1)S(1)} %get-tuple-element.50), channel_id=1, source_target_pairs={{0,2},{1,3},{2,0},{3,1},{4,6},{5,7},{6,4},{7,5},{8,10},{9,11},{10,... | collective-permute-start | bytes 983048 | tf_op jit(solution)/shard_map/ppermute | solution.py:491
  112.2 0.0 slice-done
  112.2 0.0 slice-done.1
  112.2 1.1 shard_map.46
  113.3 0.1 collective-permute-start.7
  113.4 9.9 %shard_map.41 = (bf16[48,128,128]{2,1,0:T(8,128)(2,1)S(1)}, f32[512,512]{1,0:T(8,128)S(1)}) custom-call(s32[3]{0:T(128)S(1)} %copy-done.1, f32[3]{0:T(128)S(1)} %copy-done.2, f32[12,1,512]{2,1,0:T(1,128)S(1)} %broadcast_in_dim.18.refs_2_, bf16[48,128,128]{2,1,0:T(8,128)(2,1)} %collective-permute-done.2.refs_3_.refs_2_.refs_9_, ...), custom_call_target="tpu_custom_call" | custom-call | flops 1 | bytes 1 | tf_op jit(solution)/shard_map/pallas_call | solution.py:158
  123.4 3.4 %collective-permute-start.8 = (bf16[6,128,128]{2,1,0:T(8,128)(2,1)S(1)}, bf16[6,128,128]{2,1,0:T(8,128)(2,1)S(1)}, u32[]{:S(2)}, u32[]{:S(2)}) collective-permute-start(bf16[6,128,128]{2,1,0:T(8,128)(2,1)S(1)} %get-tuple-element.63), channel_id=1, source_target_pairs={{1,0},{2,1},{3,2},{4,5},{5,6},{6,7},{9,8},{10,9},{11,10},{12,13},{... | collective-permute-start | bytes 589832 | tf_op jit(solution)/shard_map/ppermute | solution.py:495
  126.7 10.6 %collective-permute-done.1.refs_3_.refs_0_ = bf16[76,64,128]{2,1,0:T(8,128)(2,1)} collective-permute-done((bf16[76,64,128]{2,1,0:T(8,128)(2,1)}, bf16[76,64,128]{2,1,0:T(8,128)(2,1)}, u32[]{:S(2)}, u32[]{:S(2)}) %collective-permute-start.1) | collective-permute-done | bytes 1245216 | tf_op jit(solution)/shard_map/ppermute | solution.py:491
  137.3 0.0 collective-permute-done.4.refs_4_
  137.3 1.7 shard_map.44
  139.0 1.3 collective-permute-start.9
  140.3 4.6 %collective-permute-start.6 = (bf16[4,128,128]{2,1,0:T(8,128)(2,1)S(1)}, bf16[4,128,128]{2,1,0:T(8,128)(2,1)S(1)}, u32[]{:S(2)}, u32[]{:S(2)}) collective-permute-start(bf16[4,128,128]{2,1,0:T(8,128)(2,1)S(1)} %get-tuple-element.52), channel_id=1, source_target_pairs={{4,0},{8,4},{12,8},{16,12},{20,16},{24,20},{28,24},{5,1},{9,5},{13... | collective-permute-start | bytes 393224 | tf_op jit(solution)/shard_map/ppermute | solution.py:486
  145.0 4.1 %shard_map.43 = (bf16[48,64,128]{2,1,0:T(8,128)(2,1)S(1)}, bf16[48,64,128]{2,1,0:T(8,128)(2,1)S(1)}) custom-call(s32[3]{0:T(128)S(1)} %copy-done.1, f32[3]{0:T(128)S(1)} %copy-done.2, f32[12,1,512]{2,1,0:T(1,128)S(1)} %broadcast_in_dim.18.refs_2_, bf16[76,64,128]{2,1,0:T(8,128)(2,1)} %collective-permute-done.1.refs_3_.refs_0_), custom_call_target="tpu_custom_call" | custom-call | flops 1 | bytes 1 | tf_op jit(solution)/shard_map/pallas_call | solution.py:158
  149.1 0.0 collective-permute-done.5.refs_4_
  149.1 0.0 collective-permute-done.6.refs_5_
  149.1 8.6 %shard_map.45.gin = f32[512,512]{1,0:T(8,128)S(1)} custom-call(s32[3]{0:T(128)S(1)} %copy-done.1, f32[3]{0:T(128)S(1)} %copy-done.2, f32[12,1,512]{2,1,0:T(1,128)S(1)} %broadcast_in_dim.18.refs_2_, bf16[76,64,128]{2,1,0:T(8,128)(2,1)} %collective-permute-done.1.refs_3_.refs_0_, bf16[20,64,128]{2,1,0:T(8,128)(2,1)S(1)} %collective-permute-done.5.refs_4_, ...), custom_call_target="tpu_custom_call" | custom-call | flops 1 | bytes 1 | tf_op jit(solution)/shard_map/pallas_call | solution.py:158
  157.7 0.0 collective-permute-done.7.refs_7_
  157.7 0.0 collective-permute-done.8.refs_8_
  157.7 0.0 collective-permute-done.9.refs_9_
  157.7 2.3 %shard_map.47 = bf16[32,64,128]{2,1,0:T(8,128)(2,1)S(1)} custom-call(s32[3]{0:T(128)S(1)} %copy-done.1, f32[3]{0:T(128)S(1)} %copy-done.2, f32[6,1,128]{2,1,0:T(1,128)S(1)} %reshape.12.wn, f32[6,1,128]{2,1,0:T(1,128)S(1)} %reshape.13.wh, f32[4,1,128]{2,1,0:T(1,128)S(1)} %dynamic-slice_bitcast_fusion.1.wr, f32[4,1,128]{2,1,0:T(1,128)S(1)} %dynamic-slice_bitcast_fusion.wx, ...), custom_call_target="tpu_custom_call" | custom-call | flops 1 | bytes 1 | tf_op jit(solution)/shard_map/pallas_call | solution.py:339
  160.0 20.2 %all_to_all.5 = bf16[32,64,128]{2,1,0:T(8,128)(2,1)S(1)} all-to-all(bf16[32,64,128]{2,1,0:T(8,128)(2,1)S(1)} %shard_map.47), channel_id=1, replica_groups=mesh['space'=8,'mode'=4] {'space','mode'}, dimensions={0} | all-to-all | bytes 1048576 | tf_op jit(solution)/shard_map/all_to_all | solution.py:554
  180.2 0.1 convert_reduce_fusion
  180.2 0.6 broadcast_multiply_fusion
  (5 shorter events, 0.1 us)
Async XLA Ops:
  0.6 8.4 %copy-start.1 = (s32[3]{0:T(128)S(1)}, s32[3]{0:T(128)}, u32[]{:S(2)}) copy-start(s32[3]{0:T(128)} %pad_add_fusion.order.refs_0_) | copy-start | bytes 40
  4.6 36.5 %collective-permute-start.3 = (bf16[48,128,128]{2,1,0:T(8,128)(2,1)}, bf16[48,128,128]{2,1,0:T(8,128)(2,1)S(1)}, u32[]{:S(2)}, u32[]{:S(2)}) collective-permute-start(bf16[48,128,128]{2,1,0:T(8,128)(2,1)} %get-tuple-element.38), channel_id=1, source_target_pairs={{0,1},{1,0},{2,3},{3,2},{4,5},{5,4},{6,7},{7,6},{8,9},{9,8},{10,11... | collective-permute-start | bytes 4718600 | tf_op jit(solution)/shard_map/ppermute | solution.py:491
  6.8 70.1 %collective-permute-start.2 = (bf16[48,128,128]{2,1,0:T(8,128)(2,1)}, bf16[48,128,128]{2,1,0:T(8,128)(2,1)}, u32[]{:S(2)}, u32[]{:S(2)}) collective-permute-start(bf16[48,128,128]{2,1,0:T(8,128)(2,1)} %get-tuple-element.35), channel_id=1, source_target_pairs={{0,3},{1,2},{2,1},{3,0},{4,7},{5,6},{6,5},{7,4},{8,11},{9,10},{10,... | collective-permute-start | bytes 4718600 | tf_op jit(solution)/shard_map/ppermute | solution.py:491
  9.0 2.8 %copy-start = (bf16[128,12,2048]{2,0,1:T(8,128)(2,1)S(1)}, bf16[128,12,2048]{2,0,1:T(8,128)(2,1)}, u32[]{:S(2)}) copy-start(bf16[128,12,2048]{2,0,1:T(8,128)(2,1)} %param.3) | copy-start | bytes 18874372
  11.8 2.5 %copy-start.4 = (s32[12,2048]{1,0:T(8,128)S(1)}, s32[12,2048]{1,0:T(8,128)}, u32[]{:S(2)}) copy-start(s32[12,2048]{1,0:T(8,128)} %param.4) | copy-start | bytes 294916
  11.8 9.7 %copy-start.2 = (f32[3]{0:T(128)S(1)}, f32[3]{0:T(128)}, u32[]{:S(2)}) copy-start(f32[3]{0:T(128)} %velocity.1) | copy-start | bytes 40
  14.1 123.3 %collective-permute-start.1 = (bf16[76,64,128]{2,1,0:T(8,128)(2,1)}, bf16[76,64,128]{2,1,0:T(8,128)(2,1)}, u32[]{:S(2)}, u32[]{:S(2)}) collective-permute-start(bf16[76,64,128]{2,1,0:T(8,128)(2,1)} %get-tuple-element.37), channel_id=1, source_target_pairs={{0,2},{1,3},{2,0},{3,1},{4,6},{5,7},{6,4},{7,5},{8,10},{9,11},{10,... | collective-permute-start | bytes 3735560 | tf_op jit(solution)/shard_map/ppermute | solution.py:491
  14.3 0.7 copy-start.3
  14.9 5.9 %collective-permute-start = (f32[1,2048]{1,0:T(1,128)S(1)}, f32[1,2048]{1,0:T(1,128)}, u32[]{:S(2)}, u32[]{:S(2)}) collective-permute-start(f32[1,2048]{1,0:T(1,128)S(1)} %get-tuple-element.65), channel_id=1, source_target_pairs={{4,0},{8,4},{12,8},{16,12},{20,16},{24,20},{28,24},{5,1},{9,5},{13... | collective-permute-start | bytes 24584 | tf_op jit(solution)/shard_map/ppermute | solution.py:486
  21.5 90.7 %slice-start = ((s8[6291456]{0:T(1024)(128)(4,1)}), s8[4194304]{0:T(1024)(128)(4,1)S(1)}, s32[]{:S(2)}) async-start(s8[6291456]{0:T(1024)(128)(4,1)} %bitcast.10), calls=%async_computation.1 | async-start | bytes 8388608
  41.1 71.1 %slice-start.1 = ((s8[6291456]{0:T(1024)(128)(4,1)}), s8[2097152]{0:T(1024)(128)(4,1)S(1)}, s32[]{:S(2)}) async-start(s8[6291456]{0:T(1024)(128)(4,1)} %bitcast.10), calls=%async_computation.2 | async-start | bytes 4194304
  79.0 58.4 %collective-permute-start.4 = (bf16[4,384,128]{2,1,0:T(8,128)(2,1)S(1)}, bf16[4,384,128]{2,1,0:T(8,128)(2,1)S(1)}, u32[]{:S(2)}, u32[]{:S(2)}) collective-permute-start(bf16[4,384,128]{2,1,0:T(8,128)(2,1)S(1)} %get-tuple-element.48), channel_id=1, source_target_pairs={{4,0},{8,4},{12,8},{16,12},{20,16},{24,20},{28,24},{5,1},{9,5},{13... | collective-permute-start | bytes 1179656 | tf_op jit(solution)/shard_map/ppermute | solution.py:486
  83.6 65.4 %collective-permute-start.5 = (bf16[20,64,128]{2,1,0:T(8,128)(2,1)S(1)}, bf16[20,64,128]{2,1,0:T(8,128)(2,1)S(1)}, u32[]{:S(2)}, u32[]{:S(2)}) collective-permute-start(bf16[20,64,128]{2,1,0:T(8,128)(2,1)S(1)} %get-tuple-element.50), channel_id=1, source_target_pairs={{0,2},{1,3},{2,0},{3,1},{4,6},{5,7},{6,4},{7,5},{8,10},{9,11},{10,... | collective-permute-start | bytes 983048 | tf_op jit(solution)/shard_map/ppermute | solution.py:491
  113.3 44.4 %collective-permute-start.7 = (bf16[6,128,128]{2,1,0:T(8,128)(2,1)S(1)}, bf16[6,128,128]{2,1,0:T(8,128)(2,1)S(1)}, u32[]{:S(2)}, u32[]{:S(2)}) collective-permute-start(bf16[6,128,128]{2,1,0:T(8,128)(2,1)S(1)} %get-tuple-element.62), channel_id=1, source_target_pairs={{0,1},{1,0},{2,3},{3,2},{4,5},{5,4},{6,7},{7,6},{8,9},{9,8},{10,11... | collective-permute-start | bytes 589832 | tf_op jit(solution)/shard_map/ppermute | solution.py:491
  123.4 34.3 %collective-permute-start.8 = (bf16[6,128,128]{2,1,0:T(8,128)(2,1)S(1)}, bf16[6,128,128]{2,1,0:T(8,128)(2,1)S(1)}, u32[]{:S(2)}, u32[]{:S(2)}) collective-permute-start(bf16[6,128,128]{2,1,0:T(8,128)(2,1)S(1)} %get-tuple-element.63), channel_id=1, source_target_pairs={{1,0},{2,1},{3,2},{4,5},{5,6},{6,7},{9,8},{10,9},{11,10},{12,13},{... | collective-permute-start | bytes 589832 | tf_op jit(solution)/shard_map/ppermute | solution.py:495
  139.0 18.7 %collective-permute-start.9 = (bf16[6,128,128]{2,1,0:T(8,128)(2,1)S(1)}, bf16[6,128,128]{2,1,0:T(8,128)(2,1)S(1)}, u32[]{:S(2)}, u32[]{:S(2)}) collective-permute-start(bf16[6,128,128]{2,1,0:T(8,128)(2,1)S(1)} %get-tuple-element.64), channel_id=1, source_target_pairs={{1,0},{2,1},{3,2},{4,5},{5,6},{6,7},{9,8},{10,9},{11,10},{12,13},{... | collective-permute-start | bytes 589832 | tf_op jit(solution)/shard_map/ppermute | solution.py:495
  140.3 8.7 %collective-permute-start.6 = (bf16[4,128,128]{2,1,0:T(8,128)(2,1)S(1)}, bf16[4,128,128]{2,1,0:T(8,128)(2,1)S(1)}, u32[]{:S(2)}, u32[]{:S(2)}) collective-permute-start(bf16[4,128,128]{2,1,0:T(8,128)(2,1)S(1)} %get-tuple-element.52), channel_id=1, source_target_pairs={{4,0},{8,4},{12,8},{16,12},{20,16},{24,20},{28,24},{5,1},{9,5},{13... | collective-permute-start | bytes 393224 | tf_op jit(solution)/shard_map/ppermute | solution.py:486

commit v5 on v4

--- a/solution.py
+++ b/solution.py
@@ -530,11 +530,11 @@
             there.append(beside(send))
 
         x0 = after(x0, weights)
-        for d, x in ((0, x0), (1, x1), (3, x3)):
+        for d, x in ((0, x0), (3, x3), (1, x1)):
             if names:
                 x = after(x, g)
-            if d == 3:
-                meet([x0, x1, x], (2, 1, 3))
+            if d == 1:
+                meet([x0, x3, x], (1, 2, 3))
             cfg = dict(base, count=count, d=d, old=list(names))
             kept, g = phase(cfg, order, velocity, w, [x], old, None, g)
             names, old = [*names, d], [*old, (x, kept)]
@@ -547,7 +547,7 @@
         (g,) = phase(part, order, velocity, w, [front, back], old, kept, g)
         met = [list(v) for v in zip(*met)]
         g = border(
-            eps, [[0, 1, 3], [2]], [[0], [1], [2], [3]], order, velocity, weights, g,
+            eps, [[0, 3, 1], [2]], [[0], [1], [2], [3]], order, velocity, weights, g,
             *met, there, space, n,
         )
         tiles = g

time: 181 us -> 180 us (level)
  starting transfers between devices: 50.3 us -> 28.2 us
  waiting for transfers between devices: 51.3 us -> 72 us
    ppermute x5, waiting for transfers between devices: 50.4 us -> 70.9 us  [swap(): return lax.ppermute(part, 'mode', [(i, i ^ d) for i in range(n)])]
    ppermute x5, starting transfers between devices: 33.2 us -> 13.7 us  [swap(): return lax.ppermute(part, 'mode', [(i, i ^ d) for i in range(n)])]
    ppermute x3, starting transfers between devices: 12.4 us -> 9.82 us  [local(): above = lambda v: lax.ppermute(v, 'space', ahead)]
where the time goes in v5:
time: 180 us; the launch traced here: 179 us
  waiting for transfers between devices  72 us (40%)
  Pallas kernels  51.6 us (29%)
  starting transfers between devices  28.2 us (16%)
  blocking collectives  19.9 us (11%)
  local copies, waits for them, and re-layouts  5.93 us (3%)
    ppermute x5, waiting for transfers between devices, swap(): return lax.ppermute(part, 'mode', [(i, i ^ d) for i in range(n)])  70.9 us
    pallas_call x5, Pallas kernels, phase(): pl.pallas_call(functools.partial(phase_kernel, cfg), in_specs=[smem, smem...  38.2 us
    all_to_all x1, blocking collectives, local(): lax.all_to_all(tiles, ('space', 'mode'), split_axis=0, concat_axis=0, til...  19.9 us
    ppermute x5, starting transfers between devices, swap(): return lax.ppermute(part, 'mode', [(i, i ^ d) for i in range(n)])  13.7 us
    ppermute x3, starting transfers between devices, local(): above = lambda v: lax.ppermute(v, 'space', ahead)  9.82 us
    ppermute x2, starting transfers between devices, local(): beside = lambda v: lax.ppermute(v, ('space', 'mode'), relay)  4.67 us
    pallas_call x1, Pallas kernels, first_pack(): pl.pallas_call(functools.partial(first_kernel, owners, rows, tiles), in_s...  3.96 us
    pallas_call x2, Pallas kernels, lines_of(): pl.pallas_call(functools.partial(line_kernel, rows, tiles, choice), in_sp...  3.79 us
  transfers between devices with their start and end apart: 10, of which 4 were waited for; matrix products, arithmetic and copies ran while one was open for 1% of the time, Pallas kernels for 25%

profile of v5, /device:TPU:1, one launch (start us, length us, event | category | flops | bytes accessed | tf_op | source)
XLA Modules:
  0.0 179.2 jit_solution(2148216910781673903)
XLA Ops:
  0.0 0.6 pad_add_fusion.order.refs_0_
  0.6 0.0 copy-start.1
  0.6 4.0 %shard_map.37 = (bf16[48,128,128]{2,1,0:T(8,128)(2,1)}, bf16[48,128,128]{2,1,0:T(8,128)(2,1)}) custom-call(s32[3]{0:T(128)} %pad_add_fusion.order.refs_0_, bf16[12,128,2048]{2,1,0:T(8,128)(2,1)} %bitcast.8), custom_call_target="tpu_custom_call" | custom-call | tf_op jit(solution)/shard_map/pallas_call | solution.py:434
  4.6 4.2 %collective-permute-start.3 = (bf16[48,128,128]{2,1,0:T(8,128)(2,1)}, bf16[48,128,128]{2,1,0:T(8,128)(2,1)S(1)}, u32[]{:S(2)}, u32[]{:S(2)}) collective-permute-start(bf16[48,128,128]{2,1,0:T(8,128)(2,1)} %get-tuple-element.35), channel_id=1, source_target_pairs={{0,3},{1,2},{2,1},{3,0},{4,7},{5,6},{6,5},{7,4},{8,11},{9,10},{10,... | collective-permute-start | bytes 4718600 | tf_op jit(solution)/shard_map/ppermute | solution.py:491
  8.8 0.0 collective-permute-start.2
  8.8 0.0 copy-done.1
  8.8 0.0 copy-start
  8.8 2.8 %copy-done = bf16[128,12,2048]{2,0,1:T(8,128)(2,1)S(1)} copy-done((bf16[128,12,2048]{2,0,1:T(8,128)(2,1)S(1)}, bf16[128,12,2048]{2,0,1:T(8,128)(2,1)}, u32[]{:S(2)}) %copy-start) | copy-done | bytes 6291480
  11.6 0.0 copy-start.4
  11.6 0.0 copy-start.2
  11.6 2.3 %shard_map.38 = (bf16[48,128,128]{2,1,0:T(8,128)(2,1)S(1)}, bf16[76,64,128]{2,1,0:T(8,128)(2,1)}, bf16[20,64,128]{2,1,0:T(8,128)(2,1)S(1)}) custom-call(s32[3]{0:T(128)S(1)} %copy-done.1, bf16[12,128,2048]{2,1,0:T(8,128)(2,1)S(1)} %bitcast.9), custom_call_target="tpu_custom_call" | custom-call | tf_op jit(solution)/shard_map/pallas_call | solution.py:399
  13.9 0.4 collective-permute-start.1
  14.3 0.0 copy-done.4
  14.3 0.0 copy-start.3
  14.4 0.6 copy-done.3
  15.0 3.1 %collective-permute-start = (f32[1,2048]{1,0:T(1,128)S(1)}, f32[1,2048]{1,0:T(1,128)}, u32[]{:S(2)}, u32[]{:S(2)}) collective-permute-start(f32[1,2048]{1,0:T(1,128)S(1)} %get-tuple-element.65), channel_id=1, source_target_pairs={{4,0},{8,4},{12,8},{16,12},{20,16},{24,20},{28,24},{5,1},{9,5},{13... | collective-permute-start | bytes 24584 | tf_op jit(solution)/shard_map/ppermute | solution.py:486
  18.2 0.9 constant_dynamic-slice_fusion.1
  19.0 0.8 constant_dynamic-slice_fusion
  19.8 0.1 reshape.12.wn
  19.9 0.1 reshape.13.wh
  20.0 1.0 collective-permute-done
  21.0 0.7 dynamic-slice_bitcast_fusion.wx
  21.7 0.0 copy-done.2
  21.7 0.0 slice-start
  21.7 7.3 %shard_map.39 = (bf16[48,128,128]{2,1,0:T(8,128)(2,1)S(1)}, f32[512,512]{1,0:T(8,128)S(1)}) custom-call(s32[3]{0:T(128)S(1)} %copy-done.1, f32[3]{0:T(128)S(1)} %copy-done.2, f32[12,1,512]{2,1,0:T(1,128)S(1)} %broadcast_in_dim.18.refs_2_, bf16[48,128,128]{2,1,0:T(8,128)(2,1)S(1)} %get-tuple-element.40.refs_3_.refs_4_.refs_0_.refs_1_.refs_5_), custom_call_target="tpu_custom_call" | custom-call | flops 1 | bytes 1 | tf_op jit(solution)/shard_map/pallas_call | solution.py:158
  29.0 14.2 %collective-permute-done.3.refs_3_.refs_6_.refs_1_.refs_7_ = bf16[48,128,128]{2,1,0:T(8,128)(2,1)S(1)} collective-permute-done((bf16[48,128,128]{2,1,0:T(8,128)(2,1)}, bf16[48,128,128]{2,1,0:T(8,128)(2,1)S(1)}, u32[]{:S(2)}, u32[]{:S(2)}) %collective-permute-start.3) | collective-permute-done | bytes 1572896 | tf_op jit(solution)/shard_map/ppermute | solution.py:491
  43.2 0.0 slice-start.1
  43.2 8.3 %shard_map.40 = (bf16[48,128,128]{2,1,0:T(8,128)(2,1)S(1)}, f32[512,512]{1,0:T(8,128)S(1)}) custom-call(s32[3]{0:T(128)S(1)} %copy-done.1, f32[3]{0:T(128)S(1)} %copy-done.2, f32[12,1,512]{2,1,0:T(1,128)S(1)} %broadcast_in_dim.18.refs_2_, bf16[48,128,128]{2,1,0:T(8,128)(2,1)S(1)} %collective-permute-done.3.refs_3_.refs_6_.refs_1_.refs_7_, ...), custom_call_target="tpu_custom_call" | custom-call | flops 1 | bytes 1 | tf_op jit(solution)/shard_map/pallas_call | solution.py:158
  51.5 27.3 %collective-permute-done.2.refs_3_.refs_2_.refs_9_ = bf16[48,128,128]{2,1,0:T(8,128)(2,1)} collective-permute-done((bf16[48,128,128]{2,1,0:T(8,128)(2,1)}, bf16[48,128,128]{2,1,0:T(8,128)(2,1)}, u32[]{:S(2)}, u32[]{:S(2)}) %collective-permute-start.2) | collective-permute-done | bytes 1572896 | tf_op jit(solution)/shard_map/ppermute | solution.py:491
  78.8 2.1 %shard_map.42 = (bf16[6,128,128]{2,1,0:T(8,128)(2,1)S(1)}, bf16[6,384,128]{2,1,0:T(8,128)(2,1)S(1)}, bf16[4,384,128]{2,1,0:T(8,128)(2,1)S(1)}, bf16[4,384,128]{2,1,0:T(8,128)(2,1)S(1)}) custom-call(s32[3]{0:T(128)S(1)} %copy-done.1, bf16[48,128,128]{2,1,0:T(8,128)(2,1)S(1)} %get-tuple-element.40.refs_3_.refs_4_.refs_0_.refs_1_.refs_5_, ...), custom_call_target="tpu_custom_call" | custom-call | flops 1 | bytes 1 | tf_op jit(solution)/shard_map/pallas_call | solution.py:227
  80.9 2.5 %collective-permute-start.4 = (bf16[4,384,128]{2,1,0:T(8,128)(2,1)S(1)}, bf16[4,384,128]{2,1,0:T(8,128)(2,1)S(1)}, u32[]{:S(2)}, u32[]{:S(2)}) collective-permute-start(bf16[4,384,128]{2,1,0:T(8,128)(2,1)S(1)} %get-tuple-element.48), channel_id=1, source_target_pairs={{4,0},{8,4},{12,8},{16,12},{20,16},{24,20},{28,24},{5,1},{9,5},{13... | collective-permute-start | bytes 1179656 | tf_op jit(solution)/shard_map/ppermute | solution.py:486
  83.3 9.0 %collective-permute-start.5 = (bf16[20,64,128]{2,1,0:T(8,128)(2,1)S(1)}, bf16[20,64,128]{2,1,0:T(8,128)(2,1)S(1)}, u32[]{:S(2)}, u32[]{:S(2)}) collective-permute-start(bf16[20,64,128]{2,1,0:T(8,128)(2,1)S(1)} %get-tuple-element.50), channel_id=1, source_target_pairs={{0,2},{1,3},{2,0},{3,1},{4,6},{5,7},{6,4},{7,5},{8,10},{9,11},{10,... | collective-permute-start | bytes 983048 | tf_op jit(solution)/shard_map/ppermute | solution.py:491
  92.3 0.0 slice-done
  92.3 0.0 slice-done.1
  92.3 1.1 shard_map.46
  93.5 0.1 collective-permute-start.7
  93.6 9.9 %shard_map.41 = (bf16[48,128,128]{2,1,0:T(8,128)(2,1)S(1)}, f32[512,512]{1,0:T(8,128)S(1)}) custom-call(s32[3]{0:T(128)S(1)} %copy-done.1, f32[3]{0:T(128)S(1)} %copy-done.2, f32[12,1,512]{2,1,0:T(1,128)S(1)} %broadcast_in_dim.18.refs_2_, bf16[48,128,128]{2,1,0:T(8,128)(2,1)} %collective-permute-done.2.refs_3_.refs_2_.refs_9_, ...), custom_call_target="tpu_custom_call" | custom-call | flops 1 | bytes 1 | tf_op jit(solution)/shard_map/pallas_call | solution.py:158
  103.5 3.4 %collective-permute-start.8 = (bf16[6,128,128]{2,1,0:T(8,128)(2,1)S(1)}, bf16[6,128,128]{2,1,0:T(8,128)(2,1)S(1)}, u32[]{:S(2)}, u32[]{:S(2)}) collective-permute-start(bf16[6,128,128]{2,1,0:T(8,128)(2,1)S(1)} %get-tuple-element.63), channel_id=1, source_target_pairs={{1,0},{2,1},{3,2},{4,5},{5,6},{6,7},{9,8},{10,9},{11,10},{12,13},{... | collective-permute-start | bytes 589832 | tf_op jit(solution)/shard_map/ppermute | solution.py:495
  106.9 29.5 %collective-permute-done.1.refs_3_.refs_0_ = bf16[76,64,128]{2,1,0:T(8,128)(2,1)} collective-permute-done((bf16[76,64,128]{2,1,0:T(8,128)(2,1)}, bf16[76,64,128]{2,1,0:T(8,128)(2,1)}, u32[]{:S(2)}, u32[]{:S(2)}) %collective-permute-start.1) | collective-permute-done | bytes 1245216 | tf_op jit(solution)/shard_map/ppermute | solution.py:491
  136.4 0.0 collective-permute-done.4.refs_4_
  136.4 1.7 shard_map.44
  138.0 1.3 collective-permute-start.9
  139.3 4.2 %collective-permute-start.6 = (bf16[4,128,128]{2,1,0:T(8,128)(2,1)S(1)}, bf16[4,128,128]{2,1,0:T(8,128)(2,1)S(1)}, u32[]{:S(2)}, u32[]{:S(2)}) collective-permute-start(bf16[4,128,128]{2,1,0:T(8,128)(2,1)S(1)} %get-tuple-element.52), channel_id=1, source_target_pairs={{4,0},{8,4},{12,8},{16,12},{20,16},{24,20},{28,24},{5,1},{9,5},{13... | collective-permute-start | bytes 393224 | tf_op jit(solution)/shard_map/ppermute | solution.py:486
  143.6 4.1 %shard_map.43 = (bf16[48,64,128]{2,1,0:T(8,128)(2,1)S(1)}, bf16[48,64,128]{2,1,0:T(8,128)(2,1)S(1)}) custom-call(s32[3]{0:T(128)S(1)} %copy-done.1, f32[3]{0:T(128)S(1)} %copy-done.2, f32[12,1,512]{2,1,0:T(1,128)S(1)} %broadcast_in_dim.18.refs_2_, bf16[76,64,128]{2,1,0:T(8,128)(2,1)} %collective-permute-done.1.refs_3_.refs_0_), custom_call_target="tpu_custom_call" | custom-call | flops 1 | bytes 1 | tf_op jit(solution)/shard_map/pallas_call | solution.py:158
  147.6 0.0 collective-permute-done.5.refs_4_
  147.6 0.0 collective-permute-done.6.refs_5_
  147.7 8.6 %shard_map.45.gin = f32[512,512]{1,0:T(8,128)S(1)} custom-call(s32[3]{0:T(128)S(1)} %copy-done.1, f32[3]{0:T(128)S(1)} %copy-done.2, f32[12,1,512]{2,1,0:T(1,128)S(1)} %broadcast_in_dim.18.refs_2_, bf16[76,64,128]{2,1,0:T(8,128)(2,1)} %collective-permute-done.1.refs_3_.refs_0_, bf16[20,64,128]{2,1,0:T(8,128)(2,1)S(1)} %collective-permute-done.5.refs_4_, ...), custom_call_target="tpu_custom_call" | custom-call | flops 1 | bytes 1 | tf_op jit(solution)/shard_map/pallas_call | solution.py:158
  156.3 0.0 collective-permute-done.7.refs_7_
  156.3 0.0 collective-permute-done.8.refs_8_
  156.3 0.0 collective-permute-done.9.refs_9_
  156.3 2.3 %shard_map.47 = bf16[32,64,128]{2,1,0:T(8,128)(2,1)S(1)} custom-call(s32[3]{0:T(128)S(1)} %copy-done.1, f32[3]{0:T(128)S(1)} %copy-done.2, f32[6,1,128]{2,1,0:T(1,128)S(1)} %reshape.12.wn, f32[6,1,128]{2,1,0:T(1,128)S(1)} %reshape.13.wh, f32[4,1,128]{2,1,0:T(1,128)S(1)} %dynamic-slice_bitcast_fusion.1.wr, f32[4,1,128]{2,1,0:T(1,128)S(1)} %dynamic-slice_bitcast_fusion.wx, ...), custom_call_target="tpu_custom_call" | custom-call | flops 1 | bytes 1 | tf_op jit(solution)/shard_map/pallas_call | solution.py:339
  158.6 19.9 %all_to_all.5 = bf16[32,64,128]{2,1,0:T(8,128)(2,1)S(1)} all-to-all(bf16[32,64,128]{2,1,0:T(8,128)(2,1)S(1)} %shard_map.47), channel_id=1, replica_groups=mesh['space'=8,'mode'=4] {'space','mode'}, dimensions={0} | all-to-all | bytes 1048576 | tf_op jit(solution)/shard_map/all_to_all | solution.py:554
  178.4 0.1 convert_reduce_fusion
  178.5 0.6 broadcast_multiply_fusion
  (5 shorter events, 0.1 us)
Async XLA Ops:
  0.6 8.2 %copy-start.1 = (s32[3]{0:T(128)S(1)}, s32[3]{0:T(128)}, u32[]{:S(2)}) copy-start(s32[3]{0:T(128)} %pad_add_fusion.order.refs_0_) | copy-start | bytes 40
  4.6 38.6 %collective-permute-start.3 = (bf16[48,128,128]{2,1,0:T(8,128)(2,1)}, bf16[48,128,128]{2,1,0:T(8,128)(2,1)S(1)}, u32[]{:S(2)}, u32[]{:S(2)}) collective-permute-start(bf16[48,128,128]{2,1,0:T(8,128)(2,1)} %get-tuple-element.35), channel_id=1, source_target_pairs={{0,3},{1,2},{2,1},{3,0},{4,7},{5,6},{6,5},{7,4},{8,11},{9,10},{10,... | collective-permute-start | bytes 4718600 | tf_op jit(solution)/shard_map/ppermute | solution.py:491
  8.8 69.9 %collective-permute-start.2 = (bf16[48,128,128]{2,1,0:T(8,128)(2,1)}, bf16[48,128,128]{2,1,0:T(8,128)(2,1)}, u32[]{:S(2)}, u32[]{:S(2)}) collective-permute-start(bf16[48,128,128]{2,1,0:T(8,128)(2,1)} %get-tuple-element.38), channel_id=1, source_target_pairs={{0,1},{1,0},{2,3},{3,2},{4,5},{5,4},{6,7},{7,6},{8,9},{9,8},{10,11... | collective-permute-start | bytes 4718600 | tf_op jit(solution)/shard_map/ppermute | solution.py:491
  8.8 2.8 %copy-start = (bf16[128,12,2048]{2,0,1:T(8,128)(2,1)S(1)}, bf16[128,12,2048]{2,0,1:T(8,128)(2,1)}, u32[]{:S(2)}) copy-start(bf16[128,12,2048]{2,0,1:T(8,128)(2,1)} %param.3) | copy-start | bytes 18874372
  11.6 2.7 %copy-start.4 = (s32[12,2048]{1,0:T(8,128)S(1)}, s32[12,2048]{1,0:T(8,128)}, u32[]{:S(2)}) copy-start(s32[12,2048]{1,0:T(8,128)} %param.4) | copy-start | bytes 294916
  11.6 10.1 %copy-start.2 = (f32[3]{0:T(128)S(1)}, f32[3]{0:T(128)}, u32[]{:S(2)}) copy-start(f32[3]{0:T(128)} %velocity.1) | copy-start | bytes 40
  13.9 122.5 %collective-permute-start.1 = (bf16[76,64,128]{2,1,0:T(8,128)(2,1)}, bf16[76,64,128]{2,1,0:T(8,128)(2,1)}, u32[]{:S(2)}, u32[]{:S(2)}) collective-permute-start(bf16[76,64,128]{2,1,0:T(8,128)(2,1)} %get-tuple-element.37), channel_id=1, source_target_pairs={{0,2},{1,3},{2,0},{3,1},{4,6},{5,7},{6,4},{7,5},{8,10},{9,11},{10,... | collective-permute-start | bytes 3735560 | tf_op jit(solution)/shard_map/ppermute | solution.py:491
  14.3 0.7 copy-start.3
  15.0 6.0 %collective-permute-start = (f32[1,2048]{1,0:T(1,128)S(1)}, f32[1,2048]{1,0:T(1,128)}, u32[]{:S(2)}, u32[]{:S(2)}) collective-permute-start(f32[1,2048]{1,0:T(1,128)S(1)} %get-tuple-element.65), channel_id=1, source_target_pairs={{4,0},{8,4},{12,8},{16,12},{20,16},{24,20},{28,24},{5,1},{9,5},{13... | collective-permute-start | bytes 24584 | tf_op jit(solution)/shard_map/ppermute | solution.py:486
  21.7 70.6 %slice-start = ((s8[6291456]{0:T(1024)(128)(4,1)}), s8[4194304]{0:T(1024)(128)(4,1)S(1)}, s32[]{:S(2)}) async-start(s8[6291456]{0:T(1024)(128)(4,1)} %bitcast.10), calls=%async_computation.1 | async-start | bytes 8388608
  43.2 49.1 %slice-start.1 = ((s8[6291456]{0:T(1024)(128)(4,1)}), s8[2097152]{0:T(1024)(128)(4,1)S(1)}, s32[]{:S(2)}) async-start(s8[6291456]{0:T(1024)(128)(4,1)} %bitcast.10), calls=%async_computation.2 | async-start | bytes 4194304
  80.9 55.5 %collective-permute-start.4 = (bf16[4,384,128]{2,1,0:T(8,128)(2,1)S(1)}, bf16[4,384,128]{2,1,0:T(8,128)(2,1)S(1)}, u32[]{:S(2)}, u32[]{:S(2)}) collective-permute-start(bf16[4,384,128]{2,1,0:T(8,128)(2,1)S(1)} %get-tuple-element.48), channel_id=1, source_target_pairs={{4,0},{8,4},{12,8},{16,12},{20,16},{24,20},{28,24},{5,1},{9,5},{13... | collective-permute-start | bytes 1179656 | tf_op jit(solution)/shard_map/ppermute | solution.py:486
  83.3 64.3 %collective-permute-start.5 = (bf16[20,64,128]{2,1,0:T(8,128)(2,1)S(1)}, bf16[20,64,128]{2,1,0:T(8,128)(2,1)S(1)}, u32[]{:S(2)}, u32[]{:S(2)}) collective-permute-start(bf16[20,64,128]{2,1,0:T(8,128)(2,1)S(1)} %get-tuple-element.50), channel_id=1, source_target_pairs={{0,2},{1,3},{2,0},{3,1},{4,6},{5,7},{6,4},{7,5},{8,10},{9,11},{10,... | collective-permute-start | bytes 983048 | tf_op jit(solution)/shard_map/ppermute | solution.py:491
  93.5 62.8 %collective-permute-start.7 = (bf16[6,128,128]{2,1,0:T(8,128)(2,1)S(1)}, bf16[6,128,128]{2,1,0:T(8,128)(2,1)S(1)}, u32[]{:S(2)}, u32[]{:S(2)}) collective-permute-start(bf16[6,128,128]{2,1,0:T(8,128)(2,1)S(1)} %get-tuple-element.62), channel_id=1, source_target_pairs={{0,1},{1,0},{2,3},{3,2},{4,5},{5,4},{6,7},{7,6},{8,9},{9,8},{10,11... | collective-permute-start | bytes 589832 | tf_op jit(solution)/shard_map/ppermute | solution.py:491
  103.5 52.8 %collective-permute-start.8 = (bf16[6,128,128]{2,1,0:T(8,128)(2,1)S(1)}, bf16[6,128,128]{2,1,0:T(8,128)(2,1)S(1)}, u32[]{:S(2)}, u32[]{:S(2)}) collective-permute-start(bf16[6,128,128]{2,1,0:T(8,128)(2,1)S(1)} %get-tuple-element.63), channel_id=1, source_target_pairs={{1,0},{2,1},{3,2},{4,5},{5,6},{6,7},{9,8},{10,9},{11,10},{12,13},{... | collective-permute-start | bytes 589832 | tf_op jit(solution)/shard_map/ppermute | solution.py:495
  138.0 18.3 %collective-permute-start.9 = (bf16[6,128,128]{2,1,0:T(8,128)(2,1)S(1)}, bf16[6,128,128]{2,1,0:T(8,128)(2,1)S(1)}, u32[]{:S(2)}, u32[]{:S(2)}) collective-permute-start(bf16[6,128,128]{2,1,0:T(8,128)(2,1)S(1)} %get-tuple-element.64), channel_id=1, source_target_pairs={{1,0},{2,1},{3,2},{4,5},{5,6},{6,7},{9,8},{10,9},{11,10},{12,13},{... | collective-permute-start | bytes 589832 | tf_op jit(solution)/shard_map/ppermute | solution.py:495
  139.3 8.3 %collective-permute-start.6 = (bf16[4,128,128]{2,1,0:T(8,128)(2,1)S(1)}, bf16[4,128,128]{2,1,0:T(8,128)(2,1)S(1)}, u32[]{:S(2)}, u32[]{:S(2)}) collective-permute-start(bf16[4,128,128]{2,1,0:T(8,128)(2,1)S(1)} %get-tuple-element.52), channel_id=1, source_target_pairs={{4,0},{8,4},{12,8},{16,12},{20,16},{24,20},{28,24},{5,1},{9,5},{13... | collective-permute-start | bytes 393224 | tf_op jit(solution)/shard_map/ppermute | solution.py:486

commit v6 on v5

--- a/solution.py
+++ b/solution.py
@@ -53,7 +53,7 @@
                 a[t * rows + 2 * i + r, target, :] = value.astype(BF)
         return carry
 
-    lax.fori_loop(0, count // SUB, body, 0)
+    lax.fori_loop(0, count // SUB, body, 0, unroll=4)
 
 
 def phase_kernel(cfg, *refs):

time: 180 us -> 177 us (0.983)
  waiting for transfers between devices: 72 us -> 83.1 us
  Pallas kernels: 51.6 us -> 41.5 us
  starting transfers between devices: 28.2 us -> 25.7 us
    pallas_call x5, Pallas kernels: 38.2 us -> 28.1 us  [phase(): pl.pallas_call(functools.partial(phase_kernel, cfg), in_specs=[smem, smem...]
    ppermute x5, waiting for transfers between devices: 70.9 us -> 80.9 us  [swap(): return lax.ppermute(part, 'mode', [(i, i ^ d) for i in range(n)])]
    ppermute x5, starting transfers between devices: 13.7 us -> 11.2 us  [swap(): return lax.ppermute(part, 'mode', [(i, i ^ d) for i in range(n)])]
  transfers between devices with their start and end apart: 10 -> 10, of which waited for: 4 -> 5; matrix products, arithmetic and copies ran while one was open for 1% -> 1% of each run, Pallas kernels for 25% -> 20%
where the time goes in v6:
time: 177 us
  waiting for transfers between devices  83.1 us (47%)
  Pallas kernels  41.5 us (23%)
  starting transfers between devices  25.7 us (15%)
  blocking collectives  18.7 us (11%)
  local copies, waits for them, and re-layouts  5.93 us (3%)
    ppermute x5, waiting for transfers between devices, swap(): return lax.ppermute(part, 'mode', [(i, i ^ d) for i in range(n)])  80.9 us
    pallas_call x5, Pallas kernels, phase(): pl.pallas_call(functools.partial(phase_kernel, cfg), in_specs=[smem, smem...  28.1 us
    all_to_all x1, blocking collectives, local(): lax.all_to_all(tiles, ('space', 'mode'), split_axis=0, concat_axis=0, til...  18.7 us
    ppermute x5, starting transfers between devices, swap(): return lax.ppermute(part, 'mode', [(i, i ^ d) for i in range(n)])  11.2 us
    ppermute x3, starting transfers between devices, local(): above = lambda v: lax.ppermute(v, 'space', ahead)  9.82 us
    ppermute x2, starting transfers between devices, local(): beside = lambda v: lax.ppermute(v, ('space', 'mode'), relay)  4.67 us
    pallas_call x1, Pallas kernels, first_pack(): pl.pallas_call(functools.partial(first_kernel, owners, rows, tiles), in_s...  3.96 us
    pallas_call x2, Pallas kernels, lines_of(): pl.pallas_call(functools.partial(line_kernel, rows, tiles, choice), in_sp...  3.79 us
  transfers between devices with their start and end apart: 10, of which 5 were waited for; matrix products, arithmetic and copies ran while one was open for 1% of the time, Pallas kernels for 20%

profile of v6, /device:TPU:1, one launch (start us, length us, event | category | flops | bytes accessed | tf_op | source)
XLA Modules:
  0.0 176.6 jit_solution(17781333461449485039)
XLA Ops:
  0.0 0.6 pad_add_fusion.order.refs_0_
  0.6 0.0 copy-start.1
  0.6 4.0 %shard_map.37 = (bf16[48,128,128]{2,1,0:T(8,128)(2,1)}, bf16[48,128,128]{2,1,0:T(8,128)(2,1)}) custom-call(s32[3]{0:T(128)} %pad_add_fusion.order.refs_0_, bf16[12,128,2048]{2,1,0:T(8,128)(2,1)} %bitcast.8), custom_call_target="tpu_custom_call" | custom-call | tf_op jit(solution)/shard_map/pallas_call | solution.py:434
  4.6 4.2 %collective-permute-start.3 = (bf16[48,128,128]{2,1,0:T(8,128)(2,1)}, bf16[48,128,128]{2,1,0:T(8,128)(2,1)S(1)}, u32[]{:S(2)}, u32[]{:S(2)}) collective-permute-start(bf16[48,128,128]{2,1,0:T(8,128)(2,1)} %get-tuple-element.35), channel_id=1, source_target_pairs={{0,3},{1,2},{2,1},{3,0},{4,7},{5,6},{6,5},{7,4},{8,11},{9,10},{10,... | collective-permute-start | bytes 4718600 | tf_op jit(solution)/shard_map/ppermute | solution.py:491
  8.8 0.0 collective-permute-start.2
  8.8 0.0 copy-done.1
  8.8 0.0 copy-start
  8.8 2.8 %copy-done = bf16[128,12,2048]{2,0,1:T(8,128)(2,1)S(1)} copy-done((bf16[128,12,2048]{2,0,1:T(8,128)(2,1)S(1)}, bf16[128,12,2048]{2,0,1:T(8,128)(2,1)}, u32[]{:S(2)}) %copy-start) | copy-done | bytes 6291480
  11.6 0.0 copy-start.4
  11.6 0.0 copy-start.2
  11.6 2.3 %shard_map.38 = (bf16[48,128,128]{2,1,0:T(8,128)(2,1)S(1)}, bf16[76,64,128]{2,1,0:T(8,128)(2,1)}, bf16[20,64,128]{2,1,0:T(8,128)(2,1)S(1)}) custom-call(s32[3]{0:T(128)S(1)} %copy-done.1, bf16[12,128,2048]{2,1,0:T(8,128)(2,1)S(1)} %bitcast.9), custom_call_target="tpu_custom_call" | custom-call | tf_op jit(solution)/shard_map/pallas_call | solution.py:399
  13.9 0.4 collective-permute-start.1
  14.3 0.0 copy-done.4
  14.3 0.0 copy-start.3
  14.4 0.6 copy-done.3
  15.0 3.1 %collective-permute-start = (f32[1,2048]{1,0:T(1,128)S(1)}, f32[1,2048]{1,0:T(1,128)}, u32[]{:S(2)}, u32[]{:S(2)}) collective-permute-start(f32[1,2048]{1,0:T(1,128)S(1)} %get-tuple-element.65), channel_id=1, source_target_pairs={{4,0},{8,4},{12,8},{16,12},{20,16},{24,20},{28,24},{5,1},{9,5},{13... | collective-permute-start | bytes 24584 | tf_op jit(solution)/shard_map/ppermute | solution.py:486
  18.2 0.9 constant_dynamic-slice_fusion.1
  19.0 0.8 constant_dynamic-slice_fusion
  19.8 0.1 reshape.12.wn
  19.9 0.1 reshape.13.wh
  20.0 1.0 collective-permute-done
  21.0 0.7 dynamic-slice_bitcast_fusion.wx
  21.7 0.0 copy-done.2
  21.7 0.0 slice-start
  21.7 4.8 %shard_map.39 = (bf16[48,128,128]{2,1,0:T(8,128)(2,1)S(1)}, f32[512,512]{1,0:T(8,128)S(1)}) custom-call(s32[3]{0:T(128)S(1)} %copy-done.1, f32[3]{0:T(128)S(1)} %copy-done.2, f32[12,1,512]{2,1,0:T(1,128)S(1)} %broadcast_in_dim.18.refs_2_, bf16[48,128,128]{2,1,0:T(8,128)(2,1)S(1)} %get-tuple-element.40.refs_3_.refs_4_.refs_0_.refs_1_.refs_5_), custom_call_target="tpu_custom_call" | custom-call | flops 1 | bytes 1 | tf_op jit(solution)/shard_map/pallas_call | solution.py:158
  26.5 16.7 %collective-permute-done.3.refs_3_.refs_6_.refs_1_.refs_7_ = bf16[48,128,128]{2,1,0:T(8,128)(2,1)S(1)} collective-permute-done((bf16[48,128,128]{2,1,0:T(8,128)(2,1)}, bf16[48,128,128]{2,1,0:T(8,128)(2,1)S(1)}, u32[]{:S(2)}, u32[]{:S(2)}) %collective-permute-start.3) | collective-permute-done | bytes 1572896 | tf_op jit(solution)/shard_map/ppermute | solution.py:491
  43.2 0.0 slice-start.1
  43.2 5.8 %shard_map.40 = (bf16[48,128,128]{2,1,0:T(8,128)(2,1)S(1)}, f32[512,512]{1,0:T(8,128)S(1)}) custom-call(s32[3]{0:T(128)S(1)} %copy-done.1, f32[3]{0:T(128)S(1)} %copy-done.2, f32[12,1,512]{2,1,0:T(1,128)S(1)} %broadcast_in_dim.18.refs_2_, bf16[48,128,128]{2,1,0:T(8,128)(2,1)S(1)} %collective-permute-done.3.refs_3_.refs_6_.refs_1_.refs_7_, ...), custom_call_target="tpu_custom_call" | custom-call | flops 1 | bytes 1 | tf_op jit(solution)/shard_map/pallas_call | solution.py:158
  49.0 29.7 %collective-permute-done.2.refs_3_.refs_2_.refs_9_ = bf16[48,128,128]{2,1,0:T(8,128)(2,1)} collective-permute-done((bf16[48,128,128]{2,1,0:T(8,128)(2,1)}, bf16[48,128,128]{2,1,0:T(8,128)(2,1)}, u32[]{:S(2)}, u32[]{:S(2)}) %collective-permute-start.2) | collective-permute-done | bytes 1572896 | tf_op jit(solution)/shard_map/ppermute | solution.py:491
  78.8 2.1 %shard_map.42 = (bf16[6,128,128]{2,1,0:T(8,128)(2,1)S(1)}, bf16[6,384,128]{2,1,0:T(8,128)(2,1)S(1)}, bf16[4,384,128]{2,1,0:T(8,128)(2,1)S(1)}, bf16[4,384,128]{2,1,0:T(8,128)(2,1)S(1)}) custom-call(s32[3]{0:T(128)S(1)} %copy-done.1, bf16[48,128,128]{2,1,0:T(8,128)(2,1)S(1)} %get-tuple-element.40.refs_3_.refs_4_.refs_0_.refs_1_.refs_5_, ...), custom_call_target="tpu_custom_call" | custom-call | flops 1 | bytes 1 | tf_op jit(solution)/shard_map/pallas_call | solution.py:227
  80.9 2.5 %collective-permute-start.4 = (bf16[4,384,128]{2,1,0:T(8,128)(2,1)S(1)}, bf16[4,384,128]{2,1,0:T(8,128)(2,1)S(1)}, u32[]{:S(2)}, u32[]{:S(2)}) collective-permute-start(bf16[4,384,128]{2,1,0:T(8,128)(2,1)S(1)} %get-tuple-element.48), channel_id=1, source_target_pairs={{4,0},{8,4},{12,8},{16,12},{20,16},{24,20},{28,24},{5,1},{9,5},{13... | collective-permute-start | bytes 1179656 | tf_op jit(solution)/shard_map/ppermute | solution.py:486
  83.3 6.5 %collective-permute-start.5 = (bf16[20,64,128]{2,1,0:T(8,128)(2,1)S(1)}, bf16[20,64,128]{2,1,0:T(8,128)(2,1)S(1)}, u32[]{:S(2)}, u32[]{:S(2)}) collective-permute-start(bf16[20,64,128]{2,1,0:T(8,128)(2,1)S(1)} %get-tuple-element.50), channel_id=1, source_target_pairs={{0,2},{1,3},{2,0},{3,1},{4,6},{5,7},{6,4},{7,5},{8,10},{9,11},{10,... | collective-permute-start | bytes 983048 | tf_op jit(solution)/shard_map/ppermute | solution.py:491
  89.9 0.0 slice-done
  89.9 0.0 slice-done.1
  89.9 1.1 shard_map.46
  91.0 0.1 collective-permute-start.7
  91.1 7.5 %shard_map.41 = (bf16[48,128,128]{2,1,0:T(8,128)(2,1)S(1)}, f32[512,512]{1,0:T(8,128)S(1)}) custom-call(s32[3]{0:T(128)S(1)} %copy-done.1, f32[3]{0:T(128)S(1)} %copy-done.2, f32[12,1,512]{2,1,0:T(1,128)S(1)} %broadcast_in_dim.18.refs_2_, bf16[48,128,128]{2,1,0:T(8,128)(2,1)} %collective-permute-done.2.refs_3_.refs_2_.refs_9_, ...), custom_call_target="tpu_custom_call" | custom-call | flops 1 | bytes 1 | tf_op jit(solution)/shard_map/pallas_call | solution.py:158
  98.6 3.4 %collective-permute-start.8 = (bf16[6,128,128]{2,1,0:T(8,128)(2,1)S(1)}, bf16[6,128,128]{2,1,0:T(8,128)(2,1)S(1)}, u32[]{:S(2)}, u32[]{:S(2)}) collective-permute-start(bf16[6,128,128]{2,1,0:T(8,128)(2,1)S(1)} %get-tuple-element.63), channel_id=1, source_target_pairs={{1,0},{2,1},{3,2},{4,5},{5,6},{6,7},{9,8},{10,9},{11,10},{12,13},{... | collective-permute-start | bytes 589832 | tf_op jit(solution)/shard_map/ppermute | solution.py:495
  101.9 34.4 %collective-permute-done.1.refs_3_.refs_0_ = bf16[76,64,128]{2,1,0:T(8,128)(2,1)} collective-permute-done((bf16[76,64,128]{2,1,0:T(8,128)(2,1)}, bf16[76,64,128]{2,1,0:T(8,128)(2,1)}, u32[]{:S(2)}, u32[]{:S(2)}) %collective-permute-start.1) | collective-permute-done | bytes 1245216 | tf_op jit(solution)/shard_map/ppermute | solution.py:491
  136.4 0.0 collective-permute-done.4.refs_4_
  136.4 1.7 shard_map.44
  138.0 1.3 collective-permute-start.9
  139.3 4.2 %collective-permute-start.6 = (bf16[4,128,128]{2,1,0:T(8,128)(2,1)S(1)}, bf16[4,128,128]{2,1,0:T(8,128)(2,1)S(1)}, u32[]{:S(2)}, u32[]{:S(2)}) collective-permute-start(bf16[4,128,128]{2,1,0:T(8,128)(2,1)S(1)} %get-tuple-element.52), channel_id=1, source_target_pairs={{4,0},{8,4},{12,8},{16,12},{20,16},{24,20},{28,24},{5,1},{9,5},{13... | collective-permute-start | bytes 393224 | tf_op jit(solution)/shard_map/ppermute | solution.py:486
  143.6 2.8 %shard_map.43 = (bf16[48,64,128]{2,1,0:T(8,128)(2,1)S(1)}, bf16[48,64,128]{2,1,0:T(8,128)(2,1)S(1)}) custom-call(s32[3]{0:T(128)S(1)} %copy-done.1, f32[3]{0:T(128)S(1)} %copy-done.2, f32[12,1,512]{2,1,0:T(1,128)S(1)} %broadcast_in_dim.18.refs_2_, bf16[76,64,128]{2,1,0:T(8,128)(2,1)} %collective-permute-done.1.refs_3_.refs_0_), custom_call_target="tpu_custom_call" | custom-call | flops 1 | bytes 1 | tf_op jit(solution)/shard_map/pallas_call | solution.py:158
  146.3 0.0 collective-permute-done.5.refs_4_
  146.3 1.2 collective-permute-done.6.refs_5_
  147.5 7.3 %shard_map.45.gin = f32[512,512]{1,0:T(8,128)S(1)} custom-call(s32[3]{0:T(128)S(1)} %copy-done.1, f32[3]{0:T(128)S(1)} %copy-done.2, f32[12,1,512]{2,1,0:T(1,128)S(1)} %broadcast_in_dim.18.refs_2_, bf16[76,64,128]{2,1,0:T(8,128)(2,1)} %collective-permute-done.1.refs_3_.refs_0_, bf16[20,64,128]{2,1,0:T(8,128)(2,1)S(1)} %collective-permute-done.5.refs_4_, ...), custom_call_target="tpu_custom_call" | custom-call | flops 1 | bytes 1 | tf_op jit(solution)/shard_map/pallas_call | solution.py:158
  154.8 0.0 collective-permute-done.7.refs_7_
  154.8 0.0 collective-permute-done.8.refs_8_
  154.8 0.0 collective-permute-done.9.refs_9_
  154.9 2.3 %shard_map.47 = bf16[32,64,128]{2,1,0:T(8,128)(2,1)S(1)} custom-call(s32[3]{0:T(128)S(1)} %copy-done.1, f32[3]{0:T(128)S(1)} %copy-done.2, f32[6,1,128]{2,1,0:T(1,128)S(1)} %reshape.12.wn, f32[6,1,128]{2,1,0:T(1,128)S(1)} %reshape.13.wh, f32[4,1,128]{2,1,0:T(1,128)S(1)} %dynamic-slice_bitcast_fusion.1.wr, f32[4,1,128]{2,1,0:T(1,128)S(1)} %dynamic-slice_bitcast_fusion.wx, ...), custom_call_target="tpu_custom_call" | custom-call | flops 1 | bytes 1 | tf_op jit(solution)/shard_map/pallas_call | solution.py:339
  157.1 18.7 %all_to_all.5 = bf16[32,64,128]{2,1,0:T(8,128)(2,1)S(1)} all-to-all(bf16[32,64,128]{2,1,0:T(8,128)(2,1)S(1)} %shard_map.47), channel_id=1, replica_groups=mesh['space'=8,'mode'=4] {'space','mode'}, dimensions={0} | all-to-all | bytes 1048576 | tf_op jit(solution)/shard_map/all_to_all | solution.py:554
  175.9 0.1 convert_reduce_fusion
  175.9 0.6 broadcast_multiply_fusion
  (5 shorter events, 0.1 us)
Async XLA Ops:
  0.6 8.2 %copy-start.1 = (s32[3]{0:T(128)S(1)}, s32[3]{0:T(128)}, u32[]{:S(2)}) copy-start(s32[3]{0:T(128)} %pad_add_fusion.order.refs_0_) | copy-start | bytes 40
  4.6 38.6 %collective-permute-start.3 = (bf16[48,128,128]{2,1,0:T(8,128)(2,1)}, bf16[48,128,128]{2,1,0:T(8,128)(2,1)S(1)}, u32[]{:S(2)}, u32[]{:S(2)}) collective-permute-start(bf16[48,128,128]{2,1,0:T(8,128)(2,1)} %get-tuple-element.35), channel_id=1, source_target_pairs={{0,3},{1,2},{2,1},{3,0},{4,7},{5,6},{6,5},{7,4},{8,11},{9,10},{10,... | collective-permute-start | bytes 4718600 | tf_op jit(solution)/shard_map/ppermute | solution.py:491
  8.8 69.9 %collective-permute-start.2 = (bf16[48,128,128]{2,1,0:T(8,128)(2,1)}, bf16[48,128,128]{2,1,0:T(8,128)(2,1)}, u32[]{:S(2)}, u32[]{:S(2)}) collective-permute-start(bf16[48,128,128]{2,1,0:T(8,128)(2,1)} %get-tuple-element.38), channel_id=1, source_target_pairs={{0,1},{1,0},{2,3},{3,2},{4,5},{5,4},{6,7},{7,6},{8,9},{9,8},{10,11... | collective-permute-start | bytes 4718600 | tf_op jit(solution)/shard_map/ppermute | solution.py:491
  8.8 2.8 %copy-start = (bf16[128,12,2048]{2,0,1:T(8,128)(2,1)S(1)}, bf16[128,12,2048]{2,0,1:T(8,128)(2,1)}, u32[]{:S(2)}) copy-start(bf16[128,12,2048]{2,0,1:T(8,128)(2,1)} %param.3) | copy-start | bytes 18874372
  11.6 2.7 %copy-start.4 = (s32[12,2048]{1,0:T(8,128)S(1)}, s32[12,2048]{1,0:T(8,128)}, u32[]{:S(2)}) copy-start(s32[12,2048]{1,0:T(8,128)} %param.4) | copy-start | bytes 294916
  11.6 10.1 %copy-start.2 = (f32[3]{0:T(128)S(1)}, f32[3]{0:T(128)}, u32[]{:S(2)}) copy-start(f32[3]{0:T(128)} %velocity.1) | copy-start | bytes 40
  13.9 122.5 %collective-permute-start.1 = (bf16[76,64,128]{2,1,0:T(8,128)(2,1)}, bf16[76,64,128]{2,1,0:T(8,128)(2,1)}, u32[]{:S(2)}, u32[]{:S(2)}) collective-permute-start(bf16[76,64,128]{2,1,0:T(8,128)(2,1)} %get-tuple-element.37), channel_id=1, source_target_pairs={{0,2},{1,3},{2,0},{3,1},{4,6},{5,7},{6,4},{7,5},{8,10},{9,11},{10,... | collective-permute-start | bytes 3735560 | tf_op jit(solution)/shard_map/ppermute | solution.py:491
  14.3 0.7 copy-start.3
  15.0 6.0 %collective-permute-start = (f32[1,2048]{1,0:T(1,128)S(1)}, f32[1,2048]{1,0:T(1,128)}, u32[]{:S(2)}, u32[]{:S(2)}) collective-permute-start(f32[1,2048]{1,0:T(1,128)S(1)} %get-tuple-element.65), channel_id=1, source_target_pairs={{4,0},{8,4},{12,8},{16,12},{20,16},{24,20},{28,24},{5,1},{9,5},{13... | collective-permute-start | bytes 24584 | tf_op jit(solution)/shard_map/ppermute | solution.py:486
  21.7 68.2 %slice-start = ((s8[6291456]{0:T(1024)(128)(4,1)}), s8[4194304]{0:T(1024)(128)(4,1)S(1)}, s32[]{:S(2)}) async-start(s8[6291456]{0:T(1024)(128)(4,1)} %bitcast.10), calls=%async_computation.1 | async-start | bytes 8388608
  43.2 46.6 %slice-start.1 = ((s8[6291456]{0:T(1024)(128)(4,1)}), s8[2097152]{0:T(1024)(128)(4,1)S(1)}, s32[]{:S(2)}) async-start(s8[6291456]{0:T(1024)(128)(4,1)} %bitcast.10), calls=%async_computation.2 | async-start | bytes 4194304
  80.9 55.5 %collective-permute-start.4 = (bf16[4,384,128]{2,1,0:T(8,128)(2,1)S(1)}, bf16[4,384,128]{2,1,0:T(8,128)(2,1)S(1)}, u32[]{:S(2)}, u32[]{:S(2)}) collective-permute-start(bf16[4,384,128]{2,1,0:T(8,128)(2,1)S(1)} %get-tuple-element.48), channel_id=1, source_target_pairs={{4,0},{8,4},{12,8},{16,12},{20,16},{24,20},{28,24},{5,1},{9,5},{13... | collective-permute-start | bytes 1179656 | tf_op jit(solution)/shard_map/ppermute | solution.py:486
  83.3 63.0 %collective-permute-start.5 = (bf16[20,64,128]{2,1,0:T(8,128)(2,1)S(1)}, bf16[20,64,128]{2,1,0:T(8,128)(2,1)S(1)}, u32[]{:S(2)}, u32[]{:S(2)}) collective-permute-start(bf16[20,64,128]{2,1,0:T(8,128)(2,1)S(1)} %get-tuple-element.50), channel_id=1, source_target_pairs={{0,2},{1,3},{2,0},{3,1},{4,6},{5,7},{6,4},{7,5},{8,10},{9,11},{10,... | collective-permute-start | bytes 983048 | tf_op jit(solution)/shard_map/ppermute | solution.py:491
  91.0 63.8 %collective-permute-start.7 = (bf16[6,128,128]{2,1,0:T(8,128)(2,1)S(1)}, bf16[6,128,128]{2,1,0:T(8,128)(2,1)S(1)}, u32[]{:S(2)}, u32[]{:S(2)}) collective-permute-start(bf16[6,128,128]{2,1,0:T(8,128)(2,1)S(1)} %get-tuple-element.62), channel_id=1, source_target_pairs={{0,1},{1,0},{2,3},{3,2},{4,5},{5,4},{6,7},{7,6},{8,9},{9,8},{10,11... | collective-permute-start | bytes 589832 | tf_op jit(solution)/shard_map/ppermute | solution.py:491
  98.6 56.3 %collective-permute-start.8 = (bf16[6,128,128]{2,1,0:T(8,128)(2,1)S(1)}, bf16[6,128,128]{2,1,0:T(8,128)(2,1)S(1)}, u32[]{:S(2)}, u32[]{:S(2)}) collective-permute-start(bf16[6,128,128]{2,1,0:T(8,128)(2,1)S(1)} %get-tuple-element.63), channel_id=1, source_target_pairs={{1,0},{2,1},{3,2},{4,5},{5,6},{6,7},{9,8},{10,9},{11,10},{12,13},{... | collective-permute-start | bytes 589832 | tf_op jit(solution)/shard_map/ppermute | solution.py:495
  138.0 16.8 %collective-permute-start.9 = (bf16[6,128,128]{2,1,0:T(8,128)(2,1)S(1)}, bf16[6,128,128]{2,1,0:T(8,128)(2,1)S(1)}, u32[]{:S(2)}, u32[]{:S(2)}) collective-permute-start(bf16[6,128,128]{2,1,0:T(8,128)(2,1)S(1)} %get-tuple-element.64), channel_id=1, source_target_pairs={{1,0},{2,1},{3,2},{4,5},{5,6},{6,7},{9,8},{10,9},{11,10},{12,13},{... | collective-permute-start | bytes 589832 | tf_op jit(solution)/shard_map/ppermute | solution.py:495
  139.3 8.2 %collective-permute-start.6 = (bf16[4,128,128]{2,1,0:T(8,128)(2,1)S(1)}, bf16[4,128,128]{2,1,0:T(8,128)(2,1)S(1)}, u32[]{:S(2)}, u32[]{:S(2)}) collective-permute-start(bf16[4,128,128]{2,1,0:T(8,128)(2,1)S(1)} %get-tuple-element.52), channel_id=1, source_target_pairs={{4,0},{8,4},{12,8},{16,12},{20,16},{24,20},{28,24},{5,1},{9,5},{13... | collective-permute-start | bytes 393224 | tf_op jit(solution)/shard_map/ppermute | solution.py:486

commit v7 on v6

--- a/solution.py
+++ b/solution.py
@@ -12,6 +12,7 @@
 LANES = 128
 SUB = 16
 PACK_VMEM = 16
+PIECES = 3
 BF = jnp.bfloat16
 F32 = jnp.float32
 VMEM = pltpu.VMEM
@@ -360,9 +361,8 @@
                 copies.append((field.at[:, :, cut(t)], outs[k].at[t * rows : (t + 1) * rows]))
                 continue
             inside = slice(1, rows - 1)
-            if t not in (0, tiles - 1):
-                begin = 2 * (2 * tiles + 2 * deep) if kind == "rim" else 0
-                to = slice(begin + (t - 1) * deep, begin + t * deep)
+            if kind == "inner" and t not in (0, tiles - 1):
+                to = slice((t - 1) * deep, t * deep)
                 copies.append((field.at[inside, a:b, cut(t)], outs[k].at[to]))
             if kind == "rim":
                 for c in (0, 1):
@@ -389,11 +389,8 @@
             shapes.append((tiles * rows, count, LANES))
             pieces += tiles
         else:
-            length = (tiles - 2) * deep
-            pieces += tiles - 2
-            if kind == "rim":
-                length += 2 * (2 * tiles + 2 * deep)
-                pieces += 4 * tiles + 4
+            length = (tiles - 2) * deep if kind == "inner" else 2 * (2 * tiles + 2 * deep)
+            pieces += tiles - 2 if kind == "inner" else 4 * tiles + 4
             shapes.append((length, b - a, LANES))
     anywhere = pl.BlockSpec(memory_space=pl.ANY)
     return pl.pallas_call(
@@ -412,17 +409,24 @@
     loads, stores = [], []
     for k, d in enumerate(owners):
         wide = pl.ds(pl.multiple_of((order[0] ^ d) * tiles * LANES, LANES), tiles * LANES)
-        loads.append(pltpu.make_async_copy(field.at[:, :, wide], stage.at[k], into.at[k]))
-        loads[-1].start()
+        for c in range(PIECES):
+            some = slice(c * rows // PIECES, (c + 1) * rows // PIECES)
+            loads.append(
+                pltpu.make_async_copy(
+                    field.at[some, :, wide], stage.at[k, some], into.at[k * PIECES + c]
+                )
+            )
+            loads[-1].start()
     for k in range(count):
-        loads[k].wait()
-        for t in range(tiles):
-            lanes = slice(t * LANES, (t + 1) * LANES)
-            to = outs[k].at[t * rows : (t + 1) * rows]
-            stores.append(
-                pltpu.make_async_copy(stage.at[k, :, :, lanes], to, out_of.at[k * tiles + t])
-            )
-            stores[-1].start()
+        for c in range(PIECES):
+            a, b = c * rows // PIECES, (c + 1) * rows // PIECES
+            loads[k * PIECES + c].wait()
+            for t in range(tiles):
+                lanes = slice(t * LANES, (t + 1) * LANES)
+                to = outs[k].at[t * rows + a : t * rows + b]
+                sem = out_of.at[(k * PIECES + c) * tiles + t]
+                stores.append(pltpu.make_async_copy(stage.at[k, a:b, :, lanes], to, sem))
+                stores[-1].start()
     for c in stores:
         c.wait()
 
@@ -438,8 +442,8 @@
         out_shape=[shape] * len(owners),
         scratch_shapes=[
             VMEM((len(owners), rows, count, tiles * LANES), BF),
-            pltpu.SemaphoreType.DMA((len(owners),)),
-            pltpu.SemaphoreType.DMA((len(owners) * tiles,)),
+            pltpu.SemaphoreType.DMA((len(owners) * PIECES,)),
+            pltpu.SemaphoreType.DMA((len(owners) * PIECES * tiles,)),
         ],
         compiler_params=pltpu.CompilerParams(vmem_limit_bytes=60 << 20),
     )(order, field)
@@ -513,11 +517,12 @@
         tiles = spread_out(total, n, space, q, count)
     else:
         half = count // 2
-        p1, p3 = first_pack((1, 3), tiles, order, field)
-        x1, x3 = swap(p1, 1), swap(p3, 3)
-        jobs = [(0, "full", 0, 0), (2, "rim", 0, half), (2, "inner", half, count)]
-        x0, p2, p2b = pack(jobs, tiles, order, after(field, p3))
-        front, back = swap(p2, 2), swap(p2b, 2)
+        p3, p1 = first_pack((3, 1), tiles, order, field)
+        x3, x1 = swap(p3, 3), swap(p1, 1)
+        jobs = [(0, "full", 0, 0), (2, "rim", 0, half), (2, "inner", 0, half), (2, "inner", half, count)]
+        x0, p2, p2a, p2b = pack(jobs, tiles, order, after(field, p3))
+        rim = swap(p2, 2)
+        front, back = swap(p2a, 2), swap(p2b, 2)
         base = dict(base, whole=count, n_blocks=n)
         names, old, g = [], [], None
 
@@ -538,13 +543,14 @@
             cfg = dict(base, count=count, d=d, old=list(names))
             kept, g = phase(cfg, order, velocity, w, [x], old, None, g)
             names, old = [*names, d], [*old, (x, kept)]
+        rim = after(rim, (g, met[-1][2]))
+        meet([rim, x0], (0, 1, 1))
         front = after(front, (g, met[-1][2]))
-        meet([front, x0], (0, 1, 1))
         part = dict(base, d=2, count=half, old=names, index=0)
-        kept = phase(part, order, velocity, w, [front], [], None, None)
+        kept = phase(part, order, velocity, w, [rim, front], [], None, None)
         back = after(back, (kept[1], met[-1][2]))
         part = dict(part, index=1)
-        (g,) = phase(part, order, velocity, w, [front, back], old, kept, g)
+        (g,) = phase(part, order, velocity, w, [rim, back], old, kept, g)
         met = [list(v) for v in zip(*met)]
         g = border(
             eps, [[0, 3, 1], [2]], [[0], [1], [2], [3]], order, velocity, weights, g,

time: 177 us -> 177 us (level)
    ppermute x5 -> x6, waiting for transfers between devices: 80.9 us -> 76.8 us  [swap(): return lax.ppermute(part, 'mode', [(i, i ^ d) for i in range(n)])]
    ppermute x3, waiting for transfers between devices: 2.22 us -> 5.07 us  [local(): above = lambda v: lax.ppermute(v, 'space', ahead)]
    ppermute x5 -> x6, starting transfers between devices: 11.2 us -> 12.9 us  [swap(): return lax.ppermute(part, 'mode', [(i, i ^ d) for i in range(n)])]
    unnamed x14 -> x18, local copies, waits for them, and re-layouts: 3.45 us -> 4.19 us
  transfers between devices with their start and end apart: 10 -> 11, of which waited for: 5 -> 6; matrix products, arithmetic and copies ran while one was open for 1% -> 1% of each run, Pallas kernels for 20% -> 20%
where the time goes in v7:
time: 177 us; the launch traced here: 176 us
  waiting for transfers between devices  81.9 us (46%)
  Pallas kernels  41 us (23%)
  starting transfers between devices  26.2 us (15%)
  blocking collectives  18.9 us (11%)
  local copies, waits for them, and re-layouts  6.66 us (4%)
    ppermute x6, waiting for transfers between devices, swap(): return lax.ppermute(part, 'mode', [(i, i ^ d) for i in range(n)])  76.8 us
    pallas_call x5, Pallas kernels, phase(): pl.pallas_call(functools.partial(phase_kernel, cfg), in_specs=[smem, smem...  27.9 us
    all_to_all x1, blocking collectives, local(): lax.all_to_all(tiles, ('space', 'mode'), split_axis=0, concat_axis=0, til...  18.9 us
    ppermute x6, starting transfers between devices, swap(): return lax.ppermute(part, 'mode', [(i, i ^ d) for i in range(n)])  12.9 us
    ppermute x3, starting transfers between devices, local(): above = lambda v: lax.ppermute(v, 'space', ahead)  9.92 us
    ppermute x3, waiting for transfers between devices, local(): above = lambda v: lax.ppermute(v, 'space', ahead)  5.07 us
    unnamed x18, local copies, waits for them, and re-layouts  4.19 us
    pallas_call x1, Pallas kernels, first_pack(): pl.pallas_call(functools.partial(first_kernel, owners, rows, tiles), in_s...  3.82 us
  transfers between devices with their start and end apart: 11, of which 6 were waited for; matrix products, arithmetic and copies ran while one was open for 1% of the time, Pallas kernels for 20%

profile of v7, /device:TPU:1, one launch (start us, length us, event | category | flops | bytes accessed | tf_op | source)
XLA Modules:
  0.0 176.3 jit_solution(6166655597985363834)
XLA Ops:
  0.0 0.6 pad_add_fusion.order.refs_0_
  0.6 0.0 copy-start.1
  0.6 3.8 %shard_map.37 = (bf16[48,128,128]{2,1,0:T(8,128)(2,1)}, bf16[48,128,128]{2,1,0:T(8,128)(2,1)}) custom-call(s32[3]{0:T(128)} %pad_add_fusion.order.refs_0_, bf16[12,128,2048]{2,1,0:T(8,128)(2,1)} %bitcast.8), custom_call_target="tpu_custom_call" | custom-call | tf_op jit(solution)/shard_map/pallas_call | solution.py:438
  4.4 4.2 %collective-permute-start.3 = (bf16[48,128,128]{2,1,0:T(8,128)(2,1)}, bf16[48,128,128]{2,1,0:T(8,128)(2,1)S(1)}, u32[]{:S(2)}, u32[]{:S(2)}) collective-permute-start(bf16[48,128,128]{2,1,0:T(8,128)(2,1)} %get-tuple-element.37), channel_id=1, source_target_pairs={{0,3},{1,2},{2,1},{3,0},{4,7},{5,6},{6,5},{7,4},{8,11},{9,10},{10,... | collective-permute-start | bytes 4718600 | tf_op jit(solution)/shard_map/ppermute | solution.py:495
  8.7 0.0 collective-permute-start.2
  8.7 0.0 copy-done.1
  8.7 0.0 copy-start
  8.7 2.8 %copy-done = bf16[128,12,2048]{2,0,1:T(8,128)(2,1)S(1)} copy-done((bf16[128,12,2048]{2,0,1:T(8,128)(2,1)S(1)}, bf16[128,12,2048]{2,0,1:T(8,128)(2,1)}, u32[]{:S(2)}) %copy-start) | copy-done | bytes 6291480
  11.4 0.0 copy-start.6
  11.4 0.0 copy-start.2
  11.5 2.2 %shard_map.38 = (bf16[48,128,128]{2,1,0:T(8,128)(2,1)S(1)}, bf16[56,64,128]{2,1,0:T(8,128)(2,1)}, bf16[20,64,128]{2,1,0:T(8,128)(2,1)S(1)}, bf16[20,64,128]{2,1,0:T(8,128)(2,1)S(1)}) custom-call(s32[3]{0:T(128)S(1)} %copy-done.1, bf16[12,128,2048]{2,1,0:T(8,128)(2,1)S(1)} %bitcast.9), custom_call_target="tpu_custom_call" | custom-call | tf_op jit(solution)/shard_map/pallas_call | solution.py:396
  13.6 0.0 copy-start.3
  13.7 0.7 copy-done.3
  14.4 0.4 collective-permute-start.1
  14.7 0.0 copy-done.6
  14.8 0.0 copy-start.5
  14.8 0.6 copy-done.5
  15.4 3.1 %collective-permute-start = (f32[1,2048]{1,0:T(1,128)S(1)}, f32[1,2048]{1,0:T(1,128)}, u32[]{:S(2)}, u32[]{:S(2)}) collective-permute-start(f32[1,2048]{1,0:T(1,128)S(1)} %get-tuple-element.69), channel_id=1, source_target_pairs={{4,0},{8,4},{12,8},{16,12},{20,16},{24,20},{28,24},{5,1},{9,5},{13... | collective-permute-start | bytes 24584 | tf_op jit(solution)/shard_map/ppermute | solution.py:490
  18.6 0.9 constant_dynamic-slice_fusion.1
  19.5 0.8 constant_dynamic-slice_fusion
  20.2 0.1 reshape.12.wn
  20.3 0.1 reshape.13.wh
  20.4 1.0 collective-permute-done
  21.4 0.7 dynamic-slice_bitcast_fusion.wx
  22.1 0.0 copy-done.2
  22.1 0.0 slice-start
  22.1 4.8 %shard_map.39 = (bf16[48,128,128]{2,1,0:T(8,128)(2,1)S(1)}, f32[512,512]{1,0:T(8,128)S(1)}) custom-call(s32[3]{0:T(128)S(1)} %copy-done.1, f32[3]{0:T(128)S(1)} %copy-done.2, f32[12,1,512]{2,1,0:T(1,128)S(1)} %broadcast_in_dim.18.refs_2_, bf16[48,128,128]{2,1,0:T(8,128)(2,1)S(1)} %get-tuple-element.42.refs_3_.refs_4_.refs_0_.refs_1_.refs_5_), custom_call_target="tpu_custom_call" | custom-call | flops 1 | bytes 1 | tf_op jit(solution)/shard_map/pallas_call | solution.py:159
  26.9 16.1 %collective-permute-done.3.refs_3_.refs_6_.refs_1_.refs_7_ = bf16[48,128,128]{2,1,0:T(8,128)(2,1)S(1)} collective-permute-done((bf16[48,128,128]{2,1,0:T(8,128)(2,1)}, bf16[48,128,128]{2,1,0:T(8,128)(2,1)S(1)}, u32[]{:S(2)}, u32[]{:S(2)}) %collective-permute-start.3) | collective-permute-done | bytes 1572896 | tf_op jit(solution)/shard_map/ppermute | solution.py:495
  43.1 0.0 slice-start.1
  43.1 5.8 %shard_map.40 = (bf16[48,128,128]{2,1,0:T(8,128)(2,1)S(1)}, f32[512,512]{1,0:T(8,128)S(1)}) custom-call(s32[3]{0:T(128)S(1)} %copy-done.1, f32[3]{0:T(128)S(1)} %copy-done.2, f32[12,1,512]{2,1,0:T(1,128)S(1)} %broadcast_in_dim.18.refs_2_, bf16[48,128,128]{2,1,0:T(8,128)(2,1)S(1)} %collective-permute-done.3.refs_3_.refs_6_.refs_1_.refs_7_, ...), custom_call_target="tpu_custom_call" | custom-call | flops 1 | bytes 1 | tf_op jit(solution)/shard_map/pallas_call | solution.py:159
  48.9 29.7 %collective-permute-done.2.refs_3_.refs_2_.refs_9_ = bf16[48,128,128]{2,1,0:T(8,128)(2,1)} collective-permute-done((bf16[48,128,128]{2,1,0:T(8,128)(2,1)}, bf16[48,128,128]{2,1,0:T(8,128)(2,1)}, u32[]{:S(2)}, u32[]{:S(2)}) %collective-permute-start.2) | collective-permute-done | bytes 1572896 | tf_op jit(solution)/shard_map/ppermute | solution.py:495
  78.6 0.0 copy-start.4
  78.6 2.2 %shard_map.42 = (bf16[6,128,128]{2,1,0:T(8,128)(2,1)S(1)}, bf16[6,384,128]{2,1,0:T(8,128)(2,1)S(1)}, bf16[4,384,128]{2,1,0:T(8,128)(2,1)S(1)}, bf16[4,384,128]{2,1,0:T(8,128)(2,1)S(1)}) custom-call(s32[3]{0:T(128)S(1)} %copy-done.1, bf16[48,128,128]{2,1,0:T(8,128)(2,1)S(1)} %get-tuple-element.42.refs_3_.refs_4_.refs_0_.refs_1_.refs_5_, ...), custom_call_target="tpu_custom_call" | custom-call | flops 1 | bytes 1 | tf_op jit(solution)/shard_map/pallas_call | solution.py:228
  80.8 2.5 %collective-permute-start.4 = (bf16[4,384,128]{2,1,0:T(8,128)(2,1)S(1)}, bf16[4,384,128]{2,1,0:T(8,128)(2,1)S(1)}, u32[]{:S(2)}, u32[]{:S(2)}) collective-permute-start(bf16[4,384,128]{2,1,0:T(8,128)(2,1)S(1)} %get-tuple-element.50), channel_id=1, source_target_pairs={{4,0},{8,4},{12,8},{16,12},{20,16},{24,20},{28,24},{5,1},{9,5},{13... | collective-permute-start | bytes 1179656 | tf_op jit(solution)/shard_map/ppermute | solution.py:490
  83.2 0.0 copy-done.4
  83.3 6.5 %collective-permute-start.6 = (bf16[20,64,128]{2,1,0:T(8,128)(2,1)S(1)}, bf16[20,64,128]{2,1,0:T(8,128)(2,1)S(1)}, u32[]{:S(2)}, u32[]{:S(2)}) collective-permute-start(bf16[20,64,128]{2,1,0:T(8,128)(2,1)S(1)} %copy-done.4), channel_id=1, source_target_pairs={{0,2},{1,3},{2,0},{3,1},{4,6},{5,7},{6,4},{7,5},{8,10},{9,11},{10,... | collective-permute-start | bytes 983048 | tf_op jit(solution)/shard_map/ppermute | solution.py:495
  89.8 0.1 collective-permute-start.5
  89.9 0.0 slice-done
  89.9 0.0 slice-done.1
  89.9 1.1 shard_map.46
  91.0 1.7 collective-permute-start.8
  92.7 7.5 %shard_map.41 = (bf16[48,128,128]{2,1,0:T(8,128)(2,1)S(1)}, f32[512,512]{1,0:T(8,128)S(1)}) custom-call(s32[3]{0:T(128)S(1)} %copy-done.1, f32[3]{0:T(128)S(1)} %copy-done.2, f32[12,1,512]{2,1,0:T(1,128)S(1)} %broadcast_in_dim.18.refs_2_, bf16[48,128,128]{2,1,0:T(8,128)(2,1)} %collective-permute-done.2.refs_3_.refs_2_.refs_9_, ...), custom_call_target="tpu_custom_call" | custom-call | flops 1 | bytes 1 | tf_op jit(solution)/shard_map/pallas_call | solution.py:159
  100.2 29.0 %collective-permute-done.1.refs_0_.refs_3_ = bf16[56,64,128]{2,1,0:T(8,128)(2,1)} collective-permute-done((bf16[56,64,128]{2,1,0:T(8,128)(2,1)}, bf16[56,64,128]{2,1,0:T(8,128)(2,1)}, u32[]{:S(2)}, u32[]{:S(2)}) %collective-permute-start.1) | collective-permute-done | bytes 917536 | tf_op jit(solution)/shard_map/ppermute | solution.py:495
  129.2 1.3 collective-permute-start.9
  130.5 0.0 collective-permute-done.4.refs_4_
  130.5 1.6 shard_map.43
  132.1 2.1 %collective-permute-start.10 = (bf16[6,128,128]{2,1,0:T(8,128)(2,1)S(1)}, bf16[6,128,128]{2,1,0:T(8,128)(2,1)S(1)}, u32[]{:S(2)}, u32[]{:S(2)}) collective-permute-start(bf16[6,128,128]{2,1,0:T(8,128)(2,1)S(1)} %get-tuple-element.68), channel_id=1, source_target_pairs={{1,0},{2,1},{3,2},{4,5},{5,6},{6,7},{9,8},{10,9},{11,10},{12,13},{... | collective-permute-start | bytes 589832 | tf_op jit(solution)/shard_map/ppermute | solution.py:499
  134.1 2.0 %collective-permute-done.6.refs_4_ = bf16[20,64,128]{2,1,0:T(8,128)(2,1)S(1)} collective-permute-done((bf16[20,64,128]{2,1,0:T(8,128)(2,1)S(1)}, bf16[20,64,128]{2,1,0:T(8,128)(2,1)S(1)}, u32[]{:S(2)}, u32[]{:S(2)}) %collective-permute-start.6) | collective-permute-done | bytes 327712 | tf_op jit(solution)/shard_map/ppermute | solution.py:495
  136.1 4.3 %collective-permute-start.7 = (bf16[4,128,128]{2,1,0:T(8,128)(2,1)S(1)}, bf16[4,128,128]{2,1,0:T(8,128)(2,1)S(1)}, u32[]{:S(2)}, u32[]{:S(2)}) collective-permute-start(bf16[4,128,128]{2,1,0:T(8,128)(2,1)S(1)} %get-tuple-element.54), channel_id=1, source_target_pairs={{4,0},{8,4},{12,8},{16,12},{20,16},{24,20},{28,24},{5,1},{9,5},{13... | collective-permute-start | bytes 393224 | tf_op jit(solution)/shard_map/ppermute | solution.py:490
  140.4 4.0 %collective-permute-done.7.refs_5_ = bf16[4,128,128]{2,1,0:T(8,128)(2,1)S(1)} collective-permute-done((bf16[4,128,128]{2,1,0:T(8,128)(2,1)S(1)}, bf16[4,128,128]{2,1,0:T(8,128)(2,1)S(1)}, u32[]{:S(2)}, u32[]{:S(2)}) %collective-permute-start.7) | collective-permute-done | bytes 131104 | tf_op jit(solution)/shard_map/ppermute | solution.py:490
  144.5 2.6 %shard_map.44 = (bf16[48,64,128]{2,1,0:T(8,128)(2,1)S(1)}, bf16[48,64,128]{2,1,0:T(8,128)(2,1)S(1)}) custom-call(s32[3]{0:T(128)S(1)} %copy-done.1, f32[3]{0:T(128)S(1)} %copy-done.2, f32[12,1,512]{2,1,0:T(1,128)S(1)} %broadcast_in_dim.18.refs_2_, bf16[56,64,128]{2,1,0:T(8,128)(2,1)} %collective-permute-done.1.refs_0_.refs_3_, ...), custom_call_target="tpu_custom_call" | custom-call | flops 1 | bytes 1 | tf_op jit(solution)/shard_map/pallas_call | solution.py:159
  147.1 0.0 collective-permute-done.5.refs_4_
  147.1 7.2 %shard_map.45.gin = f32[512,512]{1,0:T(8,128)S(1)} custom-call(s32[3]{0:T(128)S(1)} %copy-done.1, f32[3]{0:T(128)S(1)} %copy-done.2, f32[12,1,512]{2,1,0:T(1,128)S(1)} %broadcast_in_dim.18.refs_2_, bf16[56,64,128]{2,1,0:T(8,128)(2,1)} %collective-permute-done.1.refs_0_.refs_3_, bf16[20,64,128]{2,1,0:T(8,128)(2,1)S(1)} %collective-permute-done.5.refs_4_, ...), custom_call_target="tpu_custom_call" | custom-call | flops 1 | bytes 1 | tf_op jit(solution)/shard_map/pallas_call | solution.py:159
  154.3 0.0 collective-permute-done.8.refs_7_
  154.3 0.0 collective-permute-done.9.refs_8_
  154.3 0.0 collective-permute-done.10.refs_9_
  154.4 2.3 %shard_map.47 = bf16[32,64,128]{2,1,0:T(8,128)(2,1)S(1)} custom-call(s32[3]{0:T(128)S(1)} %copy-done.1, f32[3]{0:T(128)S(1)} %copy-done.2, f32[6,1,128]{2,1,0:T(1,128)S(1)} %reshape.12.wn, f32[6,1,128]{2,1,0:T(1,128)S(1)} %reshape.13.wh, f32[4,1,128]{2,1,0:T(1,128)S(1)} %dynamic-slice_bitcast_fusion.1.wr, f32[4,1,128]{2,1,0:T(1,128)S(1)} %dynamic-slice_bitcast_fusion.wx, ...), custom_call_target="tpu_custom_call" | custom-call | flops 1 | bytes 1 | tf_op jit(solution)/shard_map/pallas_call | solution.py:340
  156.6 18.9 %all_to_all.5 = bf16[32,64,128]{2,1,0:T(8,128)(2,1)S(1)} all-to-all(bf16[32,64,128]{2,1,0:T(8,128)(2,1)S(1)} %shard_map.47), channel_id=1, replica_groups=mesh['space'=8,'mode'=4] {'space','mode'}, dimensions={0} | all-to-all | bytes 1048576 | tf_op jit(solution)/shard_map/all_to_all | solution.py:560
  175.6 0.1 convert_reduce_fusion
  175.6 0.6 broadcast_multiply_fusion
  (5 shorter events, 0.1 us)
Async XLA Ops:
  0.6 8.1 %copy-start.1 = (s32[3]{0:T(128)S(1)}, s32[3]{0:T(128)}, u32[]{:S(2)}) copy-start(s32[3]{0:T(128)} %pad_add_fusion.order.refs_0_) | copy-start | bytes 40
  4.4 38.6 %collective-permute-start.3 = (bf16[48,128,128]{2,1,0:T(8,128)(2,1)}, bf16[48,128,128]{2,1,0:T(8,128)(2,1)S(1)}, u32[]{:S(2)}, u32[]{:S(2)}) collective-permute-start(bf16[48,128,128]{2,1,0:T(8,128)(2,1)} %get-tuple-element.37), channel_id=1, source_target_pairs={{0,3},{1,2},{2,1},{3,0},{4,7},{5,6},{6,5},{7,4},{8,11},{9,10},{10,... | collective-permute-start | bytes 4718600 | tf_op jit(solution)/shard_map/ppermute | solution.py:495
  8.7 69.9 %collective-permute-start.2 = (bf16[48,128,128]{2,1,0:T(8,128)(2,1)}, bf16[48,128,128]{2,1,0:T(8,128)(2,1)}, u32[]{:S(2)}, u32[]{:S(2)}) collective-permute-start(bf16[48,128,128]{2,1,0:T(8,128)(2,1)} %get-tuple-element.40), channel_id=1, source_target_pairs={{0,1},{1,0},{2,3},{3,2},{4,5},{5,4},{6,7},{7,6},{8,9},{9,8},{10,11... | collective-permute-start | bytes 4718600 | tf_op jit(solution)/shard_map/ppermute | solution.py:495
  8.7 2.8 %copy-start = (bf16[128,12,2048]{2,0,1:T(8,128)(2,1)S(1)}, bf16[128,12,2048]{2,0,1:T(8,128)(2,1)}, u32[]{:S(2)}) copy-start(bf16[128,12,2048]{2,0,1:T(8,128)(2,1)} %param.3) | copy-start | bytes 18874372
  11.4 3.3 %copy-start.6 = (s32[12,2048]{1,0:T(8,128)S(1)}, s32[12,2048]{1,0:T(8,128)}, u32[]{:S(2)}) copy-start(s32[12,2048]{1,0:T(8,128)} %param.4) | copy-start | bytes 294916
  11.4 10.7 %copy-start.2 = (f32[3]{0:T(128)S(1)}, f32[3]{0:T(128)}, u32[]{:S(2)}) copy-start(f32[3]{0:T(128)} %velocity.1) | copy-start | bytes 40
  13.6 0.7 copy-start.3
  14.4 114.8 %collective-permute-start.1 = (bf16[56,64,128]{2,1,0:T(8,128)(2,1)}, bf16[56,64,128]{2,1,0:T(8,128)(2,1)}, u32[]{:S(2)}, u32[]{:S(2)}) collective-permute-start(bf16[56,64,128]{2,1,0:T(8,128)(2,1)} %get-tuple-element.39), channel_id=1, source_target_pairs={{0,2},{1,3},{2,0},{3,1},{4,6},{5,7},{6,4},{7,5},{8,10},{9,11},{10,... | collective-permute-start | bytes 2752520 | tf_op jit(solution)/shard_map/ppermute | solution.py:495
  14.8 0.7 copy-start.5
  15.4 6.0 %collective-permute-start = (f32[1,2048]{1,0:T(1,128)S(1)}, f32[1,2048]{1,0:T(1,128)}, u32[]{:S(2)}, u32[]{:S(2)}) collective-permute-start(f32[1,2048]{1,0:T(1,128)S(1)} %get-tuple-element.69), channel_id=1, source_target_pairs={{4,0},{8,4},{12,8},{16,12},{20,16},{24,20},{28,24},{5,1},{9,5},{13... | collective-permute-start | bytes 24584 | tf_op jit(solution)/shard_map/ppermute | solution.py:490
  22.1 67.7 %slice-start = ((s8[6291456]{0:T(1024)(128)(4,1)}), s8[4194304]{0:T(1024)(128)(4,1)S(1)}, s32[]{:S(2)}) async-start(s8[6291456]{0:T(1024)(128)(4,1)} %bitcast.10), calls=%async_computation.1 | async-start | bytes 8388608
  43.1 46.8 %slice-start.1 = ((s8[6291456]{0:T(1024)(128)(4,1)}), s8[2097152]{0:T(1024)(128)(4,1)S(1)}, s32[]{:S(2)}) async-start(s8[6291456]{0:T(1024)(128)(4,1)} %bitcast.10), calls=%async_computation.2 | async-start | bytes 4194304
  78.6 4.6 %copy-start.4 = (bf16[20,64,128]{2,1,0:T(8,128)(2,1)S(1)}, bf16[20,64,128]{2,1,0:T(8,128)(2,1)}, u32[]{:S(2)}) copy-start(bf16[20,64,128]{2,1,0:T(8,128)(2,1)} %copy-done.3) | copy-start | bytes 983044
  80.8 49.7 %collective-permute-start.4 = (bf16[4,384,128]{2,1,0:T(8,128)(2,1)S(1)}, bf16[4,384,128]{2,1,0:T(8,128)(2,1)S(1)}, u32[]{:S(2)}, u32[]{:S(2)}) collective-permute-start(bf16[4,384,128]{2,1,0:T(8,128)(2,1)S(1)} %get-tuple-element.50), channel_id=1, source_target_pairs={{4,0},{8,4},{12,8},{16,12},{20,16},{24,20},{28,24},{5,1},{9,5},{13... | collective-permute-start | bytes 1179656 | tf_op jit(solution)/shard_map/ppermute | solution.py:490
  83.3 52.8 %collective-permute-start.6 = (bf16[20,64,128]{2,1,0:T(8,128)(2,1)S(1)}, bf16[20,64,128]{2,1,0:T(8,128)(2,1)S(1)}, u32[]{:S(2)}, u32[]{:S(2)}) collective-permute-start(bf16[20,64,128]{2,1,0:T(8,128)(2,1)S(1)} %copy-done.4), channel_id=1, source_target_pairs={{0,2},{1,3},{2,0},{3,1},{4,6},{5,7},{6,4},{7,5},{8,10},{9,11},{10,... | collective-permute-start | bytes 983048 | tf_op jit(solution)/shard_map/ppermute | solution.py:495
  89.8 57.3 %collective-permute-start.5 = (bf16[20,64,128]{2,1,0:T(8,128)(2,1)S(1)}, bf16[20,64,128]{2,1,0:T(8,128)(2,1)S(1)}, u32[]{:S(2)}, u32[]{:S(2)}) collective-permute-start(bf16[20,64,128]{2,1,0:T(8,128)(2,1)S(1)} %get-tuple-element.52), channel_id=1, source_target_pairs={{0,2},{1,3},{2,0},{3,1},{4,6},{5,7},{6,4},{7,5},{8,10},{9,11},{10,... | collective-permute-start | bytes 983048 | tf_op jit(solution)/shard_map/ppermute | solution.py:495
  91.0 63.3 %collective-permute-start.8 = (bf16[6,128,128]{2,1,0:T(8,128)(2,1)S(1)}, bf16[6,128,128]{2,1,0:T(8,128)(2,1)S(1)}, u32[]{:S(2)}, u32[]{:S(2)}) collective-permute-start(bf16[6,128,128]{2,1,0:T(8,128)(2,1)S(1)} %get-tuple-element.66), channel_id=1, source_target_pairs={{0,1},{1,0},{2,3},{3,2},{4,5},{5,4},{6,7},{7,6},{8,9},{9,8},{10,11... | collective-permute-start | bytes 589832 | tf_op jit(solution)/shard_map/ppermute | solution.py:495
  129.2 25.1 %collective-permute-start.9 = (bf16[6,128,128]{2,1,0:T(8,128)(2,1)S(1)}, bf16[6,128,128]{2,1,0:T(8,128)(2,1)S(1)}, u32[]{:S(2)}, u32[]{:S(2)}) collective-permute-start(bf16[6,128,128]{2,1,0:T(8,128)(2,1)S(1)} %get-tuple-element.67), channel_id=1, source_target_pairs={{1,0},{2,1},{3,2},{4,5},{5,6},{6,7},{9,8},{10,9},{11,10},{12,13},{... | collective-permute-start | bytes 589832 | tf_op jit(solution)/shard_map/ppermute | solution.py:499
  132.1 22.3 %collective-permute-start.10 = (bf16[6,128,128]{2,1,0:T(8,128)(2,1)S(1)}, bf16[6,128,128]{2,1,0:T(8,128)(2,1)S(1)}, u32[]{:S(2)}, u32[]{:S(2)}) collective-permute-start(bf16[6,128,128]{2,1,0:T(8,128)(2,1)S(1)} %get-tuple-element.68), channel_id=1, source_target_pairs={{1,0},{2,1},{3,2},{4,5},{5,6},{6,7},{9,8},{10,9},{11,10},{12,13},{... | collective-permute-start | bytes 589832 | tf_op jit(solution)/shard_map/ppermute | solution.py:499
  136.1 8.4 %collective-permute-start.7 = (bf16[4,128,128]{2,1,0:T(8,128)(2,1)S(1)}, bf16[4,128,128]{2,1,0:T(8,128)(2,1)S(1)}, u32[]{:S(2)}, u32[]{:S(2)}) collective-permute-start(bf16[4,128,128]{2,1,0:T(8,128)(2,1)S(1)} %get-tuple-element.54), channel_id=1, source_target_pairs={{4,0},{8,4},{12,8},{16,12},{20,16},{24,20},{28,24},{5,1},{9,5},{13... | collective-permute-start | bytes 393224 | tf_op jit(solution)/shard_map/ppermute | solution.py:490
